TPU v7x, 32 devices: a whole 2x2x4 slice. The times are simulated.
32 devices in a mesh: seq: 8 (over z, x), tensor: 4 (over y, core).
Axes of the slice: x: 2, y: 2, z: 4, core: 2. Of those that a mesh axis runs over, the one named last changes fastest.
Arguments:
- patches: bfloat16 [4096, 640], P('seq'), may hold values from -6 to 6
- keep_lists: int32 [16, 128], P('seq'), may hold values from 0 to 255, as said below
- visible_counts: int32 [16], P('seq'), may hold values from 76 to 128
- embed_weight: bfloat16 [640, 2560], replicated, may hold values from -0.25 to 0.25
- position_table: bfloat16 [256, 2560], replicated, may hold values from -6 to 6
- local_gain: float32 [2560], replicated, may hold values from 0.5 to 1.5
- local_projection: bfloat16 [2560, 16, 384], P('seq', 'tensor'), as said below
- local_output: bfloat16 [2560, 2048], P('seq', 'tensor'), may hold values from -0.125 to 0.125
- global_gain: float32 [2560], replicated, may hold values from 0.5 to 1.5
- global_projection: bfloat16 [2560, 16, 384], P('seq', 'tensor'), as said below
- global_output: bfloat16 [2560, 2048], P('seq', 'tensor'), may hold values from -0.125 to 0.125
Outputs:
- encoded: bfloat16 [16, 256, 2560], P(None, 'seq', 'tensor')
Inputs may be any that keep to these rules, and one draw needn't show every extreme that they name: `keep_lists`: each row holds 128 different positions within a window; its first visible_counts entries are the window's visible patches, the others masked ones. `local_projection`: entries lie within plus or minus 16 times 2560 ** -0.5. `global_projection`: entries lie within plus or minus 16 times 2560 ** -0.5.
All inputs are finite; a program needn't handle non-finite values.
Results may differ from a plain program's by a relative error of at most 0.008.
Values may be sent and summed in bfloat16 or wider, within the bound.
No kernel may reach another device: no remote copies, remote signals or barrier semaphores. Data moves between devices by JAX's collectives and lax.ppermute only.
A program may use at most 128 MiB of HBM per device.

v0:
```python
import functools
import math

import jax
import jax.numpy as jnp
from jax import lax
from jax.experimental import pallas as pl
from jax.experimental.pallas import tpu as pltpu
from jax.sharding import PartitionSpec as P


EPSILON = 1e-05


def normed(values, gain):
    floats = values.astype(jnp.float32)
    center = floats - jnp.mean(floats, axis=-1, keepdims=True)
    spread = jnp.mean(center * center, axis=-1, keepdims=True)
    return (center * lax.rsqrt(spread + EPSILON) * gain).astype(jnp.bfloat16)


def local_attend(heads, allowed, width):
    queries, key_part, value_part = (
        heads[..., :width],
        heads[..., width : 2 * width],
        heads[..., 2 * width :],
    )
    scores = jnp.einsum(
        "gqe,gke->gqk", queries, key_part, preferred_element_type=jnp.float32
    ) * width ** (-0.5)
    scores = jnp.where(allowed, scores, -jnp.inf)
    top = jnp.max(scores, axis=-1, keepdims=True)
    weights = jnp.exp(scores - top)
    weights = (weights / jnp.sum(weights, axis=-1, keepdims=True)).astype(jnp.bfloat16)
    return jnp.einsum("gqk,gke->gqe", weights, value_part, preferred_element_type=jnp.float32).astype(
        jnp.bfloat16
    )


def global_kernel(own_ref, query_a, query_b, place_ref, codes_ref, heads_a, heads_b, *refs):
    *pair_refs, out_ref = refs
    tile, width = out_ref.shape
    step, half = pl.program_id(0), pl.num_programs(0) // 2
    query = jnp.where(step < half, query_a[...], query_b[...])
    contract = (((1,), (1,)), ((), ()))
    apart = len(pair_refs) == 2
    blocks = [(ref, width, width * 2, True) for ref in (heads_a, heads_b)] if apart else []
    blocks += [(ref, 0, width, not apart) for ref in pair_refs]
    ident = own_ref[0] + step * tile + lax.broadcasted_iota(jnp.int32, (tile, 1), 0)
    parts, begin = [], 0
    for ref, key, _, own in blocks:
        keys = ref.shape[0]
        scores = lax.dot_general(
            query, ref[:, key : key + width], contract, preferred_element_type=jnp.float32
        )
        allowed = place_ref[...] == codes_ref[:, begin : begin + keys]
        if own:
            columns = lax.broadcasted_iota(jnp.int32, scores.shape, 1) + begin
            allowed = allowed | (ident == columns)
        parts.append(jnp.where(allowed, scores, -jnp.inf))
        begin += keys
    top = functools.reduce(jnp.maximum, [jnp.max(p, axis=-1, keepdims=True) for p in parts])
    total, mixed = 0.0, 0.0
    factor = width ** (-0.5) * math.log2(math.e)
    for (ref, _, value, _), scores in zip(blocks, parts, strict=True):
        weights = jnp.exp2((scores - top) * factor)
        total = total + jnp.sum(weights, axis=-1, keepdims=True)
        mixed = mixed + jnp.dot(
            weights.astype(jnp.bfloat16),
            ref[:, value : value + width],
            preferred_element_type=jnp.float32,
        )
    out_ref[...] = (mixed / total).astype(out_ref.dtype)


def global_attend(own, place, codes, heads_a, heads_b, pairs, tile):
    rows = heads_a.shape[0]
    width = heads_a.shape[1] // 3
    half = rows // tile
    whole = [heads_a, heads_b, *pairs]
    return pl.pallas_call(
        global_kernel,
        grid_spec=pltpu.PrefetchScalarGridSpec(
            num_scalar_prefetch=1,
            grid=(2 * half,),
            in_specs=[
                pl.BlockSpec((tile, width), lambda i, _: (jnp.minimum(i, half - 1), 0)),
                pl.BlockSpec((tile, width), lambda i, _: (jnp.maximum(i - half, 0), 0)),
                pl.BlockSpec((tile, 1), lambda i, _: (i, 0)),
                pl.BlockSpec(codes.shape, lambda i, _: (0, 0)),
            ]
            + [pl.BlockSpec(p.shape, lambda i, _: (0, 0)) for p in whole],
            out_specs=pl.BlockSpec((tile, width), lambda i, _: (i, 0)),
        ),
        out_shape=jax.ShapeDtypeStruct((2 * rows, width), heads_a.dtype),
        name="global_attend",
    )(own, heads_a, heads_b, place, codes, *whole)


def after(value, *others):
    return lax.optimization_barrier((value, *others))[0]


def shards(
    patches,
    keep_lists,
    visible_counts,
    embed_weight,
    position_table,
    local_gain,
    local_projection,
    local_output,
    global_gain,
    global_projection,
    global_output,
):
    windows_here, slots = keep_lists.shape
    window_cells, width = position_table.shape
    heads_here = local_projection.shape[1]
    head = local_projection.shape[2] // 3
    seq_count = lax.axis_size("seq")
    tensor_count = lax.axis_size("tensor")
    share = width // tensor_count
    depth = heads_here
    across = seq_count // depth
    assert depth == 4 and tensor_count == 4 and across * depth == seq_count
    rows_here = windows_here * slots
    all_rows = depth * rows_here
    patch_in = patches.shape[1]
    quarter = rows_here // tensor_count
    s = lax.axis_index("seq")
    t = lax.axis_index("tensor")
    z = s // across
    x = s % across

    def swap_z(value, k):
        return lax.ppermute(
            value,
            "seq",
            [(a * across + b, (a ^ k) * across + b) for a in range(depth) for b in range(across)],
        )

    def swap_t(value, k):
        return lax.ppermute(value, "tensor", [(a, a ^ k) for a in range(tensor_count)])

    def from_x(value):
        if across == 2:
            return [value, lax.ppermute(value, "seq", [(a, a ^ 1) for a in range(seq_count)])]
        groups = [[a * across + b for b in range(across)] for a in range(depth)]
        every = lax.all_gather(value, "seq", axis=0, axis_index_groups=groups)
        return [every[b] for b in range(across)]

    def pick(stacked, index, axis=0):
        return lax.dynamic_index_in_dim(stacked, index, axis, keepdims=False)

    def place(pieces, order, tie):
        pieces, _ = lax.optimization_barrier((pieces, tie))
        shape = (len(pieces), across) + pieces[0][0].shape
        placed = jnp.zeros(shape, pieces[0][0].dtype)
        spots = [x, 1 - x] if across == 2 else range(across)
        for every, at in zip(pieces, order, strict=True):
            for piece, spot in zip(every, spots, strict=True):
                placed = lax.dynamic_update_slice(placed, piece[None, None], (at, spot, 0, 0))
        return placed.reshape(shape[0], shape[1] * shape[2], shape[3])

    def send_heads(by_head):
        return [pick(by_head, z)] + [swap_z(pick(by_head, z ^ k), k) for k in range(1, depth)]

    natural = [z ^ k for k in range(depth)]

    offsets = jnp.arange(windows_here, dtype=jnp.int32)[:, None] * window_cells
    picked = patches[(keep_lists + offsets).reshape(-1)]
    notes = jnp.concatenate([keep_lists.reshape(-1), visible_counts]).astype(jnp.bfloat16)
    notes = jnp.pad(notes[None], ((0, 15), (0, patch_in - notes.shape[0])))
    message = jnp.concatenate(
        [lax.dynamic_slice_in_dim(picked, t * quarter, quarter, 0), notes], axis=0
    )
    came = [swap_z(message, k) for k in range(1, depth)]
    remote = jnp.stack(came)
    remote_y = swap_t(remote, 2)
    both = jnp.stack([remote, remote_y])
    both_c = swap_t(both, 1)
    by_t = jnp.stack([both[0], both_c[0], both[1], both_c[1]])
    far = jnp.stack([pick(by_t, t ^ k)[:, :quarter] for k in range(tensor_count)], axis=1)
    tiles = jnp.concatenate([picked, far.reshape((depth - 1) * rows_here, patch_in)], axis=0)
    facts = jnp.concatenate([notes[:1], after(remote, remote_y)[:, quarter]]).astype(jnp.float32)
    keep = facts[:, :rows_here].astype(jnp.int32)
    counts = facts[:, rows_here : rows_here + windows_here].astype(jnp.int32)
    windows_held = depth * windows_here
    slot_ids = jnp.arange(slots, dtype=jnp.int32)
    visible = slot_ids[None, :] < counts.reshape(windows_held, 1)
    codes = jnp.where(visible, keep.reshape(windows_held, slots), -1)

    sent = send_heads(jnp.transpose(local_projection, (1, 0, 2)))
    sent_x = [from_x(sent[k]) for k in range(depth)]
    head_x = sent_x
    back_z = swap_z(local_output, 1)
    back_x = [from_x(local_output)]
    sent = send_heads(jnp.transpose(after(global_projection, remote_y), (1, 0, 2)))
    far_x = [from_x(sent[k]) for k in range(depth)]
    table_z = [global_output] + [swap_z(global_output, k) for k in range(1, depth)]
    table_x = [from_x(table_z[k]) for k in range(depth)]

    cell_ids = jnp.arange(window_cells, dtype=jnp.int32)
    hot = (keep.reshape(-1)[:, None] == cell_ids[None, :]).astype(jnp.bfloat16)
    embedded = jnp.dot(
        jnp.concatenate([tiles, hot], axis=1),
        jnp.concatenate([embed_weight, position_table], axis=0),
        preferred_element_type=jnp.float32,
    )
    start = embedded.astype(jnp.bfloat16)
    back_x.append(from_x(after(back_z, start)))
    local_full = place(head_x, natural, start).reshape(width, 3 * head)
    allowed = visible[:, None, :] | jnp.eye(slots, dtype=bool)[None]
    local_heads = jnp.dot(
        normed(start, local_gain), local_full, preferred_element_type=jnp.float32
    ).astype(jnp.bfloat16)
    local_mixed = local_attend(
        local_heads.reshape(windows_held, slots, 3 * head), allowed, head
    ).reshape(depth, rows_here, head)

    low, high = t & 1, t >> 1

    def gather_sum(partial):
        half = pick(partial, low, 1) + swap_t(pick(partial, 1 - low, 1), 1)
        sent = pick(half, 1 - high).astype(jnp.bfloat16)
        return pick(half, high) + swap_t(sent, 2).astype(jnp.float32)

    got = [jnp.stack([local_mixed[k], local_mixed[k ^ 2]]) for k in range(depth)]
    got = jnp.stack([got[0]] + [swap_z(got[k], k) for k in range(1, depth)])
    row = jnp.concatenate([pick(got, z ^ k) for k in range(depth)], axis=-1)
    local_back = place(back_x, [z & 1, 1 - (z & 1)], local_mixed)
    partial = jnp.einsum("jrc,qdc->jqrd", row, local_back, preferred_element_type=jnp.float32)
    start_here = lax.dynamic_slice(
        start,
        (2 * high * rows_here, (2 * (z >> 1) + low) * share),
        (rows_here, share),
    )
    after_local = (start_here.astype(jnp.float32) + gather_sum(partial)).astype(jnp.bfloat16)

    pieces = [after_local] + [swap_z(after_local, k) for k in range(1, depth)]
    pieces_y = [swap_t(pieces[k], 2) for k in range(depth)]
    global_full = place(far_x, natural, pieces[1]).reshape(width, 3 * head)

    def project_rows(parts):
        every = jnp.concatenate(parts)
        heads = []
        for i in range(2):
            quarters = []
            for quarter in range(tensor_count):
                plane = (z >> 1) ^ (quarter >> 1)
                spot = 4 * (low ^ (quarter & 1)) + 2 * plane + (i ^ plane ^ high)
                quarters.append(pick(every, spot))
            rows = jnp.concatenate(quarters, axis=1)
            heads.append(
                jnp.dot(
                    normed(rows, global_gain), global_full, preferred_element_type=jnp.float32
                ).astype(jnp.bfloat16)
            )
        return jnp.concatenate(heads, axis=0)

    near = [jnp.stack([pieces[k], pieces_y[k]]) for k in range(depth)]
    far = [swap_t(near[k], 1) for k in range(depth)]
    heads_a = project_rows([near[0], near[2], far[0], far[2]])
    pairs = from_x(heads_a[:, head:])
    heads_b = project_rows([near[1], near[3], far[1], far[3]])
    pairs_b = from_x(heads_b[:, head:])
    pairs = [p for both in zip(pairs, pairs_b, strict=True) for p in both]
    turn = (0, 2, 1, 3)
    spot = 0 if across == 2 else x
    place_here = jnp.stack([keep[k] for k in turn]).reshape(all_rows, 1)
    codes_by_z = codes.reshape(depth, rows_here)
    every_code = from_x(jnp.stack([codes_by_z[k] for k in turn]).reshape(1, all_rows))
    own = jnp.full((1,), spot * all_rows, jnp.int32)
    if across == 2:
        pairs = pairs[2:]
    global_mixed = global_attend(
        own, place_here, jnp.concatenate(every_code, axis=1), heads_a, heads_b, pairs, 256 // across
    ).reshape(depth, rows_here, head)
    global_mixed = [global_mixed[k] for k in turn]

    got = jnp.stack([global_mixed[0]] + [swap_z(global_mixed[k], k) for k in range(1, depth)])
    row = jnp.concatenate([pick(got, z ^ k) for k in range(depth)], axis=-1)
    global_back = place(table_x, natural, global_mixed[0])
    partial = jnp.einsum("rc,tdc->trd", row, global_back, preferred_element_type=jnp.float32)
    plane = (z >> 1) ^ high
    held = 2 * plane + (plane ^ high)
    residual = pick(jnp.concatenate([near[0], near[2]]), held)
    total = gather_sum(partial.reshape(2, 2, rows_here, share))
    encoded = (residual.astype(jnp.float32) + total).astype(jnp.bfloat16)
    own_codes = codes[:windows_here]
    cells_each = window_cells // seq_count
    cells = cell_ids.reshape(seq_count, 1, cells_each, 1)
    spread_hot = (own_codes[None, :, None, :] == cells).astype(jnp.bfloat16)
    spread = jnp.einsum(
        "swpj,wjd->swpd",
        spread_hot,
        encoded.reshape(windows_here, slots, share),
        preferred_element_type=jnp.float32,
    ).astype(jnp.bfloat16)
    result = lax.all_to_all(spread, "seq", split_axis=0, concat_axis=0, tiled=True)
    return result.reshape(seq_count * windows_here, cells_each, share)


def solution(mesh):
    run = place_and_run(mesh)
    return run


def place_and_run(mesh):
    placed = (
        P("seq", None),
        P("seq", None),
        P("seq"),
        P(),
        P(),
        P(),
        P("seq", "tensor", None),
        P("seq", "tensor"),
        P(),
        P("seq", "tensor", None),
        P("seq", "tensor"),
    )

    return jax.shard_map(
        shards, mesh=mesh, in_specs=placed, out_specs=P(None, "seq", "tensor"), check_vma=False
    )
```

profile of v0, /device:TPU:0, one launch (start us, length us, event | category | flops | bytes accessed | tf_op | source)
XLA Modules:
  0.0 251.2 jit_solution(11898181972476318882)
XLA Ops:
  2.8 3.1 %collective-permute-start = (bf16[80,640]{1,0:T(8,128)(2,1)S(1)}, bf16[80,640]{1,0:T(8,128)(2,1)S(1)}, u32[]{:S(2)}, u32[]{:S(2)}) collective-permute-start(bf16[80,640]{1,0:T(8,128)(2,1)S(1)} %pad_maximum_fusion.19), channel_id=1, source_target_pairs={{0,8},{4,12},{8,0},{12,4},{16,24},{20,28},{24,16},{28,20},{1,9},{5... | collective-permute-start | bytes 307208 | tf_op jit(solution)/shard_map/ppermute | solution.py:137
  6.0 2.6 %collective-permute-start.1 = (bf16[80,640]{1,0:T(8,128)(2,1)S(1)}, bf16[80,640]{1,0:T(8,128)(2,1)S(1)}, u32[]{:S(2)}, u32[]{:S(2)}) collective-permute-start(bf16[80,640]{1,0:T(8,128)(2,1)S(1)} %pad_maximum_fusion.19), channel_id=1, source_target_pairs={{0,16},{4,20},{8,24},{12,28},{16,0},{20,4},{24,8},{28,12},{1,17},{... | collective-permute-start | bytes 307208 | tf_op jit(solution)/shard_map/ppermute | solution.py:137
  8.9 7.8 %collective-permute-done.1 = bf16[80,640]{1,0:T(8,128)(2,1)S(1)} collective-permute-done((bf16[80,640]{1,0:T(8,128)(2,1)S(1)}, bf16[80,640]{1,0:T(8,128)(2,1)S(1)}, u32[]{:S(2)}, u32[]{:S(2)}) %collective-permute-start.1) | collective-permute-done | bytes 102432 | tf_op jit(solution)/shard_map/ppermute | solution.py:137
  16.8 1.6 collective-permute-start.3
  18.3 2.0 constant_dynamic-slice_fusion
  21.1 1.7 collective-permute-start.9
  23.5 1.4 collective-permute-start.11
  27.0 1.6 collective-permute-start.8
  29.2 1.6 collective-permute-done.9
  31.8 11.8 %collective-permute-done.11 = bf16[320,384]{1,0:T(8,128)(2,1)} collective-permute-done((bf16[320,384]{1,0:T(8,128)(2,1)}, bf16[320,384]{1,0:T(8,128)(2,1)}, u32[]{:S(2)}, u32[]{:S(2)}) %collective-permute-start.11) | collective-permute-done | bytes 245792 | tf_op jit(solution)/shard_map/ppermute | solution.py:137
  43.6 1.5 collective-permute-start.10
  45.6 1.5 collective-permute-start.14
  47.8 1.5 copy-done.24
  49.7 6.1 %convert_reduce_fusion = (f32[1024]{0:T(1024)S(1)}, bf16[1024,2560]{1,0:T(8,128)(2,1)S(1)}) fusion(bf16[256,2560]{1,0:T(8,128)(2,1)S(1)} %copy-done.25, bf16[640,2560]{1,0:T(8,128)(2,1)S(1)} %copy-done.24, bf16[1024,256]{1,0:T(8,128)(2,1)S(1)} %fusion.78, bf16[768,640]{1,0:T(8,128)(2,1)S(1)} %bitcast.303, bf16[256,640]{1,0:T(8,128)(2,1)S(1)} %gather_fusion), kind=kOutput, calls=%fused_computation.3 | convolution fusion | flops 4720163840 | bytes 11669504 | tf_op jit(solution)/shard_map/dot_general | solution.py:206
  55.8 1.5 fusion.3
  61.4 3.0 %fusion.39 = bf16[1024,384]{1,0:T(8,128)(2,1)S(1)} fusion(bf16[2560,384]{1,0:T(8,128)(2,1)S(1)} %bitcast.295, bf16[1024,2560]{1,0:T(8,128)(2,1)S(1)} %get-tuple-element.132, f32[2560]{0:T(1024)S(1)} %copy-done.26, f32[1024]{0:T(1024)S(1)} %add_rsqrt_fusion, f32[1024]{0:T(1024)S(1)} %broadcast_multiply_fusion), kind=kOutput, calls=%fused_computation.50 | convolution fusion | flops 2026766336 | bytes 8013824 | tf_op jit(solution)/shard_map/dot_general | solution.py:215
  65.2 4.1 %collective-permute-start.16 = (bf16[2,256,128]{2,1,0:T(8,128)(2,1)S(1)}, bf16[2,256,128]{2,1,0:T(8,128)(2,1)S(1)}, u32[]{:S(2)}, u32[]{:S(2)}) collective-permute-start(bf16[2,256,128]{2,1,0:T(8,128)(2,1)S(1)} %get-tuple-element.118), channel_id=1, source_target_pairs={{0,16},{4,20},{8,24},{12,28},{16,0},{20,4},{24,8},{28,12},{1,17},{... | collective-permute-start | bytes 393224 | tf_op jit(solution)/shard_map/ppermute | solution.py:137
  69.4 1.5 collective-permute-start.17
  71.5 4.8 %collective-permute-done.16 = bf16[2,256,128]{2,1,0:T(8,128)(2,1)S(1)} collective-permute-done((bf16[2,256,128]{2,1,0:T(8,128)(2,1)S(1)}, bf16[2,256,128]{2,1,0:T(8,128)(2,1)S(1)}, u32[]{:S(2)}, u32[]{:S(2)}) %collective-permute-start.16) | collective-permute-done | bytes 131104 | tf_op jit(solution)/shard_map/ppermute | solution.py:137
  77.1 1.9 collective-permute-start.26
  79.9 3.2 %collective-permute-start.28 = (bf16[320,512]{1,0:T(8,128)(2,1)S(1)}, bf16[320,512]{1,0:T(8,128)(2,1)S(1)}, u32[]{:S(2)}, u32[]{:S(2)}) collective-permute-start(bf16[320,512]{1,0:T(8,128)(2,1)S(1)} %copy-done.16), channel_id=1, source_target_pairs={{0,24},{4,28},{8,16},{12,20},{16,8},{20,12},{24,0},{28,4},{1,25},{... | collective-permute-start | bytes 983048 | tf_op jit(solution)/shard_map/ppermute | solution.py:137
  85.4 1.5 copy-done.12
  91.4 10.8 %collective-permute-done.26 = bf16[320,512]{1,0:T(8,128)(2,1)} collective-permute-done((bf16[320,512]{1,0:T(8,128)(2,1)S(1)}, bf16[320,512]{1,0:T(8,128)(2,1)}, u32[]{:S(2)}, u32[]{:S(2)}) %collective-permute-start.26) | collective-permute-done | bytes 327712 | tf_op jit(solution)/shard_map/ppermute | solution.py:137
  106.3 4.1 %collective-permute-start.33 = (bf16[320,384]{1,0:T(8,128)(2,1)S(1)}, bf16[320,384]{1,0:T(8,128)(2,1)S(1)}, u32[]{:S(2)}, u32[]{:S(2)}) collective-permute-start(bf16[320,384]{1,0:T(8,128)(2,1)S(1)} %get-tuple-element.95), channel_id=1, source_target_pairs={{0,8},{4,12},{8,0},{12,4},{16,24},{20,28},{24,16},{28,20},{1,9},{5... | collective-permute-start | bytes 737288 | tf_op jit(solution)/shard_map/ppermute | solution.py:137
  110.4 2.7 %collective-permute-done.25 = bf16[320,512]{1,0:T(8,128)(2,1)S(1)} collective-permute-done((bf16[320,512]{1,0:T(8,128)(2,1)}, bf16[320,512]{1,0:T(8,128)(2,1)S(1)}, u32[]{:S(2)}, u32[]{:S(2)}) %collective-permute-start.25) | collective-permute-done | bytes 327712 | tf_op jit(solution)/shard_map/ppermute | solution.py:148
  113.1 4.8 %collective-permute-done.27 = bf16[320,512]{1,0:T(8,128)(2,1)S(1)} collective-permute-done((bf16[320,512]{1,0:T(8,128)(2,1)}, bf16[320,512]{1,0:T(8,128)(2,1)S(1)}, u32[]{:S(2)}, u32[]{:S(2)}) %collective-permute-start.27) | collective-permute-done | bytes 327712 | tf_op jit(solution)/shard_map/ppermute | solution.py:148
  117.9 2.5 collective-permute-start.37
  120.4 4.0 %collective-permute-done.29 = bf16[320,512]{1,0:T(8,128)(2,1)S(1)} collective-permute-done((bf16[320,512]{1,0:T(8,128)(2,1)S(1)}, bf16[320,512]{1,0:T(8,128)(2,1)S(1)}, u32[]{:S(2)}, u32[]{:S(2)}) %collective-permute-start.29) | collective-permute-done | bytes 327712 | tf_op jit(solution)/shard_map/ppermute | solution.py:148
  126.0 1.5 bitcast_add_fusion.1
  132.0 2.8 %collective-permute-done.19 = bf16[256,640]{1,0:T(8,128)(2,1)S(1)} collective-permute-done((bf16[256,640]{1,0:T(8,128)(2,1)S(1)}, bf16[256,640]{1,0:T(8,128)(2,1)S(1)}, u32[]{:S(2)}, u32[]{:S(2)}) %collective-permute-start.19) | collective-permute-done | bytes 327712 | tf_op jit(solution)/shard_map/ppermute | solution.py:144
  137.4 3.3 %collective-permute-start.41 = (bf16[256,640]{1,0:T(8,128)(2,1)S(1)}, bf16[256,640]{1,0:T(8,128)(2,1)S(1)}, u32[]{:S(2)}, u32[]{:S(2)}) collective-permute-start(bf16[256,640]{1,0:T(8,128)(2,1)S(1)} %get-tuple-element.68), channel_id=1, source_target_pairs={{0,24},{4,28},{8,16},{12,20},{16,8},{20,12},{24,0},{28,4},{1,25},{... | collective-permute-start | bytes 983048 | tf_op jit(solution)/shard_map/ppermute | solution.py:137
  142.4 2.4 collective-permute-done.39
  145.5 2.9 %collective-permute-start.40 = (bf16[256,640]{1,0:T(8,128)(2,1)S(1)}, bf16[256,640]{1,0:T(8,128)(2,1)S(1)}, u32[]{:S(2)}, u32[]{:S(2)}) collective-permute-start(bf16[256,640]{1,0:T(8,128)(2,1)S(1)} %collective-permute-done.39), channel_id=1, source_target_pairs={{0,2},{1,3},{2,0},{3,1},{4,6},{5,7},{6,4},{7,5},{8,10},{9,11},{10,... | collective-permute-start | bytes 983048 | tf_op jit(solution)/shard_map/ppermute | solution.py:144
  148.5 3.4 %collective-permute-done.41 = bf16[256,640]{1,0:T(8,128)(2,1)S(1)} collective-permute-done((bf16[256,640]{1,0:T(8,128)(2,1)S(1)}, bf16[256,640]{1,0:T(8,128)(2,1)S(1)}, u32[]{:S(2)}, u32[]{:S(2)}) %collective-permute-start.41) | collective-permute-done | bytes 327712 | tf_op jit(solution)/shard_map/ppermute | solution.py:137
  151.8 1.5 collective-permute-start.42
  153.4 10.4 %collective-permute-done.21 = bf16[256,640]{1,0:T(8,128)(2,1)S(1)} collective-permute-done((bf16[256,640]{1,0:T(8,128)(2,1)S(1)}, bf16[256,640]{1,0:T(8,128)(2,1)S(1)}, u32[]{:S(2)}, u32[]{:S(2)}) %collective-permute-start.21) | collective-permute-done | bytes 327712 | tf_op jit(solution)/shard_map/ppermute | solution.py:137
  163.8 1.5 collective-permute-start.22
  166.4 4.5 %collective-permute-done.22 = bf16[256,640]{1,0:T(8,128)(2,1)S(1)} collective-permute-done((bf16[256,640]{1,0:T(8,128)(2,1)S(1)}, bf16[256,640]{1,0:T(8,128)(2,1)S(1)}, u32[]{:S(2)}, u32[]{:S(2)}) %collective-permute-start.22) | collective-permute-done | bytes 327712 | tf_op jit(solution)/shard_map/ppermute | solution.py:144
  175.9 1.5 collective-permute-start.47
  183.6 1.4 collective-permute-done.47.refs_1_
  185.0 5.1 %collective-permute-done.46.refs_0_ = bf16[512,256]{1,0:T(8,128)(2,1)S(1)} collective-permute-done((bf16[512,256]{1,0:T(8,128)(2,1)S(1)}, bf16[512,256]{1,0:T(8,128)(2,1)S(1)}, u32[]{:S(2)}, u32[]{:S(2)}) %collective-permute-start.46) | collective-permute-done | bytes 262176 | tf_op jit(solution)/shard_map/ppermute | solution.py:148
  190.8 8.2 %global_attend.1 = bf16[1024,128]{1,0:T(8,128)(2,1)} custom-call(s32[1]{0:T(128)} %constant.196.clone.1.own_ref, bf16[512,384]{1,0:T(8,128)(2,1)} %pad_maximum_fusion.12.query_a.heads_a, bf16[512,384]{1,0:T(8,128)(2,1)} %pad_maximum_fusion.13.query_b.heads_b, s32[1024,1]{1,0:T(8,128)} %bitcast.290, s32[1,2048]{1,0:T(1,128)} %pad_add_fusion.codes_ref, ...), custom_call_target="tpu_custom_call" | custom-call | tf_op jit(solution)/shard_map/global_attend/pallas_call | solution.py:81
  200.5 6.9 %collective-permute-start.49 = (bf16[256,128]{1,0:T(8,128)(2,1)S(1)}, bf16[256,128]{1,0:T(8,128)(2,1)S(1)}, u32[]{:S(2)}, u32[]{:S(2)}) collective-permute-start(bf16[256,128]{1,0:T(8,128)(2,1)S(1)} %get-tuple-element.111), channel_id=1, source_target_pairs={{0,16},{4,20},{8,24},{12,28},{16,0},{20,4},{24,8},{28,12},{1,17},{... | collective-permute-start | bytes 196616 | tf_op jit(solution)/shard_map/ppermute | solution.py:137
  207.5 4.1 %collective-permute-done.49 = bf16[256,128]{1,0:T(8,128)(2,1)S(1)} collective-permute-done((bf16[256,128]{1,0:T(8,128)(2,1)S(1)}, bf16[256,128]{1,0:T(8,128)(2,1)S(1)}, u32[]{:S(2)}, u32[]{:S(2)}) %collective-permute-start.49) | collective-permute-done | bytes 65568 | tf_op jit(solution)/shard_map/ppermute | solution.py:137
  211.5 1.9 collective-permute-done.50
  214.7 3.0 %collective-permute-done.51 = f32[2,256,640]{2,1,0:T(8,128)S(1)} collective-permute-done((f32[2,256,640]{2,1,0:T(8,128)S(1)}, f32[2,256,640]{2,1,0:T(8,128)S(1)}, u32[]{:S(2)}, u32[]{:S(2)}) %collective-permute-start.51) | collective-permute-done | bytes 1310752 | tf_op jit(solution)/shard_map/ppermute | solution.py:144
  218.5 9.3 %collective-permute-done.52 = bf16[256,640]{1,0:T(8,128)(2,1)} collective-permute-done((bf16[256,640]{1,0:T(8,128)(2,1)S(1)}, bf16[256,640]{1,0:T(8,128)(2,1)}, u32[]{:S(2)}, u32[]{:S(2)}) %collective-permute-start.52) | collective-permute-done | bytes 327712 | tf_op jit(solution)/shard_map/ppermute | solution.py:144
  229.7 20.7 %all_to_all.5 = bf16[8,2,32,640]{3,2,1,0:T(8,128)(2,1)S(1)} all-to-all(bf16[8,2,32,640]{3,2,1,0:T(8,128)(2,1)S(1)} %copy.40), channel_id=1, replica_groups=mesh['seq'=8,'tensor'=4] {'seq'}, dimensions={0} | all-to-all | bytes 1310720 | tf_op jit(solution)/shard_map/all_to_all | solution.py:301
  (264 shorter events, 57.6 us)
Async XLA Ops:
  6.0 10.7 %collective-permute-start.1 = (bf16[80,640]{1,0:T(8,128)(2,1)S(1)}, bf16[80,640]{1,0:T(8,128)(2,1)S(1)}, u32[]{:S(2)}, u32[]{:S(2)}) collective-permute-start(bf16[80,640]{1,0:T(8,128)(2,1)S(1)} %pad_maximum_fusion.19), channel_id=1, source_target_pairs={{0,16},{4,20},{8,24},{12,28},{16,0},{20,4},{24,8},{28,12},{1,17},{... | collective-permute-start | bytes 307208 | tf_op jit(solution)/shard_map/ppermute | solution.py:137
  8.6 8.1 %collective-permute-start.2 = (bf16[80,640]{1,0:T(8,128)(2,1)S(1)}, bf16[80,640]{1,0:T(8,128)(2,1)S(1)}, u32[]{:S(2)}, u32[]{:S(2)}) collective-permute-start(bf16[80,640]{1,0:T(8,128)(2,1)S(1)} %pad_maximum_fusion.19), channel_id=1, source_target_pairs={{0,24},{4,28},{8,16},{12,20},{16,8},{20,12},{24,0},{28,4},{1,25},{... | collective-permute-start | bytes 307208 | tf_op jit(solution)/shard_map/ppermute | solution.py:137
  16.8 11.9 %collective-permute-start.3 = (bf16[3,80,640]{2,1,0:T(8,128)(2,1)S(1)}, bf16[3,80,640]{2,1,0:T(8,128)(2,1)S(1)}, u32[]{:S(2)}, u32[]{:S(2)}) collective-permute-start(bf16[3,80,640]{2,1,0:T(8,128)(2,1)S(1)} %get-tuple-element.36), channel_id=1, source_target_pairs={{0,2},{1,3},{2,0},{3,1},{4,6},{5,7},{6,4},{7,5},{8,10},{9,11},{10,... | collective-permute-start | bytes 921608 | tf_op jit(solution)/shard_map/ppermute | solution.py:144
  21.1 9.7 %collective-permute-start.9 = (bf16[320,384]{1,0:T(8,128)(2,1)}, bf16[320,384]{1,0:T(8,128)(2,1)S(1)}, u32[]{:S(2)}, u32[]{:S(2)}) collective-permute-start(bf16[320,384]{1,0:T(8,128)(2,1)} %bitcast.274), channel_id=1, source_target_pairs={{0,8},{4,12},{8,0},{12,4},{16,24},{20,28},{24,16},{28,20},{1,9},{5... | collective-permute-start | bytes 737288 | tf_op jit(solution)/shard_map/ppermute | solution.py:137
  23.5 20.1 %collective-permute-start.11 = (bf16[320,384]{1,0:T(8,128)(2,1)}, bf16[320,384]{1,0:T(8,128)(2,1)}, u32[]{:S(2)}, u32[]{:S(2)}) collective-permute-start(bf16[320,384]{1,0:T(8,128)(2,1)} %bitcast.273), channel_id=1, source_target_pairs={{0,16},{4,20},{8,24},{12,28},{16,0},{20,4},{24,8},{28,12},{1,17},{... | collective-permute-start | bytes 737288 | tf_op jit(solution)/shard_map/ppermute | solution.py:137
  25.6 19.4 %collective-permute-start.13 = (bf16[320,384]{1,0:T(8,128)(2,1)}, bf16[320,384]{1,0:T(8,128)(2,1)}, u32[]{:S(2)}, u32[]{:S(2)}) collective-permute-start(bf16[320,384]{1,0:T(8,128)(2,1)} %bitcast.272), channel_id=1, source_target_pairs={{0,24},{4,28},{8,16},{12,20},{16,8},{20,12},{24,0},{28,4},{1,25},{... | collective-permute-start | bytes 737288 | tf_op jit(solution)/shard_map/ppermute | solution.py:137
  27.0 30.3 %collective-permute-start.8 = (bf16[320,384]{1,0:T(8,128)(2,1)S(1)}, bf16[320,384]{1,0:T(8,128)(2,1)}, u32[]{:S(2)}, u32[]{:S(2)}) collective-permute-start(bf16[320,384]{1,0:T(8,128)(2,1)S(1)} %bitcast.304), channel_id=1, source_target_pairs={{0,4},{4,0},{8,12},{12,8},{16,20},{20,16},{24,28},{28,24},{1,5},{5... | collective-permute-start | bytes 737288 | tf_op jit(solution)/shard_map/ppermute | solution.py:148
  28.7 16.9 %collective-permute-start.4 = (bf16[2,3,80,640]{3,2,1,0:T(8,128)(2,1)S(1)}, bf16[2,3,80,640]{3,2,1,0:T(8,128)(2,1)S(1)}, u32[]{:S(2)}, u32[]{:S(2)}) collective-permute-start(bf16[2,3,80,640]{3,2,1,0:T(8,128)(2,1)S(1)} %pad_maximum_fusion.10), channel_id=1, source_target_pairs={{0,1},{1,0},{2,3},{3,2},{4,5},{5,4},{6,7},{7,6},{8,9},{9,8},{10,11... | collective-permute-start | bytes 1843208 | tf_op jit(solution)/shard_map/ppermute | solution.py:144
  30.8 40.1 %collective-permute-start.6 = (bf16[320,512]{1,0:T(8,128)(2,1)S(1)}, bf16[320,512]{1,0:T(8,128)(2,1)}, u32[]{:S(2)}, u32[]{:S(2)}) collective-permute-start(bf16[320,512]{1,0:T(8,128)(2,1)S(1)} %copy-done.15), channel_id=1, source_target_pairs={{0,8},{4,12},{8,0},{12,4},{16,24},{20,28},{24,16},{28,20},{1,9},{5... | collective-permute-start | bytes 983048 | tf_op jit(solution)/shard_map/ppermute | solution.py:137
  43.6 14.4 %collective-permute-start.10 = (bf16[320,384]{1,0:T(8,128)(2,1)S(1)}, bf16[320,384]{1,0:T(8,128)(2,1)S(1)}, u32[]{:S(2)}, u32[]{:S(2)}) collective-permute-start(bf16[320,384]{1,0:T(8,128)(2,1)S(1)} %collective-permute-done.9), channel_id=1, source_target_pairs={{0,4},{4,0},{8,12},{12,8},{16,20},{20,16},{24,28},{28,24},{1,5},{5... | collective-permute-start | bytes 737288 | tf_op jit(solution)/shard_map/ppermute | solution.py:148
  45.1 12.9 %collective-permute-start.12 = (bf16[320,384]{1,0:T(8,128)(2,1)}, bf16[320,384]{1,0:T(8,128)(2,1)S(1)}, u32[]{:S(2)}, u32[]{:S(2)}) collective-permute-start(bf16[320,384]{1,0:T(8,128)(2,1)} %collective-permute-done.11), channel_id=1, source_target_pairs={{0,4},{4,0},{8,12},{12,8},{16,20},{20,16},{24,28},{28,24},{1,5},{5... | collective-permute-start | bytes 737288 | tf_op jit(solution)/shard_map/ppermute | solution.py:148
  45.6 12.3 %collective-permute-start.14 = (bf16[320,384]{1,0:T(8,128)(2,1)}, bf16[320,384]{1,0:T(8,128)(2,1)S(1)}, u32[]{:S(2)}, u32[]{:S(2)}) collective-permute-start(bf16[320,384]{1,0:T(8,128)(2,1)} %collective-permute-done.13), channel_id=1, source_target_pairs={{0,4},{4,0},{8,12},{12,8},{16,20},{20,16},{24,28},{28,24},{1,5},{5... | collective-permute-start | bytes 737288 | tf_op jit(solution)/shard_map/ppermute | solution.py:148
  57.4 25.9 %collective-permute-start.5 = (bf16[320,512]{1,0:T(8,128)(2,1)S(1)}, bf16[320,512]{1,0:T(8,128)(2,1)S(1)}, u32[]{:S(2)}, u32[]{:S(2)}) collective-permute-start(bf16[320,512]{1,0:T(8,128)(2,1)S(1)} %copy-done.15), channel_id=1, source_target_pairs={{0,4},{4,0},{8,12},{12,8},{16,20},{20,16},{24,28},{28,24},{1,5},{5... | collective-permute-start | bytes 983048 | tf_op jit(solution)/shard_map/ppermute | solution.py:148
  65.2 11.0 %collective-permute-start.16 = (bf16[2,256,128]{2,1,0:T(8,128)(2,1)S(1)}, bf16[2,256,128]{2,1,0:T(8,128)(2,1)S(1)}, u32[]{:S(2)}, u32[]{:S(2)}) collective-permute-start(bf16[2,256,128]{2,1,0:T(8,128)(2,1)S(1)} %get-tuple-element.118), channel_id=1, source_target_pairs={{0,16},{4,20},{8,24},{12,28},{16,0},{20,4},{24,8},{28,12},{1,17},{... | collective-permute-start | bytes 393224 | tf_op jit(solution)/shard_map/ppermute | solution.py:137
  69.3 7.8 %collective-permute-start.15 = (bf16[2,256,128]{2,1,0:T(8,128)(2,1)S(1)}, bf16[2,256,128]{2,1,0:T(8,128)(2,1)S(1)}, u32[]{:S(2)}, u32[]{:S(2)}) collective-permute-start(bf16[2,256,128]{2,1,0:T(8,128)(2,1)S(1)} %get-tuple-element.119), channel_id=1, source_target_pairs={{0,8},{4,12},{8,0},{12,4},{16,24},{20,28},{24,16},{28,20},{1,9},{5... | collective-permute-start | bytes 393224 | tf_op jit(solution)/shard_map/ppermute | solution.py:137
  69.4 10.5 %collective-permute-start.17 = (bf16[2,256,128]{2,1,0:T(8,128)(2,1)S(1)}, bf16[2,256,128]{2,1,0:T(8,128)(2,1)S(1)}, u32[]{:S(2)}, u32[]{:S(2)}) collective-permute-start(bf16[2,256,128]{2,1,0:T(8,128)(2,1)S(1)} %get-tuple-element.120), channel_id=1, source_target_pairs={{0,24},{4,28},{8,16},{12,20},{16,8},{20,12},{24,0},{28,4},{1,25},{... | collective-permute-start | bytes 393224 | tf_op jit(solution)/shard_map/ppermute | solution.py:137
  70.9 12.4 %collective-permute-start.7 = (bf16[320,512]{1,0:T(8,128)(2,1)}, bf16[320,512]{1,0:T(8,128)(2,1)S(1)}, u32[]{:S(2)}, u32[]{:S(2)}) collective-permute-start(bf16[320,512]{1,0:T(8,128)(2,1)} %collective-permute-done.6), channel_id=1, source_target_pairs={{0,4},{4,0},{8,12},{12,8},{16,20},{20,16},{24,28},{28,24},{1,5},{5... | collective-permute-start | bytes 983048 | tf_op jit(solution)/shard_map/ppermute | solution.py:148
  76.3 14.3 %collective-permute-start.24 = (bf16[320,512]{1,0:T(8,128)(2,1)S(1)}, bf16[320,512]{1,0:T(8,128)(2,1)}, u32[]{:S(2)}, u32[]{:S(2)}) collective-permute-start(bf16[320,512]{1,0:T(8,128)(2,1)S(1)} %copy-done.16), channel_id=1, source_target_pairs={{0,8},{4,12},{8,0},{12,4},{16,24},{20,28},{24,16},{28,20},{1,9},{5... | collective-permute-start | bytes 983048 | tf_op jit(solution)/shard_map/ppermute | solution.py:137
  77.1 25.1 %collective-permute-start.26 = (bf16[320,512]{1,0:T(8,128)(2,1)S(1)}, bf16[320,512]{1,0:T(8,128)(2,1)}, u32[]{:S(2)}, u32[]{:S(2)}) collective-permute-start(bf16[320,512]{1,0:T(8,128)(2,1)S(1)} %copy-done.16), channel_id=1, source_target_pairs={{0,16},{4,20},{8,24},{12,28},{16,0},{20,4},{24,8},{28,12},{1,17},{... | collective-permute-start | bytes 983048 | tf_op jit(solution)/shard_map/ppermute | solution.py:137
  79.9 23.7 %collective-permute-start.28 = (bf16[320,512]{1,0:T(8,128)(2,1)S(1)}, bf16[320,512]{1,0:T(8,128)(2,1)S(1)}, u32[]{:S(2)}, u32[]{:S(2)}) collective-permute-start(bf16[320,512]{1,0:T(8,128)(2,1)S(1)} %copy-done.16), channel_id=1, source_target_pairs={{0,24},{4,28},{8,16},{12,20},{16,8},{20,12},{24,0},{28,4},{1,25},{... | collective-permute-start | bytes 983048 | tf_op jit(solution)/shard_map/ppermute | solution.py:137
  88.1 37.9 %collective-permute-start.18 = (f32[2,256,640]{2,1,0:T(8,128)}, f32[2,256,640]{2,1,0:T(8,128)}, u32[]{:S(2)}, u32[]{:S(2)}) collective-permute-start(f32[2,256,640]{2,1,0:T(8,128)} %dynamic-slice_bitcast_fusion.1), channel_id=1, source_target_pairs={{0,1},{1,0},{2,3},{3,2},{4,5},{5,4},{6,7},{7,6},{8,9},{9,8},{10,11... | collective-permute-start | bytes 3932168 | tf_op jit(solution)/shard_map/ppermute | solution.py:144
  88.2 16.1 %collective-permute-start.45 = (s32[1,1024]{1,0:T(1,128)S(1)}, s32[1,1024]{1,0:T(1,128)S(1)}, u32[]{:S(2)}, u32[]{:S(2)}) collective-permute-start(s32[1,1024]{1,0:T(1,128)S(1)} %bitcast.325), channel_id=1, source_target_pairs={{0,4},{4,0},{8,12},{12,8},{16,20},{20,16},{24,28},{28,24},{1,5},{5... | collective-permute-start | bytes 12296 | tf_op jit(solution)/shard_map/ppermute | solution.py:148
  90.6 15.7 %collective-permute-start.23 = (bf16[320,512]{1,0:T(8,128)(2,1)S(1)}, bf16[320,512]{1,0:T(8,128)(2,1)S(1)}, u32[]{:S(2)}, u32[]{:S(2)}) collective-permute-start(bf16[320,512]{1,0:T(8,128)(2,1)S(1)} %copy-done.16), channel_id=1, source_target_pairs={{0,4},{4,0},{8,12},{12,8},{16,20},{20,16},{24,28},{28,24},{1,5},{5... | collective-permute-start | bytes 983048 | tf_op jit(solution)/shard_map/ppermute | solution.py:148
  102.3 10.8 %collective-permute-start.25 = (bf16[320,512]{1,0:T(8,128)(2,1)}, bf16[320,512]{1,0:T(8,128)(2,1)S(1)}, u32[]{:S(2)}, u32[]{:S(2)}) collective-permute-start(bf16[320,512]{1,0:T(8,128)(2,1)} %collective-permute-done.24), channel_id=1, source_target_pairs={{0,4},{4,0},{8,12},{12,8},{16,20},{20,16},{24,28},{28,24},{1,5},{5... | collective-permute-start | bytes 983048 | tf_op jit(solution)/shard_map/ppermute | solution.py:148
  103.6 14.3 %collective-permute-start.27 = (bf16[320,512]{1,0:T(8,128)(2,1)}, bf16[320,512]{1,0:T(8,128)(2,1)S(1)}, u32[]{:S(2)}, u32[]{:S(2)}) collective-permute-start(bf16[320,512]{1,0:T(8,128)(2,1)} %collective-permute-done.26), channel_id=1, source_target_pairs={{0,4},{4,0},{8,12},{12,8},{16,20},{20,16},{24,28},{28,24},{1,5},{5... | collective-permute-start | bytes 983048 | tf_op jit(solution)/shard_map/ppermute | solution.py:148
  104.3 20.1 %collective-permute-start.29 = (bf16[320,512]{1,0:T(8,128)(2,1)S(1)}, bf16[320,512]{1,0:T(8,128)(2,1)S(1)}, u32[]{:S(2)}, u32[]{:S(2)}) collective-permute-start(bf16[320,512]{1,0:T(8,128)(2,1)S(1)} %collective-permute-done.28), channel_id=1, source_target_pairs={{0,4},{4,0},{8,12},{12,8},{16,20},{20,16},{24,28},{28,24},{1,5},{5... | collective-permute-start | bytes 983048 | tf_op jit(solution)/shard_map/ppermute | solution.py:148
  106.3 22.8 %collective-permute-start.33 = (bf16[320,384]{1,0:T(8,128)(2,1)S(1)}, bf16[320,384]{1,0:T(8,128)(2,1)S(1)}, u32[]{:S(2)}, u32[]{:S(2)}) collective-permute-start(bf16[320,384]{1,0:T(8,128)(2,1)S(1)} %get-tuple-element.95), channel_id=1, source_target_pairs={{0,8},{4,12},{8,0},{12,4},{16,24},{20,28},{24,16},{28,20},{1,9},{5... | collective-permute-start | bytes 737288 | tf_op jit(solution)/shard_map/ppermute | solution.py:137
  113.1 16.9 %collective-permute-start.35 = (bf16[320,384]{1,0:T(8,128)(2,1)S(1)}, bf16[320,384]{1,0:T(8,128)(2,1)S(1)}, u32[]{:S(2)}, u32[]{:S(2)}) collective-permute-start(bf16[320,384]{1,0:T(8,128)(2,1)S(1)} %get-tuple-element.94), channel_id=1, source_target_pairs={{0,16},{4,20},{8,24},{12,28},{16,0},{20,4},{24,8},{28,12},{1,17},{... | collective-permute-start | bytes 737288 | tf_op jit(solution)/shard_map/ppermute | solution.py:137
  117.9 13.3 %collective-permute-start.37 = (bf16[320,384]{1,0:T(8,128)(2,1)S(1)}, bf16[320,384]{1,0:T(8,128)(2,1)S(1)}, u32[]{:S(2)}, u32[]{:S(2)}) collective-permute-start(bf16[320,384]{1,0:T(8,128)(2,1)S(1)} %get-tuple-element.93), channel_id=1, source_target_pairs={{0,24},{4,28},{8,16},{12,20},{16,8},{20,12},{24,0},{28,4},{1,25},{... | collective-permute-start | bytes 737288 | tf_op jit(solution)/shard_map/ppermute | solution.py:137
  124.4 11.6 %collective-permute-start.32 = (bf16[320,384]{1,0:T(8,128)(2,1)S(1)}, bf16[320,384]{1,0:T(8,128)(2,1)S(1)}, u32[]{:S(2)}, u32[]{:S(2)}) collective-permute-start(bf16[320,384]{1,0:T(8,128)(2,1)S(1)} %get-tuple-element.59), channel_id=1, source_target_pairs={{0,4},{4,0},{8,12},{12,8},{16,20},{20,16},{24,28},{28,24},{1,5},{5... | collective-permute-start | bytes 737288 | tf_op jit(solution)/shard_map/ppermute | solution.py:148
  127.6 7.2 %collective-permute-start.19 = (bf16[256,640]{1,0:T(8,128)(2,1)S(1)}, bf16[256,640]{1,0:T(8,128)(2,1)S(1)}, u32[]{:S(2)}, u32[]{:S(2)}) collective-permute-start(bf16[256,640]{1,0:T(8,128)(2,1)S(1)} %fusion.89), channel_id=1, source_target_pairs={{0,2},{1,3},{2,0},{3,1},{4,6},{5,7},{6,4},{7,5},{8,10},{9,11},{10,... | collective-permute-start | bytes 983048 | tf_op jit(solution)/shard_map/ppermute | solution.py:144
  129.1 8.3 %collective-permute-start.34 = (bf16[320,384]{1,0:T(8,128)(2,1)S(1)}, bf16[320,384]{1,0:T(8,128)(2,1)S(1)}, u32[]{:S(2)}, u32[]{:S(2)}) collective-permute-start(bf16[320,384]{1,0:T(8,128)(2,1)S(1)} %collective-permute-done.33), channel_id=1, source_target_pairs={{0,4},{4,0},{8,12},{12,8},{16,20},{20,16},{24,28},{28,24},{1,5},{5... | collective-permute-start | bytes 737288 | tf_op jit(solution)/shard_map/ppermute | solution.py:148
  130.0 10.7 %collective-permute-start.36 = (bf16[320,384]{1,0:T(8,128)(2,1)S(1)}, bf16[320,384]{1,0:T(8,128)(2,1)S(1)}, u32[]{:S(2)}, u32[]{:S(2)}) collective-permute-start(bf16[320,384]{1,0:T(8,128)(2,1)S(1)} %collective-permute-done.35), channel_id=1, source_target_pairs={{0,4},{4,0},{8,12},{12,8},{16,20},{20,16},{24,28},{28,24},{1,5},{5... | collective-permute-start | bytes 737288 | tf_op jit(solution)/shard_map/ppermute | solution.py:148
  131.2 11.3 %collective-permute-start.38 = (bf16[320,384]{1,0:T(8,128)(2,1)S(1)}, bf16[320,384]{1,0:T(8,128)(2,1)S(1)}, u32[]{:S(2)}, u32[]{:S(2)}) collective-permute-start(bf16[320,384]{1,0:T(8,128)(2,1)S(1)} %collective-permute-done.37), channel_id=1, source_target_pairs={{0,4},{4,0},{8,12},{12,8},{16,20},{20,16},{24,28},{28,24},{1,5},{5... | collective-permute-start | bytes 737288 | tf_op jit(solution)/shard_map/ppermute | solution.py:148
  135.9 8.9 %collective-permute-start.39 = (bf16[256,640]{1,0:T(8,128)(2,1)S(1)}, bf16[256,640]{1,0:T(8,128)(2,1)S(1)}, u32[]{:S(2)}, u32[]{:S(2)}) collective-permute-start(bf16[256,640]{1,0:T(8,128)(2,1)S(1)} %get-tuple-element.68), channel_id=1, source_target_pairs={{0,8},{4,12},{8,0},{12,4},{16,24},{20,28},{24,16},{28,20},{1,9},{5... | collective-permute-start | bytes 983048 | tf_op jit(solution)/shard_map/ppermute | solution.py:137
  136.0 8.9 %collective-permute-start.20 = (bf16[256,640]{1,0:T(8,128)(2,1)S(1)}, bf16[256,640]{1,0:T(8,128)(2,1)S(1)}, u32[]{:S(2)}, u32[]{:S(2)}) collective-permute-start(bf16[256,640]{1,0:T(8,128)(2,1)S(1)} %get-tuple-element.68), channel_id=1, source_target_pairs={{0,2},{1,3},{2,0},{3,1},{4,6},{5,7},{6,4},{7,5},{8,10},{9,11},{10,... | collective-permute-start | bytes 983048 | tf_op jit(solution)/shard_map/ppermute | solution.py:144
  137.4 14.4 %collective-permute-start.41 = (bf16[256,640]{1,0:T(8,128)(2,1)S(1)}, bf16[256,640]{1,0:T(8,128)(2,1)S(1)}, u32[]{:S(2)}, u32[]{:S(2)}) collective-permute-start(bf16[256,640]{1,0:T(8,128)(2,1)S(1)} %get-tuple-element.68), channel_id=1, source_target_pairs={{0,24},{4,28},{8,16},{12,20},{16,8},{20,12},{24,0},{28,4},{1,25},{... | collective-permute-start | bytes 983048 | tf_op jit(solution)/shard_map/ppermute | solution.py:137
  140.7 23.1 %collective-permute-start.21 = (bf16[256,640]{1,0:T(8,128)(2,1)S(1)}, bf16[256,640]{1,0:T(8,128)(2,1)S(1)}, u32[]{:S(2)}, u32[]{:S(2)}) collective-permute-start(bf16[256,640]{1,0:T(8,128)(2,1)S(1)} %get-tuple-element.68), channel_id=1, source_target_pairs={{0,16},{4,20},{8,24},{12,28},{16,0},{20,4},{24,8},{28,12},{1,17},{... | collective-permute-start | bytes 983048 | tf_op jit(solution)/shard_map/ppermute | solution.py:137
  145.0 26.3 %collective-permute-start.30 = (bf16[2,256,640]{2,1,0:T(8,128)(2,1)S(1)}, bf16[2,256,640]{2,1,0:T(8,128)(2,1)S(1)}, u32[]{:S(2)}, u32[]{:S(2)}) collective-permute-start(bf16[2,256,640]{2,1,0:T(8,128)(2,1)S(1)} %pad_maximum_fusion.6), channel_id=1, source_target_pairs={{0,1},{1,0},{2,3},{3,2},{4,5},{5,4},{6,7},{7,6},{8,9},{9,8},{10,11... | collective-permute-start | bytes 1966088 | tf_op jit(solution)/shard_map/ppermute | solution.py:144
  145.5 20.2 %collective-permute-start.40 = (bf16[256,640]{1,0:T(8,128)(2,1)S(1)}, bf16[256,640]{1,0:T(8,128)(2,1)S(1)}, u32[]{:S(2)}, u32[]{:S(2)}) collective-permute-start(bf16[256,640]{1,0:T(8,128)(2,1)S(1)} %collective-permute-done.39), channel_id=1, source_target_pairs={{0,2},{1,3},{2,0},{3,1},{4,6},{5,7},{6,4},{7,5},{8,10},{9,11},{10,... | collective-permute-start | bytes 983048 | tf_op jit(solution)/shard_map/ppermute | solution.py:144
  151.8 13.7 %collective-permute-start.42 = (bf16[256,640]{1,0:T(8,128)(2,1)S(1)}, bf16[256,640]{1,0:T(8,128)(2,1)S(1)}, u32[]{:S(2)}, u32[]{:S(2)}) collective-permute-start(bf16[256,640]{1,0:T(8,128)(2,1)S(1)} %collective-permute-done.41), channel_id=1, source_target_pairs={{0,2},{1,3},{2,0},{3,1},{4,6},{5,7},{6,4},{7,5},{8,10},{9,11},{10,... | collective-permute-start | bytes 983048 | tf_op jit(solution)/shard_map/ppermute | solution.py:144
  163.8 7.1 %collective-permute-start.22 = (bf16[256,640]{1,0:T(8,128)(2,1)S(1)}, bf16[256,640]{1,0:T(8,128)(2,1)S(1)}, u32[]{:S(2)}, u32[]{:S(2)}) collective-permute-start(bf16[256,640]{1,0:T(8,128)(2,1)S(1)} %collective-permute-done.21), channel_id=1, source_target_pairs={{0,2},{1,3},{2,0},{3,1},{4,6},{5,7},{6,4},{7,5},{8,10},{9,11},{10,... | collective-permute-start | bytes 983048 | tf_op jit(solution)/shard_map/ppermute | solution.py:144
  171.0 6.4 %collective-permute-start.31 = (bf16[2,256,640]{2,1,0:T(8,128)(2,1)S(1)}, bf16[2,256,640]{2,1,0:T(8,128)(2,1)S(1)}, u32[]{:S(2)}, u32[]{:S(2)}) collective-permute-start(bf16[2,256,640]{2,1,0:T(8,128)(2,1)S(1)} %pad_maximum_fusion.7), channel_id=1, source_target_pairs={{0,1},{1,0},{2,3},{3,2},{4,5},{5,4},{6,7},{7,6},{8,9},{9,8},{10,11... | collective-permute-start | bytes 1966088 | tf_op jit(solution)/shard_map/ppermute | solution.py:144
  175.9 9.1 %collective-permute-start.47 = (bf16[512,256]{1,0:T(8,128)(2,1)S(1)}, bf16[512,256]{1,0:T(8,128)(2,1)S(1)}, u32[]{:S(2)}, u32[]{:S(2)}) collective-permute-start(bf16[512,256]{1,0:T(8,128)(2,1)S(1)} %fusion.95), channel_id=1, source_target_pairs={{0,4},{4,0},{8,12},{12,8},{16,20},{20,16},{24,28},{28,24},{1,5},{5... | collective-permute-start | bytes 786440 | tf_op jit(solution)/shard_map/ppermute | solution.py:148
  181.3 8.8 %collective-permute-start.46 = (bf16[512,256]{1,0:T(8,128)(2,1)S(1)}, bf16[512,256]{1,0:T(8,128)(2,1)S(1)}, u32[]{:S(2)}, u32[]{:S(2)}) collective-permute-start(bf16[512,256]{1,0:T(8,128)(2,1)S(1)} %fusion.96), channel_id=1, source_target_pairs={{0,4},{4,0},{8,12},{12,8},{16,20},{20,16},{24,28},{28,24},{1,5},{5... | collective-permute-start | bytes 786440 | tf_op jit(solution)/shard_map/ppermute | solution.py:148
  199.9 7.5 %collective-permute-start.48 = (bf16[256,128]{1,0:T(8,128)(2,1)S(1)}, bf16[256,128]{1,0:T(8,128)(2,1)S(1)}, u32[]{:S(2)}, u32[]{:S(2)}) collective-permute-start(bf16[256,128]{1,0:T(8,128)(2,1)S(1)} %get-tuple-element.112), channel_id=1, source_target_pairs={{0,8},{4,12},{8,0},{12,4},{16,24},{20,28},{24,16},{28,20},{1,9},{5... | collective-permute-start | bytes 196616 | tf_op jit(solution)/shard_map/ppermute | solution.py:137
  200.5 11.0 %collective-permute-start.49 = (bf16[256,128]{1,0:T(8,128)(2,1)S(1)}, bf16[256,128]{1,0:T(8,128)(2,1)S(1)}, u32[]{:S(2)}, u32[]{:S(2)}) collective-permute-start(bf16[256,128]{1,0:T(8,128)(2,1)S(1)} %get-tuple-element.111), channel_id=1, source_target_pairs={{0,16},{4,20},{8,24},{12,28},{16,0},{20,4},{24,8},{28,12},{1,17},{... | collective-permute-start | bytes 196616 | tf_op jit(solution)/shard_map/ppermute | solution.py:137
  217.9 9.9 %collective-permute-start.52 = (bf16[256,640]{1,0:T(8,128)(2,1)S(1)}, bf16[256,640]{1,0:T(8,128)(2,1)}, u32[]{:S(2)}, u32[]{:S(2)}) collective-permute-start(bf16[256,640]{1,0:T(8,128)(2,1)S(1)} %fusion.90), channel_id=1, source_target_pairs={{0,2},{1,3},{2,0},{3,1},{4,6},{5,7},{6,4},{7,5},{8,10},{9,11},{10,... | collective-permute-start | bytes 983048 | tf_op jit(solution)/shard_map/ppermute | solution.py:144
  (33 other events, 334.4 us)
where the time goes:
time: 252 us; the launch traced here: 251 us
  waiting for transfers between devices  99.3 us (39%)
  starting transfers between devices  68.4 us (27%)
  local copies, waits for them, and re-layouts  23.9 us (9%)
  blocking collectives  20.7 us (8%)
  matrix products  15.7 us (6%)
  other arithmetic  13.9 us (6%)
  Pallas kernels  8.18 us (3%)
    ppermute x22, waiting for transfers between devices, swap_z(): lax.ppermute(value, 'seq', [(a * across + b, (a ^ k) * across + b) for a...  61.2 us
    ppermute x22, starting transfers between devices, swap_z(): lax.ppermute(value, 'seq', [(a * across + b, (a ^ k) * across + b) for a...  40.6 us
    all_to_all x1, blocking collectives, shards(): lax.all_to_all(spread, 'seq', split_axis=0, concat_axis=0, tiled=True)  20.7 us
    ppermute x14, waiting for transfers between devices, swap_t(): lax.ppermute(value, 'tensor', [(a, a ^ k) for a in range(tensor_count)])  19.7 us
    ppermute x17, waiting for transfers between devices, from_x(): lax.ppermute(value, 'seq', [(a, a ^ 1) for a in range(seq_count)])  18.5 us
    ppermute x17, starting transfers between devices, from_x(): lax.ppermute(value, 'seq', [(a, a ^ 1) for a in range(seq_count)])  17.9 us
    ppermute x14, starting transfers between devices, swap_t(): lax.ppermute(value, 'tensor', [(a, a ^ k) for a in range(tensor_count)])  9.9 us
    unnamed x76, local copies, waits for them, and re-layouts  9.3 us
  transfers between devices with their start and end apart: 53, of which 24 were waited for; matrix products, arithmetic and copies ran while one was open for 16% of the time, Pallas kernels for 0%

commit v1 on v0

--- a/solution.py
+++ b/solution.py
@@ -37,64 +37,202 @@
     )
 
 
-def global_kernel(own_ref, query_a, query_b, place_ref, codes_ref, heads_a, heads_b, *refs):
-    *pair_refs, out_ref = refs
-    tile, width = out_ref.shape
-    step, half = pl.program_id(0), pl.num_programs(0) // 2
-    query = jnp.where(step < half, query_a[...], query_b[...])
-    contract = (((1,), (1,)), ((), ()))
-    apart = len(pair_refs) == 2
-    blocks = [(ref, width, width * 2, True) for ref in (heads_a, heads_b)] if apart else []
-    blocks += [(ref, 0, width, not apart) for ref in pair_refs]
-    ident = own_ref[0] + step * tile + lax.broadcasted_iota(jnp.int32, (tile, 1), 0)
+def scores_over(query, place, ident, codes_ref, pair_refs, own):
+    width = query.shape[1]
+    factor = width ** (-0.5) * math.log2(math.e)
     parts, begin = [], 0
-    for ref, key, _, own in blocks:
+    for ref in pair_refs:
         keys = ref.shape[0]
         scores = lax.dot_general(
-            query, ref[:, key : key + width], contract, preferred_element_type=jnp.float32
-        )
-        allowed = place_ref[...] == codes_ref[:, begin : begin + keys]
+            query, ref[:, :width], (((1,), (1,)), ((), ())), preferred_element_type=jnp.float32
+        )
+        allowed = place == codes_ref[:, begin : begin + keys]
         if own:
             columns = lax.broadcasted_iota(jnp.int32, scores.shape, 1) + begin
             allowed = allowed | (ident == columns)
         parts.append(jnp.where(allowed, scores, -jnp.inf))
         begin += keys
     top = functools.reduce(jnp.maximum, [jnp.max(p, axis=-1, keepdims=True) for p in parts])
+    return parts, top, factor
+
+
+def weigh(parts, top, factor, pair_refs, width):
     total, mixed = 0.0, 0.0
-    factor = width ** (-0.5) * math.log2(math.e)
-    for (ref, _, value, _), scores in zip(blocks, parts, strict=True):
+    for ref, scores in zip(pair_refs, parts, strict=True):
         weights = jnp.exp2((scores - top) * factor)
         total = total + jnp.sum(weights, axis=-1, keepdims=True)
         mixed = mixed + jnp.dot(
-            weights.astype(jnp.bfloat16),
-            ref[:, value : value + width],
-            preferred_element_type=jnp.float32,
-        )
-    out_ref[...] = (mixed / total).astype(out_ref.dtype)
-
-
-def global_attend(own, place, codes, heads_a, heads_b, pairs, tile):
-    rows = heads_a.shape[0]
-    width = heads_a.shape[1] // 3
+            weights.astype(jnp.bfloat16), ref[:, width:], preferred_element_type=jnp.float32
+        )
+    return total, mixed
+
+
+def own_kernel(own_ref, query_a, query_b, place_ref, codes_ref, *refs):
+    *pair_refs, top_ref, total_ref, mixed_ref = refs
+    tile, width = mixed_ref.shape
+    step, half = pl.program_id(0), pl.num_programs(0) // 2
+    query = jnp.where(step < half, query_a[...], query_b[...])
+    ident = own_ref[0] + step * tile + lax.broadcasted_iota(jnp.int32, (tile, 1), 0)
+    parts, top, factor = scores_over(query, place_ref[...], ident, codes_ref, pair_refs, True)
+    total, mixed = weigh(parts, top, factor, pair_refs, width)
+    top_ref[...], total_ref[...], mixed_ref[...] = top, total, mixed
+
+
+def rest_kernel(query_a, query_b, place_ref, codes_ref, top_ref, total_ref, mixed_ref, *refs):
+    *pair_refs, out_ref = refs
+    _, width = out_ref.shape
+    step, half = pl.program_id(0), pl.num_programs(0) // 2
+    query = jnp.where(step < half, query_a[...], query_b[...])
+    parts, top, factor = scores_over(query, place_ref[...], None, codes_ref, pair_refs, False)
+    before = top_ref[...]
+    top = jnp.maximum(top, before)
+    total, mixed = weigh(parts, top, factor, pair_refs, width)
+    scale = jnp.exp2((before - top) * factor)
+    total = total + total_ref[...] * scale
+    out_ref[...] = ((mixed + mixed_ref[...] * scale) / total).astype(out_ref.dtype)
+
+
+def global_attend(own, place, codes, query_a, query_b, pairs, tile):
+    rows, width = query_a.shape
     half = rows // tile
-    whole = [heads_a, heads_b, *pairs]
+    first = not isinstance(own, tuple)
+
+    def by_tile(columns):
+        return pl.BlockSpec((tile, columns), lambda i: (i, 0))
+
+    specs = [
+        pl.BlockSpec((tile, width), lambda i: (jnp.minimum(i, half - 1), 0)),
+        pl.BlockSpec((tile, width), lambda i: (jnp.maximum(i - half, 0), 0)),
+        by_tile(1),
+        pl.BlockSpec(codes.shape, lambda i: (0, 0)),
+    ]
+    pair_specs = [pl.BlockSpec(p.shape, lambda i: (0, 0)) for p in pairs]
+    kinds = [
+        jax.ShapeDtypeStruct((2 * rows, columns), kind)
+        for columns, kind in (
+            ((1, jnp.float32), (1, jnp.float32), (width, jnp.float32))
+            if first
+            else ((width, query_a.dtype),)
+        )
+    ]
+    if first:
+        return pl.pallas_call(
+            own_kernel,
+            grid=(2 * half,),
+            in_specs=[pl.BlockSpec(memory_space=pltpu.SMEM), *specs, *pair_specs],
+            out_specs=[by_tile(1), by_tile(1), by_tile(width)],
+            out_shape=kinds,
+            name="own_attend",
+        )(own, query_a, query_b, place, codes, *pairs)
     return pl.pallas_call(
-        global_kernel,
-        grid_spec=pltpu.PrefetchScalarGridSpec(
-            num_scalar_prefetch=1,
-            grid=(2 * half,),
-            in_specs=[
-                pl.BlockSpec((tile, width), lambda i, _: (jnp.minimum(i, half - 1), 0)),
-                pl.BlockSpec((tile, width), lambda i, _: (jnp.maximum(i - half, 0), 0)),
-                pl.BlockSpec((tile, 1), lambda i, _: (i, 0)),
-                pl.BlockSpec(codes.shape, lambda i, _: (0, 0)),
-            ]
-            + [pl.BlockSpec(p.shape, lambda i, _: (0, 0)) for p in whole],
-            out_specs=pl.BlockSpec((tile, width), lambda i, _: (i, 0)),
-        ),
-        out_shape=jax.ShapeDtypeStruct((2 * rows, width), heads_a.dtype),
-        name="global_attend",
-    )(own, heads_a, heads_b, place, codes, *whole)
+        rest_kernel,
+        grid=(2 * half,),
+        in_specs=[*specs, by_tile(1), by_tile(1), by_tile(width), *pair_specs],
+        out_specs=by_tile(width),
+        out_shape=kinds[0],
+        name="rest_attend",
+    )(query_a, query_b, place, codes, *own, *pairs)
+
+
+def fill(table_ref, piece_refs, spots_ref):
+    parts = table_ref.shape[0]
+    across = len(piece_refs) // parts
+    for i, ref in enumerate(piece_refs):
+        at, spot = spots_ref[i // across], spots_ref[parts + i % across]
+        rows = ref.shape[0]
+        table_ref[at, pl.ds(pl.multiple_of(spot * rows, rows), rows), :] = ref[...]
+
+
+def whole_vmem(count):
+    return [pl.BlockSpec(memory_space=pltpu.VMEM)] * count
+
+
+def rows_kernel(bits_ref, spots_ref, gains_ref, *refs):
+    *refs, query_ref, pair_ref, table_ref = refs
+    own, own_y, far, far_y = refs[0:2], refs[2:4], refs[4:6], refs[6:8]
+    fill(table_ref, refs[8:], spots_ref)
+    upper, high, low = bits_ref[0], bits_ref[1], bits_ref[2]
+    rows, width = own[0].shape[0], query_ref.shape[1]
+    choices = (
+        (high, (own[0], far[0], own_y[1], far_y[1])),
+        (1 - high, (own_y[0], far_y[0], own[1], far[1])),
+    )
+    for row, parts in choices:
+        floats = [ref[...].astype(jnp.float32) for ref in parts]
+        count = sum(f.shape[1] for f in floats)
+        mean = sum(jnp.sum(f, axis=-1, keepdims=True) for f in floats) / count
+        floats = [f - mean for f in floats]
+        spread = sum(jnp.sum(f * f, axis=-1, keepdims=True) for f in floats) / count
+        total = None
+        for i, f in enumerate(floats):
+            half = upper if i < 2 else 1 - upper
+            quarter = 2 * half + (low if i % 2 == 0 else 1 - low)
+            ready = (f * gains_ref[quarter]).astype(jnp.bfloat16)
+            product = jnp.dot(ready, table_ref[quarter], preferred_element_type=jnp.float32)
+            total = product if total is None else total + product
+        heads = (total * lax.rsqrt(spread + EPSILON)).astype(query_ref.dtype)
+        begin = pl.multiple_of(row * rows, rows)
+        query_ref[pl.ds(begin, rows), :] = heads[:, :width]
+        pair_ref[pl.ds(begin, rows), :] = heads[:, width:]
+
+
+def project_rows(bits, spots, gains, own, own_y, far, far_y, pieces, head):
+    rows, share = own[0].shape
+    operands = [*own, *own_y, *far, *far_y, *pieces]
+    kind = own[0].dtype
+    return pl.pallas_call(
+        rows_kernel,
+        in_specs=[pl.BlockSpec(memory_space=pltpu.SMEM)] * 2 + whole_vmem(1 + len(operands)),
+        out_specs=whole_vmem(2),
+        out_shape=[
+            jax.ShapeDtypeStruct((2 * rows, head), kind),
+            jax.ShapeDtypeStruct((2 * rows, 2 * head), kind),
+        ],
+        scratch_shapes=[pltpu.VMEM((gains.shape[0], share, 3 * head), kind)],
+        name="project_rows",
+    )(bits, spots, gains, *operands)
+
+
+def back_kernel(bits_ref, spots_ref, *refs):
+    *refs, keep_ref, send_ref, row_ref, table_ref = refs
+    depth = row_ref.shape[2] // refs[0].shape[2]
+    fill(table_ref, refs[depth:], spots_ref)
+    low, head = bits_ref[2], refs[0].shape[2]
+    for k in range(depth):
+        begin = pl.multiple_of(bits_ref[3 + k] * head, head)
+        row_ref[:, :, pl.ds(begin, head)] = refs[k][...]
+    contract = (((1,), (1,)), ((), ()))
+    apart = row_ref.shape[0] == 2
+    for i in range(2):
+        row = row_ref[i if apart else 0]
+        keep, send = (low, 1 - low) if apart else (2 * i + low, 2 * i + 1 - low)
+        keep_ref[i] = lax.dot_general(
+            row, table_ref[keep], contract, preferred_element_type=jnp.float32
+        )
+        send_ref[i] = lax.dot_general(
+            row, table_ref[send], contract, preferred_element_type=jnp.float32
+        ).astype(send_ref.dtype)
+
+
+def project_back(bits, spots, mixed, pieces, parts, share):
+    groups, rows, head = mixed[0].shape
+    kind = mixed[0].dtype
+    width = len(mixed) * head
+    return pl.pallas_call(
+        back_kernel,
+        in_specs=[pl.BlockSpec(memory_space=pltpu.SMEM)] * 2
+        + whole_vmem(len(mixed) + len(pieces)),
+        out_specs=whole_vmem(2),
+        out_shape=[
+            jax.ShapeDtypeStruct((2, rows, share), jnp.float32),
+            jax.ShapeDtypeStruct((2, rows, share), kind),
+        ],
+        scratch_shapes=[
+            pltpu.VMEM((groups, rows, width), kind),
+            pltpu.VMEM((parts, share, width), kind),
+        ],
+        name="project_back",
+    )(bits, spots, *mixed, *pieces)
 
 
 def after(value, *others):
@@ -153,15 +291,22 @@
     def pick(stacked, index, axis=0):
         return lax.dynamic_index_in_dim(stacked, index, axis, keepdims=False)
 
+    spots_x = [x, 1 - x] if across == 2 else list(range(across))
+
     def place(pieces, order, tie):
         pieces, _ = lax.optimization_barrier((pieces, tie))
         shape = (len(pieces), across) + pieces[0][0].shape
         placed = jnp.zeros(shape, pieces[0][0].dtype)
-        spots = [x, 1 - x] if across == 2 else range(across)
         for every, at in zip(pieces, order, strict=True):
-            for piece, spot in zip(every, spots, strict=True):
+            for piece, spot in zip(every, spots_x, strict=True):
                 placed = lax.dynamic_update_slice(placed, piece[None, None], (at, spot, 0, 0))
         return placed.reshape(shape[0], shape[1] * shape[2], shape[3])
+
+    def integers(values):
+        return jnp.stack([jnp.asarray(v, jnp.int32) for v in values])
+
+    def flat(lists):
+        return [piece for every in lists for piece in every]
 
     def send_heads(by_head):
         return [pick(by_head, z)] + [swap_z(pick(by_head, z ^ k), k) for k in range(1, depth)]
@@ -219,75 +364,69 @@
         local_heads.reshape(windows_held, slots, 3 * head), allowed, head
     ).reshape(depth, rows_here, head)
 
-    low, high = t & 1, t >> 1
-
-    def gather_sum(partial):
-        half = pick(partial, low, 1) + swap_t(pick(partial, 1 - low, 1), 1)
-        sent = pick(half, 1 - high).astype(jnp.bfloat16)
-        return pick(half, high) + swap_t(sent, 2).astype(jnp.float32)
+    low, high, upper = t & 1, t >> 1, z >> 1
+    bits = integers([upper, high, low, *natural])
+    spots_whole = integers([*natural, *spots_x])
+    spots_half = integers([z & 1, 1 - (z & 1), *spots_x])
+
+    def gather_sum(keep, send):
+        come = swap_t(send, 1)
+
+        def part(index):
+            return pick(keep, index) + pick(come, index).astype(jnp.float32)
+
+        other = swap_t(part(1 - high).astype(jnp.bfloat16), 2)
+        return part(high) + other.astype(jnp.float32)
 
     got = [jnp.stack([local_mixed[k], local_mixed[k ^ 2]]) for k in range(depth)]
-    got = jnp.stack([got[0]] + [swap_z(got[k], k) for k in range(1, depth)])
-    row = jnp.concatenate([pick(got, z ^ k) for k in range(depth)], axis=-1)
-    local_back = place(back_x, [z & 1, 1 - (z & 1)], local_mixed)
-    partial = jnp.einsum("jrc,qdc->jqrd", row, local_back, preferred_element_type=jnp.float32)
+    got = [got[0]] + [swap_z(got[k], k) for k in range(1, depth)]
+    parts = project_back(bits, spots_half, got, flat(back_x), 2, share)
     start_here = lax.dynamic_slice(
-        start,
-        (2 * high * rows_here, (2 * (z >> 1) + low) * share),
-        (rows_here, share),
-    )
-    after_local = (start_here.astype(jnp.float32) + gather_sum(partial)).astype(jnp.bfloat16)
-
-    pieces = [after_local] + [swap_z(after_local, k) for k in range(1, depth)]
+        start, (2 * high * rows_here, (2 * upper + low) * share), (rows_here, share)
+    )
+    after_local = (start_here.astype(jnp.float32) + gather_sum(*parts)).astype(jnp.bfloat16)
+
+    pieces = [after_local] + [swap_z(after_local, k) for k in (1, 2)]
+    pieces.append(swap_z(after(after_local, pieces[1]), 3))
     pieces_y = [swap_t(pieces[k], 2) for k in range(depth)]
-    global_full = place(far_x, natural, pieces[1]).reshape(width, 3 * head)
-
-    def project_rows(parts):
-        every = jnp.concatenate(parts)
-        heads = []
-        for i in range(2):
-            quarters = []
-            for quarter in range(tensor_count):
-                plane = (z >> 1) ^ (quarter >> 1)
-                spot = 4 * (low ^ (quarter & 1)) + 2 * plane + (i ^ plane ^ high)
-                quarters.append(pick(every, spot))
-            rows = jnp.concatenate(quarters, axis=1)
-            heads.append(
-                jnp.dot(
-                    normed(rows, global_gain), global_full, preferred_element_type=jnp.float32
-                ).astype(jnp.bfloat16)
-            )
-        return jnp.concatenate(heads, axis=0)
-
-    near = [jnp.stack([pieces[k], pieces_y[k]]) for k in range(depth)]
-    far = [swap_t(near[k], 1) for k in range(depth)]
-    heads_a = project_rows([near[0], near[2], far[0], far[2]])
-    pairs = from_x(heads_a[:, head:])
-    heads_b = project_rows([near[1], near[3], far[1], far[3]])
-    pairs_b = from_x(heads_b[:, head:])
-    pairs = [p for both in zip(pairs, pairs_b, strict=True) for p in both]
+    far = [swap_t(pieces[k], 1) for k in range(depth)]
+    far_y = [swap_t(pieces_y[k], 1) for k in range(depth)]
+    gains = global_gain.reshape(tensor_count, 1, share)
+
+    def project_planes(planes):
+        groups = [[group[k] for k in planes] for group in (pieces, pieces_y, far, far_y)]
+        return project_rows(bits, spots_whole, gains, *groups, flat(far_x), head)
+
+    query_a, pairs_a = project_planes((0, 2))
+    query_b, pairs_b = project_planes((1, 3))
+    pairs_a, pairs_b = from_x(pairs_a), from_x(pairs_b)
+    pairs = flat(zip(pairs_a, pairs_b, strict=True))
     turn = (0, 2, 1, 3)
     spot = 0 if across == 2 else x
     place_here = jnp.stack([keep[k] for k in turn]).reshape(all_rows, 1)
     codes_by_z = codes.reshape(depth, rows_here)
     every_code = from_x(jnp.stack([codes_by_z[k] for k in turn]).reshape(1, all_rows))
     own = jnp.full((1,), spot * all_rows, jnp.int32)
+    tile = 512 // across
     if across == 2:
-        pairs = pairs[2:]
-    global_mixed = global_attend(
-        own, place_here, jnp.concatenate(every_code, axis=1), heads_a, heads_b, pairs, 256 // across
-    ).reshape(depth, rows_here, head)
+        so_far = global_attend(own, place_here, every_code[0], query_a, query_b, pairs[:2], tile)
+        global_mixed = global_attend(
+            tuple(so_far), place_here, every_code[1], query_a, query_b, pairs[2:], tile
+        )
+    else:
+        codes_all = jnp.concatenate(every_code, axis=1)
+        _, total, mixed = global_attend(own, place_here, codes_all, query_a, query_b, pairs, tile)
+        global_mixed = (mixed / total).astype(query_a.dtype)
+    global_mixed = global_mixed.reshape(depth, 1, rows_here, head)
     global_mixed = [global_mixed[k] for k in turn]
-
-    got = jnp.stack([global_mixed[0]] + [swap_z(global_mixed[k], k) for k in range(1, depth)])
-    row = jnp.concatenate([pick(got, z ^ k) for k in range(depth)], axis=-1)
-    global_back = place(table_x, natural, global_mixed[0])
-    partial = jnp.einsum("rc,tdc->trd", row, global_back, preferred_element_type=jnp.float32)
-    plane = (z >> 1) ^ high
-    held = 2 * plane + (plane ^ high)
-    residual = pick(jnp.concatenate([near[0], near[2]]), held)
-    total = gather_sum(partial.reshape(2, 2, rows_here, share))
-    encoded = (residual.astype(jnp.float32) + total).astype(jnp.bfloat16)
+    got = [global_mixed[0]] + [swap_z(global_mixed[k], k) for k in range(1, depth)]
+    parts = project_back(bits, spots_whole, got, flat(table_x), tensor_count, share)
+    residual = jnp.where(
+        upper == 0,
+        jnp.where(high == 0, pieces[0], pieces[2]),
+        jnp.where(high == 0, pieces_y[2], pieces_y[0]),
+    )
+    encoded = (residual.astype(jnp.float32) + gather_sum(*parts)).astype(jnp.bfloat16)
     own_codes = codes[:windows_here]
     cells_each = window_cells // seq_count
     cells = cell_ids.reshape(seq_count, 1, cells_each, 1)

time: 252 us -> 267 us (1.060)
  Pallas kernels: 8.18 us -> 30.2 us
  waiting for transfers between devices: 99.3 us -> 107 us
  matrix products: 15.7 us -> 10.1 us
  other arithmetic: 13.9 us -> 10.2 us
  local copies, waits for them, and re-layouts: 23.9 us -> 20.3 us
    pallas_call x1 -> x6, Pallas kernels: 8.18 us -> 30.2 us  [the longest x2 11.6 us: project_rows(): pl.pallas_call(rows_kernel, in_specs=[pl.BlockSpec(memory_space=pltpu.SME...]
    ppermute x14 -> x18, waiting for transfers between devices: 19.7 us -> 32 us  [swap_t(): lax.ppermute(value, 'tensor', [(a, a ^ k) for a in range(tensor_count)])]
    ppermute x17, waiting for transfers between devices: 18.5 us -> 11.7 us  [from_x(): lax.ppermute(value, 'seq', [(a, a ^ 1) for a in range(seq_count)])]
    dot_general x6 -> x0, matrix products: 5.56 us -> none  [the longest x4 3.8 us: project_rows(): jnp.dot(normed(rows, global_gain), global_full, preferred_element_type=jn...]
    convert_element_type x1 -> x4, other arithmetic: 1.36 us -> 4.78 us  [the longest x2 2.3 us: gather_sum(): other = swap_t(part(1 - high).astype(jnp.bfloat16), 2)]
    dynamic_update_slice x28 -> x8, local copies, waits for them, and re-layouts: 6.83 us -> 4.14 us  [place(): lax.dynamic_update_slice(placed, piece[None, None], (at, spot, 0, 0))]
    unnamed x76 -> x101, local copies, waits for them, and re-layouts: 9.3 us -> 8.45 us
    ppermute x14 -> x18, starting transfers between devices: 9.9 us -> 9.87 us  [swap_t(): lax.ppermute(value, 'tensor', [(a, a ^ k) for a in range(tensor_count)])]
  transfers between devices with their start and end apart: 53 -> 57, of which waited for: 24 -> 20; matrix products, arithmetic and copies ran while one was open for 16% -> 11% of each run, Pallas kernels for 0% -> 8%
where the time goes in v1:
time: 267 us
  waiting for transfers between devices  107 us (40%)
  starting transfers between devices  67.5 us (25%)
  Pallas kernels  30.2 us (11%)
  local copies, waits for them, and re-layouts  20.3 us (8%)
  blocking collectives  20.1 us (8%)
  other arithmetic  10.2 us (4%)
  matrix products  10.1 us (4%)
    ppermute x22, waiting for transfers between devices, swap_z(): lax.ppermute(value, 'seq', [(a * across + b, (a ^ k) * across + b) for a...  63.6 us
    ppermute x22, starting transfers between devices, swap_z(): lax.ppermute(value, 'seq', [(a * across + b, (a ^ k) * across + b) for a...  39.7 us
    ppermute x18, waiting for transfers between devices, swap_t(): lax.ppermute(value, 'tensor', [(a, a ^ k) for a in range(tensor_count)])  32 us
    all_to_all x1, blocking collectives, shards(): lax.all_to_all(spread, 'seq', split_axis=0, concat_axis=0, tiled=True)  20.1 us
    ppermute x17, starting transfers between devices, from_x(): lax.ppermute(value, 'seq', [(a, a ^ 1) for a in range(seq_count)])  18 us
    ppermute x17, waiting for transfers between devices, from_x(): lax.ppermute(value, 'seq', [(a, a ^ 1) for a in range(seq_count)])  11.7 us
    pallas_call x2, Pallas kernels, project_rows(): pl.pallas_call(rows_kernel, in_specs=[pl.BlockSpec(memory_space=pltpu.SME...  11.6 us
    ppermute x18, starting transfers between devices, swap_t(): lax.ppermute(value, 'tensor', [(a, a ^ k) for a in range(tensor_count)])  9.87 us
  transfers between devices with their start and end apart: 57, of which 20 were waited for; matrix products, arithmetic and copies ran while one was open for 11% of the time, Pallas kernels for 8%

profile of v1, /device:TPU:0, one launch (start us, length us, event | category | flops | bytes accessed | tf_op | source)
XLA Modules:
  0.0 266.6 jit_solution(14047452087040767423)
XLA Ops:
  2.9 5.1 %collective-permute-start.2 = (bf16[80,640]{1,0:T(8,128)(2,1)S(1)}, bf16[80,640]{1,0:T(8,128)(2,1)S(1)}, u32[]{:S(2)}, u32[]{:S(2)}) collective-permute-start(bf16[80,640]{1,0:T(8,128)(2,1)S(1)} %pad_maximum_fusion.8), channel_id=1, source_target_pairs={{0,24},{4,28},{8,16},{12,20},{16,8},{20,12},{24,0},{28,4},{1,25},{... | collective-permute-start | bytes 307208 | tf_op jit(solution)/shard_map/ppermute | solution.py:275
  8.6 3.2 %collective-permute-done.2 = bf16[80,640]{1,0:T(8,128)(2,1)S(1)} collective-permute-done((bf16[80,640]{1,0:T(8,128)(2,1)S(1)}, bf16[80,640]{1,0:T(8,128)(2,1)S(1)}, u32[]{:S(2)}, u32[]{:S(2)}) %collective-permute-start.2) | collective-permute-done | bytes 102432 | tf_op jit(solution)/shard_map/ppermute | solution.py:275
  11.8 4.8 %collective-permute-done.1 = bf16[80,640]{1,0:T(8,128)(2,1)S(1)} collective-permute-done((bf16[80,640]{1,0:T(8,128)(2,1)S(1)}, bf16[80,640]{1,0:T(8,128)(2,1)S(1)}, u32[]{:S(2)}, u32[]{:S(2)}) %collective-permute-start.1) | collective-permute-done | bytes 102432 | tf_op jit(solution)/shard_map/ppermute | solution.py:275
  16.7 1.6 collective-permute-start.3
  18.3 2.0 constant_dynamic-slice_fusion
  20.3 1.6 collective-permute-start.5
  23.8 2.6 collective-permute-start.8
  29.1 4.4 %collective-permute-done.6 = bf16[320,384]{1,0:T(8,128)(2,1)} collective-permute-done((bf16[320,384]{1,0:T(8,128)(2,1)}, bf16[320,384]{1,0:T(8,128)(2,1)}, u32[]{:S(2)}, u32[]{:S(2)}) %collective-permute-start.6) | collective-permute-done | bytes 245792 | tf_op jit(solution)/shard_map/ppermute | solution.py:275
  34.1 9.5 %collective-permute-done.8 = bf16[320,384]{1,0:T(8,128)(2,1)} collective-permute-done((bf16[320,384]{1,0:T(8,128)(2,1)}, bf16[320,384]{1,0:T(8,128)(2,1)}, u32[]{:S(2)}, u32[]{:S(2)}) %collective-permute-start.8) | collective-permute-done | bytes 245792 | tf_op jit(solution)/shard_map/ppermute | solution.py:275
  48.8 6.1 %convert_reduce_fusion = (f32[1024]{0:T(1024)S(1)}, bf16[1024,2560]{1,0:T(8,128)(2,1)S(1)}) fusion(bf16[256,2560]{1,0:T(8,128)(2,1)S(1)} %copy-done.43, bf16[640,2560]{1,0:T(8,128)(2,1)S(1)} %copy-done.42, bf16[1024,256]{1,0:T(8,128)(2,1)S(1)} %fusion.26, bf16[768,640]{1,0:T(8,128)(2,1)S(1)} %bitcast.147, bf16[256,640]{1,0:T(8,128)(2,1)S(1)} %gather_fusion), kind=kOutput, calls=%fused_computation.3 | convolution fusion | flops 4720163840 | bytes 11669504 | tf_op jit(solution)/shard_map/dot_general | solution.py:351
  55.0 3.4 %collective-permute-start.16 = (bf16[320,512]{1,0:T(8,128)(2,1)S(1)}, bf16[320,512]{1,0:T(8,128)(2,1)S(1)}, u32[]{:S(2)}, u32[]{:S(2)}) collective-permute-start(bf16[320,512]{1,0:T(8,128)(2,1)S(1)} %copy-done.22), channel_id=1, source_target_pairs={{0,8},{4,12},{8,0},{12,4},{16,24},{20,28},{24,16},{28,20},{1,9},{5... | collective-permute-start | bytes 983048 | tf_op jit(solution)/shard_map/ppermute | solution.py:275
  58.3 1.5 fusion.3
  64.3 3.0 %fusion.19 = bf16[1024,384]{1,0:T(8,128)(2,1)S(1)} fusion(bf16[2560,384]{1,0:T(8,128)(2,1)S(1)} %bitcast.144, bf16[1024,2560]{1,0:T(8,128)(2,1)S(1)} %get-tuple-element.90, f32[2560]{0:T(1024)S(1)} %copy-done.44, f32[1024]{0:T(1024)S(1)} %add_rsqrt_fusion, f32[1024]{0:T(1024)S(1)} %broadcast_multiply_fusion), kind=kOutput, calls=%fused_computation.22 | convolution fusion | flops 2026766336 | bytes 8013824 | tf_op jit(solution)/shard_map/dot_general | solution.py:360
  72.0 1.8 collective-permute-start.14
  76.6 4.4 %collective-permute-done.13.refs_2_ = bf16[2,256,128]{2,1,0:T(8,128)(2,1)S(1)} collective-permute-done((bf16[2,256,128]{2,1,0:T(8,128)(2,1)S(1)}, bf16[2,256,128]{2,1,0:T(8,128)(2,1)S(1)}, u32[]{:S(2)}, u32[]{:S(2)}) %collective-permute-start.13) | collective-permute-done | bytes 131104 | tf_op jit(solution)/shard_map/ppermute | solution.py:275
  81.8 3.8 %project_back.2 = (f32[2,256,640]{2,1,0:T(8,128)}, bf16[2,256,640]{2,1,0:T(8,128)(2,1)}) custom-call(s32[7]{0:T(128)} %stack.125.bits_ref, s32[4]{0:T(128)} %pad_add_fusion.spots_ref, bf16[2,256,128]{2,1,0:T(8,128)(2,1)} %get-tuple-element.78.refs_0_, bf16[2,256,128]{2,1,0:T(8,128)(2,1)} %copy-done.33, bf16[2,256,128]{2,1,0:T(8,128)(2,1)} %copy-done.34, ...), custom_call_target="tpu_custom_call" | custom-call | tf_op jit(solution)/shard_map/project_back/pallas_call | solution.py:221
  85.6 2.3 collective-permute-done.18
  89.9 2.6 collective-permute-start.28
  92.9 1.9 collective-permute-start.32
  94.9 4.0 %collective-permute-done.19 = bf16[256,640]{1,0:T(8,128)(2,1)S(1)} collective-permute-done((bf16[256,640]{1,0:T(8,128)(2,1)S(1)}, bf16[256,640]{1,0:T(8,128)(2,1)S(1)}, u32[]{:S(2)}, u32[]{:S(2)}) %collective-permute-start.19) | collective-permute-done | bytes 327712 | tf_op jit(solution)/shard_map/ppermute | solution.py:282
  100.0 2.5 collective-permute-start.34
  104.5 8.2 %collective-permute-done.30.refs_12_ = bf16[320,384]{1,0:T(8,128)(2,1)S(1)} collective-permute-done((bf16[320,384]{1,0:T(8,128)(2,1)S(1)}, bf16[320,384]{1,0:T(8,128)(2,1)S(1)}, u32[]{:S(2)}, u32[]{:S(2)}) %collective-permute-start.30) | collective-permute-done | bytes 245792 | tf_op jit(solution)/shard_map/ppermute | solution.py:275
  114.2 3.4 %collective-permute-start.20 = (bf16[256,640]{1,0:T(8,128)(2,1)S(1)}, bf16[256,640]{1,0:T(8,128)(2,1)S(1)}, u32[]{:S(2)}, u32[]{:S(2)}) collective-permute-start(bf16[256,640]{1,0:T(8,128)(2,1)S(1)} %fusion.30.refs_0_), channel_id=1, source_target_pairs={{0,16},{4,20},{8,24},{12,28},{16,0},{20,4},{24,8},{28,12},{1,17},{... | collective-permute-start | bytes 983048 | tf_op jit(solution)/shard_map/ppermute | solution.py:275
  119.2 1.5 collective-permute-start.22
  121.0 1.9 collective-permute-start.35
  122.9 17.3 %collective-permute-done.20.refs_1_ = bf16[256,640]{1,0:T(8,128)(2,1)S(1)} collective-permute-done((bf16[256,640]{1,0:T(8,128)(2,1)S(1)}, bf16[256,640]{1,0:T(8,128)(2,1)S(1)}, u32[]{:S(2)}, u32[]{:S(2)}) %collective-permute-start.20) | collective-permute-done | bytes 327712 | tf_op jit(solution)/shard_map/ppermute | solution.py:275
  140.2 1.5 collective-permute-start.21
  145.5 3.9 %collective-permute-done.21.refs_3_ = bf16[256,640]{1,0:T(8,128)(2,1)S(1)} collective-permute-done((bf16[256,640]{1,0:T(8,128)(2,1)S(1)}, bf16[256,640]{1,0:T(8,128)(2,1)S(1)}, u32[]{:S(2)}, u32[]{:S(2)}) %collective-permute-start.21) | collective-permute-done | bytes 327712 | tf_op jit(solution)/shard_map/ppermute | solution.py:282
  150.1 6.4 %collective-permute-done.36.refs_2_ = bf16[256,640]{1,0:T(8,128)(2,1)} collective-permute-done((bf16[256,640]{1,0:T(8,128)(2,1)}, bf16[256,640]{1,0:T(8,128)(2,1)}, u32[]{:S(2)}, u32[]{:S(2)}) %collective-permute-start.36) | collective-permute-done | bytes 327712 | tf_op jit(solution)/shard_map/ppermute | solution.py:282
  156.5 4.9 %collective-permute-done.37.refs_3_ = bf16[256,640]{1,0:T(8,128)(2,1)} collective-permute-done((bf16[256,640]{1,0:T(8,128)(2,1)}, bf16[256,640]{1,0:T(8,128)(2,1)}, u32[]{:S(2)}, u32[]{:S(2)}) %collective-permute-start.37) | collective-permute-done | bytes 327712 | tf_op jit(solution)/shard_map/ppermute | solution.py:282
  161.5 2.5 collective-permute-start.51
  164.1 5.9 %project_rows.2 = (bf16[512,128]{1,0:T(8,128)(2,1)}, bf16[512,256]{1,0:T(8,128)(2,1)}) custom-call(s32[7]{0:T(128)} %stack.125.bits_ref, s32[6]{0:T(128)} %stack.135.spots_ref, f32[4,1,640]{2,1,0:T(1,128)} %reshape.206.gains_ref, bf16[256,640]{1,0:T(8,128)(2,1)} %copy-done.3, bf16[256,640]{1,0:T(8,128)(2,1)} %copy-done.6, bf16[256,640]{1,0:T(8,128)(2,1)} %copy-done.8, ...), custom_call_target="tpu_custom_call" | custom-call | tf_op jit(solution)/shard_map/project_rows/pallas_call | solution.py:183
  170.0 2.0 collective-permute-start.53
  173.4 5.7 %project_rows.3 = (bf16[512,128]{1,0:T(8,128)(2,1)}, bf16[512,256]{1,0:T(8,128)(2,1)}) custom-call(s32[7]{0:T(128)} %stack.125.bits_ref, s32[6]{0:T(128)} %stack.135.spots_ref, f32[4,1,640]{2,1,0:T(1,128)} %reshape.206.gains_ref, bf16[256,640]{1,0:T(8,128)(2,1)} %collective-permute-done.34.refs_0_, bf16[256,640]{1,0:T(8,128)(2,1)} %collective-permute-done.35.refs_1_, ...), custom_call_target="tpu_custom_call" | custom-call | tf_op jit(solution)/shard_map/project_rows/pallas_call | solution.py:183
  179.7 1.6 collective-permute-start.48
  181.2 6.2 %collective-permute-done.51.refs_8_ = bf16[320,512]{1,0:T(8,128)(2,1)} collective-permute-done((bf16[320,512]{1,0:T(8,128)(2,1)}, bf16[320,512]{1,0:T(8,128)(2,1)}, u32[]{:S(2)}, u32[]{:S(2)}) %collective-permute-start.51) | collective-permute-done | bytes 327712 | tf_op jit(solution)/shard_map/ppermute | solution.py:275
  189.6 11.4 %collective-permute-done.42.codes_ref = s32[1,1024]{1,0:T(1,128)S(1)} collective-permute-done((s32[1,1024]{1,0:T(1,128)S(1)}, s32[1,1024]{1,0:T(1,128)S(1)}, u32[]{:S(2)}, u32[]{:S(2)}) %collective-permute-start.42) | collective-permute-done | bytes 4128 | tf_op jit(solution)/shard_map/ppermute | solution.py:286
  204.1 5.3 %own_attend.1 = (f32[1024,1]{1,0:T(8,128)}, f32[1024,1]{1,0:T(8,128)}, f32[1024,128]{1,0:T(8,128)}) custom-call(s32[1]{0:T(128)} %constant.124.clone.1.own_ref, bf16[512,128]{1,0:T(8,128)(2,1)} %get-tuple-element.41.query_a, bf16[512,128]{1,0:T(8,128)(2,1)} %get-tuple-element.43.query_b, s32[1024,1]{1,0:T(8,128)} %bitcast.141, s32[1,1024]{1,0:T(1,128)} %bitcast.162, ...), custom_call_target="tpu_custom_call" | custom-call | tf_op jit(solution)/shard_map/own_attend/pallas_call | solution.py:119
  210.1 5.4 %rest_attend.1 = bf16[1024,128]{1,0:T(8,128)(2,1)} custom-call(bf16[512,128]{1,0:T(8,128)(2,1)} %get-tuple-element.41.query_a, bf16[512,128]{1,0:T(8,128)(2,1)} %get-tuple-element.43.query_b, s32[1024,1]{1,0:T(8,128)} %bitcast.142, s32[1,1024]{1,0:T(1,128)} %copy-done.41, f32[1024,1]{1,0:T(8,128)} %get-tuple-element.46.top_ref, ...), custom_call_target="tpu_custom_call" | custom-call | tf_op jit(solution)/shard_map/rest_attend/pallas_call | solution.py:127
  215.5 1.6 slice_bitcast_fusion.4
  217.1 2.5 collective-permute-start.46
  219.6 1.9 collective-permute-start.47
  222.8 2.9 %collective-permute-done.47.refs_3_ = bf16[1,256,128]{2,1,0:T(8,128)(2,1)S(1)} collective-permute-done((bf16[1,256,128]{2,1,0:T(8,128)(2,1)S(1)}, bf16[1,256,128]{2,1,0:T(8,128)(2,1)S(1)}, u32[]{:S(2)}, u32[]{:S(2)}) %collective-permute-start.47) | collective-permute-done | bytes 65568 | tf_op jit(solution)/shard_map/ppermute | solution.py:275
  226.3 4.2 %project_back.3 = (f32[2,256,640]{2,1,0:T(8,128)}, bf16[2,256,640]{2,1,0:T(8,128)(2,1)}) custom-call(s32[7]{0:T(128)} %stack.125.bits_ref, s32[6]{0:T(128)} %stack.135.spots_ref, bf16[1,256,128]{2,1,0:T(8,128)(2,1)} %get-tuple-element.70.refs_0_, bf16[1,256,128]{2,1,0:T(8,128)(2,1)} %copy-done.36, bf16[1,256,128]{2,1,0:T(8,128)(2,1)} %copy-done.37, ...), custom_call_target="tpu_custom_call" | custom-call | tf_op jit(solution)/shard_map/project_back/pallas_call | solution.py:221
  230.5 2.3 collective-permute-done.55
  233.9 1.6 collective-permute-start.56
  235.5 8.2 %collective-permute-done.56 = bf16[256,640]{1,0:T(8,128)(2,1)S(1)} collective-permute-done((bf16[256,640]{1,0:T(8,128)(2,1)S(1)}, bf16[256,640]{1,0:T(8,128)(2,1)S(1)}, u32[]{:S(2)}, u32[]{:S(2)}) %collective-permute-start.56) | collective-permute-done | bytes 327712 | tf_op jit(solution)/shard_map/ppermute | solution.py:282
  245.6 20.1 %all_to_all.5 = bf16[8,2,32,640]{3,2,1,0:T(8,128)(2,1)S(1)} all-to-all(bf16[8,2,32,640]{3,2,1,0:T(8,128)(2,1)S(1)} %copy.36), channel_id=1, replica_groups=mesh['seq'=8,'tensor'=4] {'seq'}, dimensions={0} | all-to-all | bytes 1310720 | tf_op jit(solution)/shard_map/all_to_all | solution.py:440
  (240 shorter events, 53.5 us)
Async XLA Ops:
  2.9 9.0 %collective-permute-start.2 = (bf16[80,640]{1,0:T(8,128)(2,1)S(1)}, bf16[80,640]{1,0:T(8,128)(2,1)S(1)}, u32[]{:S(2)}, u32[]{:S(2)}) collective-permute-start(bf16[80,640]{1,0:T(8,128)(2,1)S(1)} %pad_maximum_fusion.8), channel_id=1, source_target_pairs={{0,24},{4,28},{8,16},{12,20},{16,8},{20,12},{24,0},{28,4},{1,25},{... | collective-permute-start | bytes 307208 | tf_op jit(solution)/shard_map/ppermute | solution.py:275
  8.0 8.6 %collective-permute-start.1 = (bf16[80,640]{1,0:T(8,128)(2,1)S(1)}, bf16[80,640]{1,0:T(8,128)(2,1)S(1)}, u32[]{:S(2)}, u32[]{:S(2)}) collective-permute-start(bf16[80,640]{1,0:T(8,128)(2,1)S(1)} %pad_maximum_fusion.8), channel_id=1, source_target_pairs={{0,16},{4,20},{8,24},{12,28},{16,0},{20,4},{24,8},{28,12},{1,17},{... | collective-permute-start | bytes 307208 | tf_op jit(solution)/shard_map/ppermute | solution.py:275
  8.0 8.6 %collective-permute-start = (bf16[80,640]{1,0:T(8,128)(2,1)S(1)}, bf16[80,640]{1,0:T(8,128)(2,1)S(1)}, u32[]{:S(2)}, u32[]{:S(2)}) collective-permute-start(bf16[80,640]{1,0:T(8,128)(2,1)S(1)} %pad_maximum_fusion.8), channel_id=1, source_target_pairs={{0,8},{4,12},{8,0},{12,4},{16,24},{20,28},{24,16},{28,20},{1,9},{5... | collective-permute-start | bytes 307208 | tf_op jit(solution)/shard_map/ppermute | solution.py:275
  16.7 11.8 %collective-permute-start.3 = (bf16[3,80,640]{2,1,0:T(8,128)(2,1)S(1)}, bf16[3,80,640]{2,1,0:T(8,128)(2,1)S(1)}, u32[]{:S(2)}, u32[]{:S(2)}) collective-permute-start(bf16[3,80,640]{2,1,0:T(8,128)(2,1)S(1)} %get-tuple-element.28), channel_id=1, source_target_pairs={{0,2},{1,3},{2,0},{3,1},{4,6},{5,7},{6,4},{7,5},{8,10},{9,11},{10,... | collective-permute-start | bytes 921608 | tf_op jit(solution)/shard_map/ppermute | solution.py:282
  20.3 34.6 %collective-permute-start.5 = (bf16[320,384]{1,0:T(8,128)(2,1)S(1)}, bf16[320,384]{1,0:T(8,128)(2,1)}, u32[]{:S(2)}, u32[]{:S(2)}) collective-permute-start(bf16[320,384]{1,0:T(8,128)(2,1)S(1)} %bitcast.148), channel_id=1, source_target_pairs={{0,4},{4,0},{8,12},{12,8},{16,20},{20,16},{24,28},{28,24},{1,5},{5... | collective-permute-start | bytes 737288 | tf_op jit(solution)/shard_map/ppermute | solution.py:286
  22.6 10.9 %collective-permute-start.6 = (bf16[320,384]{1,0:T(8,128)(2,1)}, bf16[320,384]{1,0:T(8,128)(2,1)}, u32[]{:S(2)}, u32[]{:S(2)}) collective-permute-start(bf16[320,384]{1,0:T(8,128)(2,1)} %bitcast.137), channel_id=1, source_target_pairs={{0,8},{4,12},{8,0},{12,4},{16,24},{20,28},{24,16},{28,20},{1,9},{5... | collective-permute-start | bytes 737288 | tf_op jit(solution)/shard_map/ppermute | solution.py:275
  23.8 19.8 %collective-permute-start.8 = (bf16[320,384]{1,0:T(8,128)(2,1)}, bf16[320,384]{1,0:T(8,128)(2,1)}, u32[]{:S(2)}, u32[]{:S(2)}) collective-permute-start(bf16[320,384]{1,0:T(8,128)(2,1)} %bitcast.136), channel_id=1, source_target_pairs={{0,16},{4,20},{8,24},{12,28},{16,0},{20,4},{24,8},{28,12},{1,17},{... | collective-permute-start | bytes 737288 | tf_op jit(solution)/shard_map/ppermute | solution.py:275
  27.1 17.0 %collective-permute-start.10 = (bf16[320,384]{1,0:T(8,128)(2,1)}, bf16[320,384]{1,0:T(8,128)(2,1)}, u32[]{:S(2)}, u32[]{:S(2)}) collective-permute-start(bf16[320,384]{1,0:T(8,128)(2,1)} %bitcast.135), channel_id=1, source_target_pairs={{0,24},{4,28},{8,16},{12,20},{16,8},{20,12},{24,0},{28,4},{1,25},{... | collective-permute-start | bytes 737288 | tf_op jit(solution)/shard_map/ppermute | solution.py:275
  28.6 17.0 %collective-permute-start.4 = (bf16[2,3,80,640]{3,2,1,0:T(8,128)(2,1)S(1)}, bf16[2,3,80,640]{3,2,1,0:T(8,128)(2,1)S(1)}, u32[]{:S(2)}, u32[]{:S(2)}) collective-permute-start(bf16[2,3,80,640]{3,2,1,0:T(8,128)(2,1)S(1)} %pad_maximum_fusion.2), channel_id=1, source_target_pairs={{0,1},{1,0},{2,3},{3,2},{4,5},{5,4},{6,7},{7,6},{8,9},{9,8},{10,11... | collective-permute-start | bytes 1843208 | tf_op jit(solution)/shard_map/ppermute | solution.py:282
  33.6 41.5 %collective-permute-start.15 = (bf16[320,512]{1,0:T(8,128)(2,1)S(1)}, bf16[320,512]{1,0:T(8,128)(2,1)}, u32[]{:S(2)}, u32[]{:S(2)}) collective-permute-start(bf16[320,512]{1,0:T(8,128)(2,1)S(1)} %copy-done.22), channel_id=1, source_target_pairs={{0,4},{4,0},{8,12},{12,8},{16,20},{20,16},{24,28},{28,24},{1,5},{5... | collective-permute-start | bytes 983048 | tf_op jit(solution)/shard_map/ppermute | solution.py:286
  43.6 14.7 %collective-permute-start.7 = (bf16[320,384]{1,0:T(8,128)(2,1)}, bf16[320,384]{1,0:T(8,128)(2,1)S(1)}, u32[]{:S(2)}, u32[]{:S(2)}) collective-permute-start(bf16[320,384]{1,0:T(8,128)(2,1)} %collective-permute-done.6), channel_id=1, source_target_pairs={{0,4},{4,0},{8,12},{12,8},{16,20},{20,16},{24,28},{28,24},{1,5},{5... | collective-permute-start | bytes 737288 | tf_op jit(solution)/shard_map/ppermute | solution.py:286
  44.2 14.2 %collective-permute-start.9 = (bf16[320,384]{1,0:T(8,128)(2,1)}, bf16[320,384]{1,0:T(8,128)(2,1)S(1)}, u32[]{:S(2)}, u32[]{:S(2)}) collective-permute-start(bf16[320,384]{1,0:T(8,128)(2,1)} %collective-permute-done.8), channel_id=1, source_target_pairs={{0,4},{4,0},{8,12},{12,8},{16,20},{20,16},{24,28},{28,24},{1,5},{5... | collective-permute-start | bytes 737288 | tf_op jit(solution)/shard_map/ppermute | solution.py:286
  45.7 12.7 %collective-permute-start.11 = (bf16[320,384]{1,0:T(8,128)(2,1)}, bf16[320,384]{1,0:T(8,128)(2,1)S(1)}, u32[]{:S(2)}, u32[]{:S(2)}) collective-permute-start(bf16[320,384]{1,0:T(8,128)(2,1)} %collective-permute-done.10), channel_id=1, source_target_pairs={{0,4},{4,0},{8,12},{12,8},{16,20},{20,16},{24,28},{28,24},{1,5},{5... | collective-permute-start | bytes 737288 | tf_op jit(solution)/shard_map/ppermute | solution.py:286
  55.0 13.1 %collective-permute-start.16 = (bf16[320,512]{1,0:T(8,128)(2,1)S(1)}, bf16[320,512]{1,0:T(8,128)(2,1)S(1)}, u32[]{:S(2)}, u32[]{:S(2)}) collective-permute-start(bf16[320,512]{1,0:T(8,128)(2,1)S(1)} %copy-done.22), channel_id=1, source_target_pairs={{0,8},{4,12},{8,0},{12,4},{16,24},{20,28},{24,16},{28,20},{1,9},{5... | collective-permute-start | bytes 983048 | tf_op jit(solution)/shard_map/ppermute | solution.py:275
  68.1 12.9 %collective-permute-start.17 = (bf16[320,512]{1,0:T(8,128)(2,1)S(1)}, bf16[320,512]{1,0:T(8,128)(2,1)S(1)}, u32[]{:S(2)}, u32[]{:S(2)}) collective-permute-start(bf16[320,512]{1,0:T(8,128)(2,1)S(1)} %collective-permute-done.16.refs_6_), channel_id=1, source_target_pairs={{0,4},{4,0},{8,12},{12,8},{16,20},{20,16},{24,28},{28,24},{1,5},{5... | collective-permute-start | bytes 983048 | tf_op jit(solution)/shard_map/ppermute | solution.py:286
  70.8 10.1 %collective-permute-start.13 = (bf16[2,256,128]{2,1,0:T(8,128)(2,1)S(1)}, bf16[2,256,128]{2,1,0:T(8,128)(2,1)S(1)}, u32[]{:S(2)}, u32[]{:S(2)}) collective-permute-start(bf16[2,256,128]{2,1,0:T(8,128)(2,1)S(1)} %get-tuple-element.77), channel_id=1, source_target_pairs={{0,16},{4,20},{8,24},{12,28},{16,0},{20,4},{24,8},{28,12},{1,17},{... | collective-permute-start | bytes 393224 | tf_op jit(solution)/shard_map/ppermute | solution.py:275
  72.0 9.0 %collective-permute-start.14 = (bf16[2,256,128]{2,1,0:T(8,128)(2,1)S(1)}, bf16[2,256,128]{2,1,0:T(8,128)(2,1)S(1)}, u32[]{:S(2)}, u32[]{:S(2)}) collective-permute-start(bf16[2,256,128]{2,1,0:T(8,128)(2,1)S(1)} %get-tuple-element.75), channel_id=1, source_target_pairs={{0,24},{4,28},{8,16},{12,20},{16,8},{20,12},{24,0},{28,4},{1,25},{... | collective-permute-start | bytes 393224 | tf_op jit(solution)/shard_map/ppermute | solution.py:275
  89.0 9.8 %collective-permute-start.19 = (bf16[256,640]{1,0:T(8,128)(2,1)S(1)}, bf16[256,640]{1,0:T(8,128)(2,1)S(1)}, u32[]{:S(2)}, u32[]{:S(2)}) collective-permute-start(bf16[256,640]{1,0:T(8,128)(2,1)S(1)} %fusion.31), channel_id=1, source_target_pairs={{0,2},{1,3},{2,0},{3,1},{4,6},{5,7},{6,4},{7,5},{8,10},{9,11},{10,... | collective-permute-start | bytes 983048 | tf_op jit(solution)/shard_map/ppermute | solution.py:282
  89.9 14.2 %collective-permute-start.28 = (bf16[320,384]{1,0:T(8,128)(2,1)S(1)}, bf16[320,384]{1,0:T(8,128)(2,1)S(1)}, u32[]{:S(2)}, u32[]{:S(2)}) collective-permute-start(bf16[320,384]{1,0:T(8,128)(2,1)S(1)} %get-tuple-element.57), channel_id=1, source_target_pairs={{0,8},{4,12},{8,0},{12,4},{16,24},{20,28},{24,16},{28,20},{1,9},{5... | collective-permute-start | bytes 737288 | tf_op jit(solution)/shard_map/ppermute | solution.py:275
  92.4 20.3 %collective-permute-start.30 = (bf16[320,384]{1,0:T(8,128)(2,1)S(1)}, bf16[320,384]{1,0:T(8,128)(2,1)S(1)}, u32[]{:S(2)}, u32[]{:S(2)}) collective-permute-start(bf16[320,384]{1,0:T(8,128)(2,1)S(1)} %get-tuple-element.56), channel_id=1, source_target_pairs={{0,16},{4,20},{8,24},{12,28},{16,0},{20,4},{24,8},{28,12},{1,17},{... | collective-permute-start | bytes 737288 | tf_op jit(solution)/shard_map/ppermute | solution.py:275
  92.9 21.3 %collective-permute-start.32 = (bf16[320,384]{1,0:T(8,128)(2,1)S(1)}, bf16[320,384]{1,0:T(8,128)(2,1)S(1)}, u32[]{:S(2)}, u32[]{:S(2)}) collective-permute-start(bf16[320,384]{1,0:T(8,128)(2,1)S(1)} %get-tuple-element.55), channel_id=1, source_target_pairs={{0,24},{4,28},{8,16},{12,20},{16,8},{20,12},{24,0},{28,4},{1,25},{... | collective-permute-start | bytes 737288 | tf_op jit(solution)/shard_map/ppermute | solution.py:275
  100.0 17.7 %collective-permute-start.34 = (bf16[256,640]{1,0:T(8,128)(2,1)S(1)}, bf16[256,640]{1,0:T(8,128)(2,1)}, u32[]{:S(2)}, u32[]{:S(2)}) collective-permute-start(bf16[256,640]{1,0:T(8,128)(2,1)S(1)} %fusion.30.refs_0_), channel_id=1, source_target_pairs={{0,8},{4,12},{8,0},{12,4},{16,24},{20,28},{24,16},{28,20},{1,9},{5... | collective-permute-start | bytes 983048 | tf_op jit(solution)/shard_map/ppermute | solution.py:275
  102.5 16.6 %collective-permute-start.27 = (bf16[320,384]{1,0:T(8,128)(2,1)S(1)}, bf16[320,384]{1,0:T(8,128)(2,1)S(1)}, u32[]{:S(2)}, u32[]{:S(2)}) collective-permute-start(bf16[320,384]{1,0:T(8,128)(2,1)S(1)} %get-tuple-element.58.refs_8_), channel_id=1, source_target_pairs={{0,4},{4,0},{8,12},{12,8},{16,20},{20,16},{24,28},{28,24},{1,5},{5... | collective-permute-start | bytes 737288 | tf_op jit(solution)/shard_map/ppermute | solution.py:286
  104.0 16.7 %collective-permute-start.29 = (bf16[320,384]{1,0:T(8,128)(2,1)S(1)}, bf16[320,384]{1,0:T(8,128)(2,1)S(1)}, u32[]{:S(2)}, u32[]{:S(2)}) collective-permute-start(bf16[320,384]{1,0:T(8,128)(2,1)S(1)} %collective-permute-done.28.refs_10_), channel_id=1, source_target_pairs={{0,4},{4,0},{8,12},{12,8},{16,20},{20,16},{24,28},{28,24},{1,5},{5... | collective-permute-start | bytes 737288 | tf_op jit(solution)/shard_map/ppermute | solution.py:286
  114.2 26.0 %collective-permute-start.20 = (bf16[256,640]{1,0:T(8,128)(2,1)S(1)}, bf16[256,640]{1,0:T(8,128)(2,1)S(1)}, u32[]{:S(2)}, u32[]{:S(2)}) collective-permute-start(bf16[256,640]{1,0:T(8,128)(2,1)S(1)} %fusion.30.refs_0_), channel_id=1, source_target_pairs={{0,16},{4,20},{8,24},{12,28},{16,0},{20,4},{24,8},{28,12},{1,17},{... | collective-permute-start | bytes 983048 | tf_op jit(solution)/shard_map/ppermute | solution.py:275
  117.7 24.0 %collective-permute-start.33 = (bf16[320,384]{1,0:T(8,128)(2,1)S(1)}, bf16[320,384]{1,0:T(8,128)(2,1)S(1)}, u32[]{:S(2)}, u32[]{:S(2)}) collective-permute-start(bf16[320,384]{1,0:T(8,128)(2,1)S(1)} %collective-permute-done.32.refs_14_), channel_id=1, source_target_pairs={{0,4},{4,0},{8,12},{12,8},{16,20},{20,16},{24,28},{28,24},{1,5},{5... | collective-permute-start | bytes 737288 | tf_op jit(solution)/shard_map/ppermute | solution.py:286
  119.2 22.5 %collective-permute-start.22 = (bf16[256,640]{1,0:T(8,128)(2,1)S(1)}, bf16[256,640]{1,0:T(8,128)(2,1)S(1)}, u32[]{:S(2)}, u32[]{:S(2)}) collective-permute-start(bf16[256,640]{1,0:T(8,128)(2,1)S(1)} %fusion.30.refs_0_), channel_id=1, source_target_pairs={{0,2},{1,3},{2,0},{3,1},{4,6},{5,7},{6,4},{7,5},{8,10},{9,11},{10,... | collective-permute-start | bytes 983048 | tf_op jit(solution)/shard_map/ppermute | solution.py:282
  120.7 21.5 %collective-permute-start.23 = (bf16[256,640]{1,0:T(8,128)(2,1)S(1)}, bf16[256,640]{1,0:T(8,128)(2,1)S(1)}, u32[]{:S(2)}, u32[]{:S(2)}) collective-permute-start(bf16[256,640]{1,0:T(8,128)(2,1)S(1)} %fusion.30.refs_0_), channel_id=1, source_target_pairs={{0,1},{1,0},{2,3},{3,2},{4,5},{5,4},{6,7},{7,6},{8,9},{9,8},{10,11... | collective-permute-start | bytes 983048 | tf_op jit(solution)/shard_map/ppermute | solution.py:282
  121.0 21.8 %collective-permute-start.35 = (bf16[256,640]{1,0:T(8,128)(2,1)S(1)}, bf16[256,640]{1,0:T(8,128)(2,1)}, u32[]{:S(2)}, u32[]{:S(2)}) collective-permute-start(bf16[256,640]{1,0:T(8,128)(2,1)S(1)} %fusion.30.refs_0_), channel_id=1, source_target_pairs={{0,24},{4,28},{8,16},{12,20},{16,8},{20,12},{24,0},{28,4},{1,25},{... | collective-permute-start | bytes 983048 | tf_op jit(solution)/shard_map/ppermute | solution.py:275
  140.2 9.2 %collective-permute-start.21 = (bf16[256,640]{1,0:T(8,128)(2,1)S(1)}, bf16[256,640]{1,0:T(8,128)(2,1)S(1)}, u32[]{:S(2)}, u32[]{:S(2)}) collective-permute-start(bf16[256,640]{1,0:T(8,128)(2,1)S(1)} %collective-permute-done.20.refs_1_), channel_id=1, source_target_pairs={{0,2},{1,3},{2,0},{3,1},{4,6},{5,7},{6,4},{7,5},{8,10},{9,11},{10,... | collective-permute-start | bytes 983048 | tf_op jit(solution)/shard_map/ppermute | solution.py:282
  142.2 14.3 %collective-permute-start.36 = (bf16[256,640]{1,0:T(8,128)(2,1)}, bf16[256,640]{1,0:T(8,128)(2,1)}, u32[]{:S(2)}, u32[]{:S(2)}) collective-permute-start(bf16[256,640]{1,0:T(8,128)(2,1)} %collective-permute-done.34.refs_0_), channel_id=1, source_target_pairs={{0,2},{1,3},{2,0},{3,1},{4,6},{5,7},{6,4},{7,5},{8,10},{9,11},{10,... | collective-permute-start | bytes 983048 | tf_op jit(solution)/shard_map/ppermute | solution.py:282
  142.9 18.5 %collective-permute-start.37 = (bf16[256,640]{1,0:T(8,128)(2,1)}, bf16[256,640]{1,0:T(8,128)(2,1)}, u32[]{:S(2)}, u32[]{:S(2)}) collective-permute-start(bf16[256,640]{1,0:T(8,128)(2,1)} %collective-permute-done.35.refs_1_), channel_id=1, source_target_pairs={{0,2},{1,3},{2,0},{3,1},{4,6},{5,7},{6,4},{7,5},{8,10},{9,11},{10,... | collective-permute-start | bytes 983048 | tf_op jit(solution)/shard_map/ppermute | solution.py:282
  149.4 12.1 %collective-permute-start.38 = (bf16[256,640]{1,0:T(8,128)(2,1)}, bf16[256,640]{1,0:T(8,128)(2,1)}, u32[]{:S(2)}, u32[]{:S(2)}) collective-permute-start(bf16[256,640]{1,0:T(8,128)(2,1)} %collective-permute-done.34.refs_0_), channel_id=1, source_target_pairs={{0,1},{1,0},{2,3},{3,2},{4,5},{5,4},{6,7},{7,6},{8,9},{9,8},{10,11... | collective-permute-start | bytes 983048 | tf_op jit(solution)/shard_map/ppermute | solution.py:282
  149.4 12.1 %collective-permute-start.26 = (bf16[256,640]{1,0:T(8,128)(2,1)S(1)}, bf16[256,640]{1,0:T(8,128)(2,1)}, u32[]{:S(2)}, u32[]{:S(2)}) collective-permute-start(bf16[256,640]{1,0:T(8,128)(2,1)S(1)} %collective-permute-done.21.refs_3_), channel_id=1, source_target_pairs={{0,1},{1,0},{2,3},{3,2},{4,5},{5,4},{6,7},{7,6},{8,9},{9,8},{10,11... | collective-permute-start | bytes 983048 | tf_op jit(solution)/shard_map/ppermute | solution.py:282
  150.0 20.0 %collective-permute-start.39 = (bf16[256,640]{1,0:T(8,128)(2,1)}, bf16[256,640]{1,0:T(8,128)(2,1)}, u32[]{:S(2)}, u32[]{:S(2)}) collective-permute-start(bf16[256,640]{1,0:T(8,128)(2,1)} %collective-permute-done.35.refs_1_), channel_id=1, source_target_pairs={{0,1},{1,0},{2,3},{3,2},{4,5},{5,4},{6,7},{7,6},{8,9},{9,8},{10,11... | collective-permute-start | bytes 983048 | tf_op jit(solution)/shard_map/ppermute | solution.py:282
  156.5 15.4 %collective-permute-start.40 = (bf16[256,640]{1,0:T(8,128)(2,1)}, bf16[256,640]{1,0:T(8,128)(2,1)}, u32[]{:S(2)}, u32[]{:S(2)}) collective-permute-start(bf16[256,640]{1,0:T(8,128)(2,1)} %collective-permute-done.36.refs_2_), channel_id=1, source_target_pairs={{0,1},{1,0},{2,3},{3,2},{4,5},{5,4},{6,7},{7,6},{8,9},{9,8},{10,11... | collective-permute-start | bytes 983048 | tf_op jit(solution)/shard_map/ppermute | solution.py:282
  161.4 12.0 %collective-permute-start.41 = (bf16[256,640]{1,0:T(8,128)(2,1)}, bf16[256,640]{1,0:T(8,128)(2,1)}, u32[]{:S(2)}, u32[]{:S(2)}) collective-permute-start(bf16[256,640]{1,0:T(8,128)(2,1)} %collective-permute-done.37.refs_3_), channel_id=1, source_target_pairs={{0,1},{1,0},{2,3},{3,2},{4,5},{5,4},{6,7},{7,6},{8,9},{9,8},{10,11... | collective-permute-start | bytes 983048 | tf_op jit(solution)/shard_map/ppermute | solution.py:282
  161.5 18.2 %collective-permute-start.49 = (bf16[320,512]{1,0:T(8,128)(2,1)}, bf16[320,512]{1,0:T(8,128)(2,1)}, u32[]{:S(2)}, u32[]{:S(2)}) collective-permute-start(bf16[320,512]{1,0:T(8,128)(2,1)} %refs_4_.3), channel_id=1, source_target_pairs={{0,8},{4,12},{8,0},{12,4},{16,24},{20,28},{24,16},{28,20},{1,9},{5... | collective-permute-start | bytes 983048 | tf_op jit(solution)/shard_map/ppermute | solution.py:275
  161.5 26.0 %collective-permute-start.51 = (bf16[320,512]{1,0:T(8,128)(2,1)}, bf16[320,512]{1,0:T(8,128)(2,1)}, u32[]{:S(2)}, u32[]{:S(2)}) collective-permute-start(bf16[320,512]{1,0:T(8,128)(2,1)} %refs_4_.3), channel_id=1, source_target_pairs={{0,16},{4,20},{8,24},{12,28},{16,0},{20,4},{24,8},{28,12},{1,17},{... | collective-permute-start | bytes 983048 | tf_op jit(solution)/shard_map/ppermute | solution.py:275
  170.0 19.0 %collective-permute-start.53 = (bf16[320,512]{1,0:T(8,128)(2,1)}, bf16[320,512]{1,0:T(8,128)(2,1)S(1)}, u32[]{:S(2)}, u32[]{:S(2)}) collective-permute-start(bf16[320,512]{1,0:T(8,128)(2,1)} %refs_4_.3), channel_id=1, source_target_pairs={{0,24},{4,28},{8,16},{12,20},{16,8},{20,12},{24,0},{28,4},{1,25},{... | collective-permute-start | bytes 983048 | tf_op jit(solution)/shard_map/ppermute | solution.py:275
  171.9 29.7 %collective-permute-start.43 = (bf16[512,256]{1,0:T(8,128)(2,1)}, bf16[512,256]{1,0:T(8,128)(2,1)S(1)}, u32[]{:S(2)}, u32[]{:S(2)}) collective-permute-start(bf16[512,256]{1,0:T(8,128)(2,1)} %get-tuple-element.44.refs_0_), channel_id=1, source_target_pairs={{0,4},{4,0},{8,12},{12,8},{16,20},{20,16},{24,28},{28,24},{1,5},{5... | collective-permute-start | bytes 786440 | tf_op jit(solution)/shard_map/ppermute | solution.py:286
  179.1 30.3 %collective-permute-start.44 = (bf16[512,256]{1,0:T(8,128)(2,1)}, bf16[512,256]{1,0:T(8,128)(2,1)S(1)}, u32[]{:S(2)}, u32[]{:S(2)}) collective-permute-start(bf16[512,256]{1,0:T(8,128)(2,1)} %get-tuple-element.45.refs_1_), channel_id=1, source_target_pairs={{0,4},{4,0},{8,12},{12,8},{16,20},{20,16},{24,28},{28,24},{1,5},{5... | collective-permute-start | bytes 786440 | tf_op jit(solution)/shard_map/ppermute | solution.py:286
  179.7 37.4 %collective-permute-start.48 = (bf16[320,512]{1,0:T(8,128)(2,1)S(1)}, bf16[320,512]{1,0:T(8,128)(2,1)S(1)}, u32[]{:S(2)}, u32[]{:S(2)}) collective-permute-start(bf16[320,512]{1,0:T(8,128)(2,1)S(1)} %copy-done.25), channel_id=1, source_target_pairs={{0,4},{4,0},{8,12},{12,8},{16,20},{20,16},{24,28},{28,24},{1,5},{5... | collective-permute-start | bytes 983048 | tf_op jit(solution)/shard_map/ppermute | solution.py:286
  187.5 32.1 %collective-permute-start.50 = (bf16[320,512]{1,0:T(8,128)(2,1)}, bf16[320,512]{1,0:T(8,128)(2,1)S(1)}, u32[]{:S(2)}, u32[]{:S(2)}) collective-permute-start(bf16[320,512]{1,0:T(8,128)(2,1)} %collective-permute-done.49.refs_6_), channel_id=1, source_target_pairs={{0,4},{4,0},{8,12},{12,8},{16,20},{20,16},{24,28},{28,24},{1,5},{5... | collective-permute-start | bytes 983048 | tf_op jit(solution)/shard_map/ppermute | solution.py:286
  189.0 12.0 %collective-permute-start.42 = (s32[1,1024]{1,0:T(1,128)S(1)}, s32[1,1024]{1,0:T(1,128)S(1)}, u32[]{:S(2)}, u32[]{:S(2)}) collective-permute-start(s32[1,1024]{1,0:T(1,128)S(1)} %bitcast.161), channel_id=1, source_target_pairs={{0,4},{4,0},{8,12},{12,8},{16,20},{20,16},{24,28},{28,24},{1,5},{5... | collective-permute-start | bytes 12296 | tf_op jit(solution)/shard_map/ppermute | solution.py:286
  201.1 20.4 %collective-permute-start.52 = (bf16[320,512]{1,0:T(8,128)(2,1)}, bf16[320,512]{1,0:T(8,128)(2,1)S(1)}, u32[]{:S(2)}, u32[]{:S(2)}) collective-permute-start(bf16[320,512]{1,0:T(8,128)(2,1)} %collective-permute-done.51.refs_8_), channel_id=1, source_target_pairs={{0,4},{4,0},{8,12},{12,8},{16,20},{20,16},{24,28},{28,24},{1,5},{5... | collective-permute-start | bytes 983048 | tf_op jit(solution)/shard_map/ppermute | solution.py:286
  201.6 19.9 %collective-permute-start.54 = (bf16[320,512]{1,0:T(8,128)(2,1)S(1)}, bf16[320,512]{1,0:T(8,128)(2,1)S(1)}, u32[]{:S(2)}, u32[]{:S(2)}) collective-permute-start(bf16[320,512]{1,0:T(8,128)(2,1)S(1)} %collective-permute-done.53.refs_10_), channel_id=1, source_target_pairs={{0,4},{4,0},{8,12},{12,8},{16,20},{20,16},{24,28},{28,24},{1,5},{5... | collective-permute-start | bytes 983048 | tf_op jit(solution)/shard_map/ppermute | solution.py:286
  233.9 9.8 %collective-permute-start.56 = (bf16[256,640]{1,0:T(8,128)(2,1)S(1)}, bf16[256,640]{1,0:T(8,128)(2,1)S(1)}, u32[]{:S(2)}, u32[]{:S(2)}) collective-permute-start(bf16[256,640]{1,0:T(8,128)(2,1)S(1)} %fusion.32), channel_id=1, source_target_pairs={{0,2},{1,3},{2,0},{3,1},{4,6},{5,7},{6,4},{7,5},{8,10},{9,11},{10,... | collective-permute-start | bytes 983048 | tf_op jit(solution)/shard_map/ppermute | solution.py:282
  (54 other events, 823.4 us)

commit v2 on v1

--- a/solution.py
+++ b/solution.py
@@ -79,8 +79,8 @@
 
 
 def rest_kernel(query_a, query_b, place_ref, codes_ref, top_ref, total_ref, mixed_ref, *refs):
-    *pair_refs, out_ref = refs
-    _, width = out_ref.shape
+    *pair_refs, out0, out1, out2, out3 = refs
+    width = out0.shape[2]
     step, half = pl.program_id(0), pl.num_programs(0) // 2
     query = jnp.where(step < half, query_a[...], query_b[...])
     parts, top, factor = scores_over(query, place_ref[...], None, codes_ref, pair_refs, False)
@@ -89,7 +89,12 @@
     total, mixed = weigh(parts, top, factor, pair_refs, width)
     scale = jnp.exp2((before - top) * factor)
     total = total + total_ref[...] * scale
-    out_ref[...] = ((mixed + mixed_ref[...] * scale) / total).astype(out_ref.dtype)
+    result = ((mixed + mixed_ref[...] * scale) / total).astype(out0.dtype)
+    for i, ref in enumerate((out0, out1, out2, out3)):
+
+        @pl.when(step == i)
+        def _(ref=ref):
+            ref[0] = result
 
 
 def global_attend(own, place, codes, query_a, query_b, pairs, tile):
@@ -107,14 +112,7 @@
         pl.BlockSpec(codes.shape, lambda i: (0, 0)),
     ]
     pair_specs = [pl.BlockSpec(p.shape, lambda i: (0, 0)) for p in pairs]
-    kinds = [
-        jax.ShapeDtypeStruct((2 * rows, columns), kind)
-        for columns, kind in (
-            ((1, jnp.float32), (1, jnp.float32), (width, jnp.float32))
-            if first
-            else ((width, query_a.dtype),)
-        )
-    ]
+    kinds = [jax.ShapeDtypeStruct((2 * rows, c), jnp.float32) for c in (1, 1, width)]
     if first:
         return pl.pallas_call(
             own_kernel,
@@ -128,8 +126,8 @@
         rest_kernel,
         grid=(2 * half,),
         in_specs=[*specs, by_tile(1), by_tile(1), by_tile(width), *pair_specs],
-        out_specs=by_tile(width),
-        out_shape=kinds[0],
+        out_specs=[pl.BlockSpec((1, tile, width), lambda i: (0, 0, 0))] * 4,
+        out_shape=[jax.ShapeDtypeStruct((1, tile, width), query_a.dtype)] * 4,
         name="rest_attend",
     )(query_a, query_b, place, codes, *own, *pairs)
 
@@ -416,8 +414,7 @@
     else:
         codes_all = jnp.concatenate(every_code, axis=1)
         _, total, mixed = global_attend(own, place_here, codes_all, query_a, query_b, pairs, tile)
-        global_mixed = (mixed / total).astype(query_a.dtype)
-    global_mixed = global_mixed.reshape(depth, 1, rows_here, head)
+        global_mixed = (mixed / total).astype(query_a.dtype).reshape(depth, 1, rows_here, head)
     global_mixed = [global_mixed[k] for k in turn]
     got = [global_mixed[0]] + [swap_z(global_mixed[k], k) for k in range(1, depth)]
     parts = project_back(bits, spots_whole, got, flat(table_x), tensor_count, share)

time: 267 us -> 260 us (0.974)
  waiting for transfers between devices: 107 us -> 102 us
  starting transfers between devices: 67.5 us -> 63.6 us
    ppermute x18, waiting for transfers between devices: 32 us -> 19.4 us  [swap_t(): lax.ppermute(value, 'tensor', [(a, a ^ k) for a in range(tensor_count)])]
    ppermute x22, waiting for transfers between devices: 63.6 us -> 71.7 us  [swap_z(): lax.ppermute(value, 'seq', [(a * across + b, (a ^ k) * across + b) for a...]
    ppermute x22, starting transfers between devices: 39.7 us -> 35.7 us  [swap_z(): lax.ppermute(value, 'seq', [(a * across + b, (a ^ k) * across + b) for a...]
    unnamed x101 -> x99, local copies, waits for them, and re-layouts: 8.45 us -> 10 us
  transfers between devices with their start and end apart: 57 -> 57, of which waited for: 20 -> 21; matrix products, arithmetic and copies ran while one was open for 11% -> 10% of each run, Pallas kernels for 8% -> 9%
where the time goes in v2:
time: 260 us; the launch traced here: 259 us
  waiting for transfers between devices  102 us (39%)
  starting transfers between devices  63.6 us (24%)
  Pallas kernels  30.3 us (12%)
  blocking collectives  21.5 us (8%)
  local copies, waits for them, and re-layouts  20.1 us (8%)
  other arithmetic  11 us (4%)
  matrix products  10.1 us (4%)
    ppermute x22, waiting for transfers between devices, swap_z(): lax.ppermute(value, 'seq', [(a * across + b, (a ^ k) * across + b) for a...  71.7 us
    ppermute x22, starting transfers between devices, swap_z(): lax.ppermute(value, 'seq', [(a * across + b, (a ^ k) * across + b) for a...  35.7 us
    all_to_all x1, blocking collectives, shards(): lax.all_to_all(spread, 'seq', split_axis=0, concat_axis=0, tiled=True)  21.5 us
    ppermute x18, waiting for transfers between devices, swap_t(): lax.ppermute(value, 'tensor', [(a, a ^ k) for a in range(tensor_count)])  19.4 us
    ppermute x17, starting transfers between devices, from_x(): lax.ppermute(value, 'seq', [(a, a ^ 1) for a in range(seq_count)])  18.4 us
    pallas_call x2, Pallas kernels, project_rows(): pl.pallas_call(rows_kernel, in_specs=[pl.BlockSpec(memory_space=pltpu.SME...  11.6 us
    ppermute x17, waiting for transfers between devices, from_x(): lax.ppermute(value, 'seq', [(a, a ^ 1) for a in range(seq_count)])  11.1 us
    unnamed x99, local copies, waits for them, and re-layouts  10 us
  transfers between devices with their start and end apart: 57, of which 21 were waited for; matrix products, arithmetic and copies ran while one was open for 10% of the time, Pallas kernels for 9%

profile of v2, /device:TPU:0, one launch (start us, length us, event | category | flops | bytes accessed | tf_op | source)
XLA Modules:
  0.0 259.5 jit_solution(5785698388456142979)
XLA Ops:
  2.9 5.1 %collective-permute-start.2 = (bf16[80,640]{1,0:T(8,128)(2,1)S(1)}, bf16[80,640]{1,0:T(8,128)(2,1)S(1)}, u32[]{:S(2)}, u32[]{:S(2)}) collective-permute-start(bf16[80,640]{1,0:T(8,128)(2,1)S(1)} %pad_maximum_fusion.8), channel_id=1, source_target_pairs={{0,24},{4,28},{8,16},{12,20},{16,8},{20,12},{24,0},{28,4},{1,25},{... | collective-permute-start | bytes 307208 | tf_op jit(solution)/shard_map/ppermute | solution.py:273
  8.6 3.2 %collective-permute-done.2 = bf16[80,640]{1,0:T(8,128)(2,1)S(1)} collective-permute-done((bf16[80,640]{1,0:T(8,128)(2,1)S(1)}, bf16[80,640]{1,0:T(8,128)(2,1)S(1)}, u32[]{:S(2)}, u32[]{:S(2)}) %collective-permute-start.2) | collective-permute-done | bytes 102432 | tf_op jit(solution)/shard_map/ppermute | solution.py:273
  11.8 4.8 %collective-permute-done.1 = bf16[80,640]{1,0:T(8,128)(2,1)S(1)} collective-permute-done((bf16[80,640]{1,0:T(8,128)(2,1)S(1)}, bf16[80,640]{1,0:T(8,128)(2,1)S(1)}, u32[]{:S(2)}, u32[]{:S(2)}) %collective-permute-start.1) | collective-permute-done | bytes 102432 | tf_op jit(solution)/shard_map/ppermute | solution.py:273
  16.7 1.6 collective-permute-start.3
  18.3 2.0 constant_dynamic-slice_fusion
  20.3 1.6 collective-permute-start.5
  23.8 2.6 %collective-permute-start.8 = (bf16[320,384]{1,0:T(8,128)(2,1)}, bf16[320,384]{1,0:T(8,128)(2,1)}, u32[]{:S(2)}, u32[]{:S(2)}) collective-permute-start(bf16[320,384]{1,0:T(8,128)(2,1)} %bitcast.128), channel_id=1, source_target_pairs={{0,16},{4,20},{8,24},{12,28},{16,0},{20,4},{24,8},{28,12},{1,17},{... | collective-permute-start | bytes 737288 | tf_op jit(solution)/shard_map/ppermute | solution.py:273
  29.1 4.5 %collective-permute-done.6 = bf16[320,384]{1,0:T(8,128)(2,1)} collective-permute-done((bf16[320,384]{1,0:T(8,128)(2,1)}, bf16[320,384]{1,0:T(8,128)(2,1)}, u32[]{:S(2)}, u32[]{:S(2)}) %collective-permute-start.6) | collective-permute-done | bytes 245792 | tf_op jit(solution)/shard_map/ppermute | solution.py:273
  34.1 9.5 %collective-permute-done.8 = bf16[320,384]{1,0:T(8,128)(2,1)} collective-permute-done((bf16[320,384]{1,0:T(8,128)(2,1)}, bf16[320,384]{1,0:T(8,128)(2,1)}, u32[]{:S(2)}, u32[]{:S(2)}) %collective-permute-start.8) | collective-permute-done | bytes 245792 | tf_op jit(solution)/shard_map/ppermute | solution.py:273
  48.8 6.1 %convert_reduce_fusion = (f32[1024]{0:T(1024)S(1)}, bf16[1024,2560]{1,0:T(8,128)(2,1)S(1)}) fusion(bf16[256,2560]{1,0:T(8,128)(2,1)S(1)} %copy-done.42, bf16[640,2560]{1,0:T(8,128)(2,1)S(1)} %copy-done.41, bf16[1024,256]{1,0:T(8,128)(2,1)S(1)} %fusion.26, bf16[768,640]{1,0:T(8,128)(2,1)S(1)} %bitcast.139, bf16[256,640]{1,0:T(8,128)(2,1)S(1)} %gather_fusion), kind=kOutput, calls=%fused_computation.3 | convolution fusion | flops 4720163840 | bytes 11669504 | tf_op jit(solution)/shard_map/dot_general | solution.py:349
  55.0 3.4 %collective-permute-start.16 = (bf16[320,512]{1,0:T(8,128)(2,1)}, bf16[320,512]{1,0:T(8,128)(2,1)S(1)}, u32[]{:S(2)}, u32[]{:S(2)}) collective-permute-start(bf16[320,512]{1,0:T(8,128)(2,1)} %refs_4_.2), channel_id=1, source_target_pairs={{0,8},{4,12},{8,0},{12,4},{16,24},{20,28},{24,16},{28,20},{1,9},{5... | collective-permute-start | bytes 983048 | tf_op jit(solution)/shard_map/ppermute | solution.py:273
  63.3 3.0 %fusion.19 = bf16[1024,384]{1,0:T(8,128)(2,1)S(1)} fusion(bf16[2560,384]{1,0:T(8,128)(2,1)S(1)} %bitcast.136, bf16[1024,2560]{1,0:T(8,128)(2,1)S(1)} %get-tuple-element.94, f32[2560]{0:T(1024)S(1)} %copy-done.43, f32[1024]{0:T(1024)S(1)} %add_rsqrt_fusion, f32[1024]{0:T(1024)S(1)} %broadcast_multiply_fusion), kind=kOutput, calls=%fused_computation.22 | convolution fusion | flops 2026766336 | bytes 8013824 | tf_op jit(solution)/shard_map/dot_general | solution.py:358
  71.0 1.8 collective-permute-start.14
  75.6 4.4 %collective-permute-done.13.refs_2_ = bf16[2,256,128]{2,1,0:T(8,128)(2,1)S(1)} collective-permute-done((bf16[2,256,128]{2,1,0:T(8,128)(2,1)S(1)}, bf16[2,256,128]{2,1,0:T(8,128)(2,1)S(1)}, u32[]{:S(2)}, u32[]{:S(2)}) %collective-permute-start.13) | collective-permute-done | bytes 131104 | tf_op jit(solution)/shard_map/ppermute | solution.py:273
  80.9 3.8 %project_back.2 = (f32[2,256,640]{2,1,0:T(8,128)}, bf16[2,256,640]{2,1,0:T(8,128)(2,1)}) custom-call(s32[7]{0:T(128)} %stack.125.bits_ref, s32[4]{0:T(128)} %pad_add_fusion.spots_ref, bf16[2,256,128]{2,1,0:T(8,128)(2,1)} %get-tuple-element.82.refs_0_, bf16[2,256,128]{2,1,0:T(8,128)(2,1)} %copy-done.32, bf16[2,256,128]{2,1,0:T(8,128)(2,1)} %copy-done.33, ...), custom_call_target="tpu_custom_call" | custom-call | tf_op jit(solution)/shard_map/project_back/pallas_call | solution.py:219
  84.8 2.3 collective-permute-done.18
  87.1 1.8 fusion.31
  90.2 2.5 collective-permute-start.28
  94.2 2.4 collective-permute-start.30
  96.7 8.1 %collective-permute-done.28.refs_10_ = bf16[320,384]{1,0:T(8,128)(2,1)S(1)} collective-permute-done((bf16[320,384]{1,0:T(8,128)(2,1)S(1)}, bf16[320,384]{1,0:T(8,128)(2,1)S(1)}, u32[]{:S(2)}, u32[]{:S(2)}) %collective-permute-start.28) | collective-permute-done | bytes 245792 | tf_op jit(solution)/shard_map/ppermute | solution.py:273
  104.8 1.9 collective-permute-start.32
  111.1 2.5 collective-permute-start.34
  113.6 1.5 collective-permute-start.22
  115.1 4.0 %collective-permute-done.32.refs_14_ = bf16[320,384]{1,0:T(8,128)(2,1)S(1)} collective-permute-done((bf16[320,384]{1,0:T(8,128)(2,1)}, bf16[320,384]{1,0:T(8,128)(2,1)S(1)}, u32[]{:S(2)}, u32[]{:S(2)}) %collective-permute-start.32) | collective-permute-done | bytes 245792 | tf_op jit(solution)/shard_map/ppermute | solution.py:273
  121.2 13.6 %collective-permute-done.20.refs_1_ = bf16[256,640]{1,0:T(8,128)(2,1)S(1)} collective-permute-done((bf16[256,640]{1,0:T(8,128)(2,1)S(1)}, bf16[256,640]{1,0:T(8,128)(2,1)S(1)}, u32[]{:S(2)}, u32[]{:S(2)}) %collective-permute-start.20) | collective-permute-done | bytes 327712 | tf_op jit(solution)/shard_map/ppermute | solution.py:273
  134.7 1.6 collective-permute-start.21
  137.5 1.9 collective-permute-start.35
  141.2 4.2 %collective-permute-done.21.refs_3_ = bf16[256,640]{1,0:T(8,128)(2,1)S(1)} collective-permute-done((bf16[256,640]{1,0:T(8,128)(2,1)S(1)}, bf16[256,640]{1,0:T(8,128)(2,1)S(1)}, u32[]{:S(2)}, u32[]{:S(2)}) %collective-permute-start.21) | collective-permute-done | bytes 327712 | tf_op jit(solution)/shard_map/ppermute | solution.py:280
  146.1 3.4 %collective-permute-done.35.refs_1_ = bf16[256,640]{1,0:T(8,128)(2,1)} collective-permute-done((bf16[256,640]{1,0:T(8,128)(2,1)S(1)}, bf16[256,640]{1,0:T(8,128)(2,1)}, u32[]{:S(2)}, u32[]{:S(2)}) %collective-permute-start.35) | collective-permute-done | bytes 327712 | tf_op jit(solution)/shard_map/ppermute | solution.py:273
  149.9 2.6 collective-permute-done.36.refs_2_
  153.1 5.9 %project_rows.2 = (bf16[512,128]{1,0:T(8,128)(2,1)}, bf16[512,256]{1,0:T(8,128)(2,1)}) custom-call(s32[7]{0:T(128)} %stack.125.bits_ref, s32[6]{0:T(128)} %stack.135.spots_ref, f32[4,1,640]{2,1,0:T(1,128)} %reshape.197.gains_ref, bf16[256,640]{1,0:T(8,128)(2,1)} %copy-done.3, bf16[256,640]{1,0:T(8,128)(2,1)} %copy-done.6, bf16[256,640]{1,0:T(8,128)(2,1)} %copy-done.8, ...), custom_call_target="tpu_custom_call" | custom-call | tf_op jit(solution)/shard_map/project_rows/pallas_call | solution.py:181
  159.0 9.5 %collective-permute-done.51.refs_8_ = bf16[320,512]{1,0:T(8,128)(2,1)} collective-permute-done((bf16[320,512]{1,0:T(8,128)(2,1)}, bf16[320,512]{1,0:T(8,128)(2,1)}, u32[]{:S(2)}, u32[]{:S(2)}) %collective-permute-start.51) | collective-permute-done | bytes 327712 | tf_op jit(solution)/shard_map/ppermute | solution.py:273
  168.5 1.9 collective-permute-start.53
  170.3 1.7 collective-permute-start.43
  172.5 1.7 collective-permute-start.50
  175.0 5.7 %project_rows.3 = (bf16[512,128]{1,0:T(8,128)(2,1)}, bf16[512,256]{1,0:T(8,128)(2,1)}) custom-call(s32[7]{0:T(128)} %stack.125.bits_ref, s32[6]{0:T(128)} %stack.135.spots_ref, f32[4,1,640]{2,1,0:T(1,128)} %reshape.197.gains_ref, bf16[256,640]{1,0:T(8,128)(2,1)} %collective-permute-done.34.refs_0_, bf16[256,640]{1,0:T(8,128)(2,1)} %collective-permute-done.35.refs_1_, ...), custom_call_target="tpu_custom_call" | custom-call | tf_op jit(solution)/shard_map/project_rows/pallas_call | solution.py:181
  182.1 11.0 %collective-permute-done.42.codes_ref = s32[1,1024]{1,0:T(1,128)S(1)} collective-permute-done((s32[1,1024]{1,0:T(1,128)S(1)}, s32[1,1024]{1,0:T(1,128)S(1)}, u32[]{:S(2)}, u32[]{:S(2)}) %collective-permute-start.42) | collective-permute-done | bytes 4128 | tf_op jit(solution)/shard_map/ppermute | solution.py:284
  193.1 2.5 collective-permute-start.52
  196.7 5.2 %own_attend.1 = (f32[1024,1]{1,0:T(8,128)}, f32[1024,1]{1,0:T(8,128)}, f32[1024,128]{1,0:T(8,128)}) custom-call(s32[1]{0:T(128)} %constant.124.clone.1.own_ref, bf16[512,128]{1,0:T(8,128)(2,1)} %get-tuple-element.45.query_a, bf16[512,128]{1,0:T(8,128)(2,1)} %get-tuple-element.47.query_b, s32[1024,1]{1,0:T(8,128)} %bitcast.133, s32[1,1024]{1,0:T(1,128)} %bitcast.154, ...), custom_call_target="tpu_custom_call" | custom-call | tf_op jit(solution)/shard_map/own_attend/pallas_call | solution.py:117
  202.7 5.5 %rest_attend.1 = (bf16[1,256,128]{2,1,0:T(8,128)(2,1)}, bf16[1,256,128]{2,1,0:T(8,128)(2,1)}, bf16[1,256,128]{2,1,0:T(8,128)(2,1)}, bf16[1,256,128]{2,1,0:T(8,128)(2,1)}) custom-call(bf16[512,128]{1,0:T(8,128)(2,1)} %get-tuple-element.45.query_a, bf16[512,128]{1,0:T(8,128)(2,1)} %get-tuple-element.47.query_b, s32[1024,1]{1,0:T(8,128)} %bitcast.134, ...), custom_call_target="tpu_custom_call" | custom-call | tf_op jit(solution)/shard_map/rest_attend/pallas_call | solution.py:125
  208.2 2.0 collective-permute-start.45
  210.8 1.9 collective-permute-start.47
  213.7 2.4 collective-permute-done.46.refs_2_
  217.8 4.2 %project_back.3 = (f32[2,256,640]{2,1,0:T(8,128)}, bf16[2,256,640]{2,1,0:T(8,128)(2,1)}) custom-call(s32[7]{0:T(128)} %stack.125.bits_ref, s32[6]{0:T(128)} %stack.135.spots_ref, bf16[1,256,128]{2,1,0:T(8,128)(2,1)} %get-tuple-element.53.refs_0_, bf16[1,256,128]{2,1,0:T(8,128)(2,1)} %copy-done.35, bf16[1,256,128]{2,1,0:T(8,128)(2,1)} %copy-done.36, ...), custom_call_target="tpu_custom_call" | custom-call | tf_op jit(solution)/shard_map/project_back/pallas_call | solution.py:219
  222.0 2.3 collective-permute-done.55
  225.5 1.8 collective-permute-start.56
  227.3 8.1 %collective-permute-done.56 = bf16[256,640]{1,0:T(8,128)(2,1)S(1)} collective-permute-done((bf16[256,640]{1,0:T(8,128)(2,1)S(1)}, bf16[256,640]{1,0:T(8,128)(2,1)S(1)}, u32[]{:S(2)}, u32[]{:S(2)}) %collective-permute-start.56) | collective-permute-done | bytes 327712 | tf_op jit(solution)/shard_map/ppermute | solution.py:280
  237.2 21.5 %all_to_all.5 = bf16[8,2,32,640]{3,2,1,0:T(8,128)(2,1)S(1)} all-to-all(bf16[8,2,32,640]{3,2,1,0:T(8,128)(2,1)S(1)} %copy.36), channel_id=1, replica_groups=mesh['seq'=8,'tensor'=4] {'seq'}, dimensions={0} | all-to-all | bytes 1310720 | tf_op jit(solution)/shard_map/all_to_all | solution.py:437
  (237 shorter events, 52.4 us)
Async XLA Ops:
  2.9 9.0 %collective-permute-start.2 = (bf16[80,640]{1,0:T(8,128)(2,1)S(1)}, bf16[80,640]{1,0:T(8,128)(2,1)S(1)}, u32[]{:S(2)}, u32[]{:S(2)}) collective-permute-start(bf16[80,640]{1,0:T(8,128)(2,1)S(1)} %pad_maximum_fusion.8), channel_id=1, source_target_pairs={{0,24},{4,28},{8,16},{12,20},{16,8},{20,12},{24,0},{28,4},{1,25},{... | collective-permute-start | bytes 307208 | tf_op jit(solution)/shard_map/ppermute | solution.py:273
  8.0 8.6 %collective-permute-start.1 = (bf16[80,640]{1,0:T(8,128)(2,1)S(1)}, bf16[80,640]{1,0:T(8,128)(2,1)S(1)}, u32[]{:S(2)}, u32[]{:S(2)}) collective-permute-start(bf16[80,640]{1,0:T(8,128)(2,1)S(1)} %pad_maximum_fusion.8), channel_id=1, source_target_pairs={{0,16},{4,20},{8,24},{12,28},{16,0},{20,4},{24,8},{28,12},{1,17},{... | collective-permute-start | bytes 307208 | tf_op jit(solution)/shard_map/ppermute | solution.py:273
  8.0 8.6 %collective-permute-start = (bf16[80,640]{1,0:T(8,128)(2,1)S(1)}, bf16[80,640]{1,0:T(8,128)(2,1)S(1)}, u32[]{:S(2)}, u32[]{:S(2)}) collective-permute-start(bf16[80,640]{1,0:T(8,128)(2,1)S(1)} %pad_maximum_fusion.8), channel_id=1, source_target_pairs={{0,8},{4,12},{8,0},{12,4},{16,24},{20,28},{24,16},{28,20},{1,9},{5... | collective-permute-start | bytes 307208 | tf_op jit(solution)/shard_map/ppermute | solution.py:273
  16.7 11.8 %collective-permute-start.3 = (bf16[3,80,640]{2,1,0:T(8,128)(2,1)S(1)}, bf16[3,80,640]{2,1,0:T(8,128)(2,1)S(1)}, u32[]{:S(2)}, u32[]{:S(2)}) collective-permute-start(bf16[3,80,640]{2,1,0:T(8,128)(2,1)S(1)} %get-tuple-element.32), channel_id=1, source_target_pairs={{0,2},{1,3},{2,0},{3,1},{4,6},{5,7},{6,4},{7,5},{8,10},{9,11},{10,... | collective-permute-start | bytes 921608 | tf_op jit(solution)/shard_map/ppermute | solution.py:280
  20.3 34.6 %collective-permute-start.5 = (bf16[320,384]{1,0:T(8,128)(2,1)S(1)}, bf16[320,384]{1,0:T(8,128)(2,1)S(1)}, u32[]{:S(2)}, u32[]{:S(2)}) collective-permute-start(bf16[320,384]{1,0:T(8,128)(2,1)S(1)} %bitcast.140), channel_id=1, source_target_pairs={{0,4},{4,0},{8,12},{12,8},{16,20},{20,16},{24,28},{28,24},{1,5},{5... | collective-permute-start | bytes 737288 | tf_op jit(solution)/shard_map/ppermute | solution.py:284
  22.6 10.9 %collective-permute-start.6 = (bf16[320,384]{1,0:T(8,128)(2,1)}, bf16[320,384]{1,0:T(8,128)(2,1)}, u32[]{:S(2)}, u32[]{:S(2)}) collective-permute-start(bf16[320,384]{1,0:T(8,128)(2,1)} %bitcast.129), channel_id=1, source_target_pairs={{0,8},{4,12},{8,0},{12,4},{16,24},{20,28},{24,16},{28,20},{1,9},{5... | collective-permute-start | bytes 737288 | tf_op jit(solution)/shard_map/ppermute | solution.py:273
  23.8 19.8 %collective-permute-start.8 = (bf16[320,384]{1,0:T(8,128)(2,1)}, bf16[320,384]{1,0:T(8,128)(2,1)}, u32[]{:S(2)}, u32[]{:S(2)}) collective-permute-start(bf16[320,384]{1,0:T(8,128)(2,1)} %bitcast.128), channel_id=1, source_target_pairs={{0,16},{4,20},{8,24},{12,28},{16,0},{20,4},{24,8},{28,12},{1,17},{... | collective-permute-start | bytes 737288 | tf_op jit(solution)/shard_map/ppermute | solution.py:273
  27.1 17.1 %collective-permute-start.10 = (bf16[320,384]{1,0:T(8,128)(2,1)}, bf16[320,384]{1,0:T(8,128)(2,1)}, u32[]{:S(2)}, u32[]{:S(2)}) collective-permute-start(bf16[320,384]{1,0:T(8,128)(2,1)} %bitcast.127), channel_id=1, source_target_pairs={{0,24},{4,28},{8,16},{12,20},{16,8},{20,12},{24,0},{28,4},{1,25},{... | collective-permute-start | bytes 737288 | tf_op jit(solution)/shard_map/ppermute | solution.py:273
  28.6 17.1 %collective-permute-start.4 = (bf16[2,3,80,640]{3,2,1,0:T(8,128)(2,1)S(1)}, bf16[2,3,80,640]{3,2,1,0:T(8,128)(2,1)S(1)}, u32[]{:S(2)}, u32[]{:S(2)}) collective-permute-start(bf16[2,3,80,640]{3,2,1,0:T(8,128)(2,1)S(1)} %pad_maximum_fusion.2), channel_id=1, source_target_pairs={{0,1},{1,0},{2,3},{3,2},{4,5},{5,4},{6,7},{7,6},{8,9},{9,8},{10,11... | collective-permute-start | bytes 1843208 | tf_op jit(solution)/shard_map/ppermute | solution.py:280
  33.5 40.7 %collective-permute-start.15 = (bf16[320,512]{1,0:T(8,128)(2,1)}, bf16[320,512]{1,0:T(8,128)(2,1)}, u32[]{:S(2)}, u32[]{:S(2)}) collective-permute-start(bf16[320,512]{1,0:T(8,128)(2,1)} %refs_4_.2), channel_id=1, source_target_pairs={{0,4},{4,0},{8,12},{12,8},{16,20},{20,16},{24,28},{28,24},{1,5},{5... | collective-permute-start | bytes 983048 | tf_op jit(solution)/shard_map/ppermute | solution.py:284
  43.6 14.7 %collective-permute-start.7 = (bf16[320,384]{1,0:T(8,128)(2,1)}, bf16[320,384]{1,0:T(8,128)(2,1)S(1)}, u32[]{:S(2)}, u32[]{:S(2)}) collective-permute-start(bf16[320,384]{1,0:T(8,128)(2,1)} %collective-permute-done.6), channel_id=1, source_target_pairs={{0,4},{4,0},{8,12},{12,8},{16,20},{20,16},{24,28},{28,24},{1,5},{5... | collective-permute-start | bytes 737288 | tf_op jit(solution)/shard_map/ppermute | solution.py:284
  44.2 14.2 %collective-permute-start.9 = (bf16[320,384]{1,0:T(8,128)(2,1)}, bf16[320,384]{1,0:T(8,128)(2,1)S(1)}, u32[]{:S(2)}, u32[]{:S(2)}) collective-permute-start(bf16[320,384]{1,0:T(8,128)(2,1)} %collective-permute-done.8), channel_id=1, source_target_pairs={{0,4},{4,0},{8,12},{12,8},{16,20},{20,16},{24,28},{28,24},{1,5},{5... | collective-permute-start | bytes 737288 | tf_op jit(solution)/shard_map/ppermute | solution.py:284
  45.7 12.7 %collective-permute-start.11 = (bf16[320,384]{1,0:T(8,128)(2,1)}, bf16[320,384]{1,0:T(8,128)(2,1)S(1)}, u32[]{:S(2)}, u32[]{:S(2)}) collective-permute-start(bf16[320,384]{1,0:T(8,128)(2,1)} %collective-permute-done.10), channel_id=1, source_target_pairs={{0,4},{4,0},{8,12},{12,8},{16,20},{20,16},{24,28},{28,24},{1,5},{5... | collective-permute-start | bytes 737288 | tf_op jit(solution)/shard_map/ppermute | solution.py:284
  55.0 12.1 %collective-permute-start.16 = (bf16[320,512]{1,0:T(8,128)(2,1)}, bf16[320,512]{1,0:T(8,128)(2,1)S(1)}, u32[]{:S(2)}, u32[]{:S(2)}) collective-permute-start(bf16[320,512]{1,0:T(8,128)(2,1)} %refs_4_.2), channel_id=1, source_target_pairs={{0,8},{4,12},{8,0},{12,4},{16,24},{20,28},{24,16},{28,20},{1,9},{5... | collective-permute-start | bytes 983048 | tf_op jit(solution)/shard_map/ppermute | solution.py:273
  67.1 12.9 %collective-permute-start.17 = (bf16[320,512]{1,0:T(8,128)(2,1)S(1)}, bf16[320,512]{1,0:T(8,128)(2,1)S(1)}, u32[]{:S(2)}, u32[]{:S(2)}) collective-permute-start(bf16[320,512]{1,0:T(8,128)(2,1)S(1)} %collective-permute-done.16.refs_6_), channel_id=1, source_target_pairs={{0,4},{4,0},{8,12},{12,8},{16,20},{20,16},{24,28},{28,24},{1,5},{5... | collective-permute-start | bytes 983048 | tf_op jit(solution)/shard_map/ppermute | solution.py:284
  69.9 10.1 %collective-permute-start.13 = (bf16[2,256,128]{2,1,0:T(8,128)(2,1)S(1)}, bf16[2,256,128]{2,1,0:T(8,128)(2,1)S(1)}, u32[]{:S(2)}, u32[]{:S(2)}) collective-permute-start(bf16[2,256,128]{2,1,0:T(8,128)(2,1)S(1)} %get-tuple-element.81), channel_id=1, source_target_pairs={{0,16},{4,20},{8,24},{12,28},{16,0},{20,4},{24,8},{28,12},{1,17},{... | collective-permute-start | bytes 393224 | tf_op jit(solution)/shard_map/ppermute | solution.py:273
  71.0 9.0 %collective-permute-start.14 = (bf16[2,256,128]{2,1,0:T(8,128)(2,1)S(1)}, bf16[2,256,128]{2,1,0:T(8,128)(2,1)S(1)}, u32[]{:S(2)}, u32[]{:S(2)}) collective-permute-start(bf16[2,256,128]{2,1,0:T(8,128)(2,1)S(1)} %get-tuple-element.79), channel_id=1, source_target_pairs={{0,24},{4,28},{8,16},{12,20},{16,8},{20,12},{24,0},{28,4},{1,25},{... | collective-permute-start | bytes 393224 | tf_op jit(solution)/shard_map/ppermute | solution.py:273
  88.8 17.9 %collective-permute-start.19 = (bf16[256,640]{1,0:T(8,128)(2,1)}, bf16[256,640]{1,0:T(8,128)(2,1)S(1)}, u32[]{:S(2)}, u32[]{:S(2)}) collective-permute-start(bf16[256,640]{1,0:T(8,128)(2,1)} %fusion.31), channel_id=1, source_target_pairs={{0,2},{1,3},{2,0},{3,1},{4,6},{5,7},{6,4},{7,5},{8,10},{9,11},{10,... | collective-permute-start | bytes 983048 | tf_op jit(solution)/shard_map/ppermute | solution.py:280
  90.2 14.5 %collective-permute-start.28 = (bf16[320,384]{1,0:T(8,128)(2,1)S(1)}, bf16[320,384]{1,0:T(8,128)(2,1)S(1)}, u32[]{:S(2)}, u32[]{:S(2)}) collective-permute-start(bf16[320,384]{1,0:T(8,128)(2,1)S(1)} %get-tuple-element.65), channel_id=1, source_target_pairs={{0,8},{4,12},{8,0},{12,4},{16,24},{20,28},{24,16},{28,20},{1,9},{5... | collective-permute-start | bytes 737288 | tf_op jit(solution)/shard_map/ppermute | solution.py:273
  92.7 18.4 %collective-permute-start.49 = (bf16[320,512]{1,0:T(8,128)(2,1)}, bf16[320,512]{1,0:T(8,128)(2,1)}, u32[]{:S(2)}, u32[]{:S(2)}) collective-permute-start(bf16[320,512]{1,0:T(8,128)(2,1)} %refs_4_.3), channel_id=1, source_target_pairs={{0,8},{4,12},{8,0},{12,4},{16,24},{20,28},{24,16},{28,20},{1,9},{5... | collective-permute-start | bytes 983048 | tf_op jit(solution)/shard_map/ppermute | solution.py:273
  92.7 18.3 %collective-permute-start.27 = (bf16[320,384]{1,0:T(8,128)(2,1)S(1)}, bf16[320,384]{1,0:T(8,128)(2,1)S(1)}, u32[]{:S(2)}, u32[]{:S(2)}) collective-permute-start(bf16[320,384]{1,0:T(8,128)(2,1)S(1)} %get-tuple-element.66.refs_8_), channel_id=1, source_target_pairs={{0,4},{4,0},{8,12},{12,8},{16,20},{20,16},{24,28},{28,24},{1,5},{5... | collective-permute-start | bytes 737288 | tf_op jit(solution)/shard_map/ppermute | solution.py:284
  94.2 19.3 %collective-permute-start.30 = (bf16[320,384]{1,0:T(8,128)(2,1)}, bf16[320,384]{1,0:T(8,128)(2,1)S(1)}, u32[]{:S(2)}, u32[]{:S(2)}) collective-permute-start(bf16[320,384]{1,0:T(8,128)(2,1)} %get-tuple-element.64), channel_id=1, source_target_pairs={{0,16},{4,20},{8,24},{12,28},{16,0},{20,4},{24,8},{28,12},{1,17},{... | collective-permute-start | bytes 737288 | tf_op jit(solution)/shard_map/ppermute | solution.py:273
  104.8 14.3 %collective-permute-start.32 = (bf16[320,384]{1,0:T(8,128)(2,1)}, bf16[320,384]{1,0:T(8,128)(2,1)S(1)}, u32[]{:S(2)}, u32[]{:S(2)}) collective-permute-start(bf16[320,384]{1,0:T(8,128)(2,1)} %get-tuple-element.63), channel_id=1, source_target_pairs={{0,24},{4,28},{8,16},{12,20},{16,8},{20,12},{24,0},{28,4},{1,25},{... | collective-permute-start | bytes 737288 | tf_op jit(solution)/shard_map/ppermute | solution.py:273
  107.4 13.2 %collective-permute-start.29 = (bf16[320,384]{1,0:T(8,128)(2,1)S(1)}, bf16[320,384]{1,0:T(8,128)(2,1)S(1)}, u32[]{:S(2)}, u32[]{:S(2)}) collective-permute-start(bf16[320,384]{1,0:T(8,128)(2,1)S(1)} %collective-permute-done.28.refs_10_), channel_id=1, source_target_pairs={{0,4},{4,0},{8,12},{12,8},{16,20},{20,16},{24,28},{28,24},{1,5},{5... | collective-permute-start | bytes 737288 | tf_op jit(solution)/shard_map/ppermute | solution.py:284
  111.1 23.6 %collective-permute-start.20 = (bf16[256,640]{1,0:T(8,128)(2,1)S(1)}, bf16[256,640]{1,0:T(8,128)(2,1)S(1)}, u32[]{:S(2)}, u32[]{:S(2)}) collective-permute-start(bf16[256,640]{1,0:T(8,128)(2,1)S(1)} %fusion.30.refs_0_), channel_id=1, source_target_pairs={{0,16},{4,20},{8,24},{12,28},{16,0},{20,4},{24,8},{28,12},{1,17},{... | collective-permute-start | bytes 983048 | tf_op jit(solution)/shard_map/ppermute | solution.py:273
  111.1 23.6 %collective-permute-start.34 = (bf16[256,640]{1,0:T(8,128)(2,1)S(1)}, bf16[256,640]{1,0:T(8,128)(2,1)}, u32[]{:S(2)}, u32[]{:S(2)}) collective-permute-start(bf16[256,640]{1,0:T(8,128)(2,1)S(1)} %fusion.30.refs_0_), channel_id=1, source_target_pairs={{0,8},{4,12},{8,0},{12,4},{16,24},{20,28},{24,16},{28,20},{1,9},{5... | collective-permute-start | bytes 983048 | tf_op jit(solution)/shard_map/ppermute | solution.py:273
  113.6 22.9 %collective-permute-start.22 = (bf16[256,640]{1,0:T(8,128)(2,1)S(1)}, bf16[256,640]{1,0:T(8,128)(2,1)S(1)}, u32[]{:S(2)}, u32[]{:S(2)}) collective-permute-start(bf16[256,640]{1,0:T(8,128)(2,1)S(1)} %fusion.30.refs_0_), channel_id=1, source_target_pairs={{0,2},{1,3},{2,0},{3,1},{4,6},{5,7},{6,4},{7,5},{8,10},{9,11},{10,... | collective-permute-start | bytes 983048 | tf_op jit(solution)/shard_map/ppermute | solution.py:280
  119.1 17.2 %collective-permute-start.31 = (bf16[320,384]{1,0:T(8,128)(2,1)S(1)}, bf16[320,384]{1,0:T(8,128)(2,1)S(1)}, u32[]{:S(2)}, u32[]{:S(2)}) collective-permute-start(bf16[320,384]{1,0:T(8,128)(2,1)S(1)} %collective-permute-done.30.refs_12_), channel_id=1, source_target_pairs={{0,4},{4,0},{8,12},{12,8},{16,20},{20,16},{24,28},{28,24},{1,5},{5... | collective-permute-start | bytes 737288 | tf_op jit(solution)/shard_map/ppermute | solution.py:284
  120.6 16.2 %collective-permute-start.33 = (bf16[320,384]{1,0:T(8,128)(2,1)S(1)}, bf16[320,384]{1,0:T(8,128)(2,1)S(1)}, u32[]{:S(2)}, u32[]{:S(2)}) collective-permute-start(bf16[320,384]{1,0:T(8,128)(2,1)S(1)} %collective-permute-done.32.refs_14_), channel_id=1, source_target_pairs={{0,4},{4,0},{8,12},{12,8},{16,20},{20,16},{24,28},{28,24},{1,5},{5... | collective-permute-start | bytes 737288 | tf_op jit(solution)/shard_map/ppermute | solution.py:284
  134.7 10.6 %collective-permute-start.21 = (bf16[256,640]{1,0:T(8,128)(2,1)S(1)}, bf16[256,640]{1,0:T(8,128)(2,1)S(1)}, u32[]{:S(2)}, u32[]{:S(2)}) collective-permute-start(bf16[256,640]{1,0:T(8,128)(2,1)S(1)} %collective-permute-done.20.refs_1_), channel_id=1, source_target_pairs={{0,2},{1,3},{2,0},{3,1},{4,6},{5,7},{6,4},{7,5},{8,10},{9,11},{10,... | collective-permute-start | bytes 983048 | tf_op jit(solution)/shard_map/ppermute | solution.py:280
  136.3 9.1 %collective-permute-start.24 = (bf16[256,640]{1,0:T(8,128)(2,1)S(1)}, bf16[256,640]{1,0:T(8,128)(2,1)}, u32[]{:S(2)}, u32[]{:S(2)}) collective-permute-start(bf16[256,640]{1,0:T(8,128)(2,1)S(1)} %collective-permute-done.20.refs_1_), channel_id=1, source_target_pairs={{0,1},{1,0},{2,3},{3,2},{4,5},{5,4},{6,7},{7,6},{8,9},{9,8},{10,11... | collective-permute-start | bytes 983048 | tf_op jit(solution)/shard_map/ppermute | solution.py:280
  136.5 9.0 %collective-permute-start.25 = (bf16[256,640]{1,0:T(8,128)(2,1)S(1)}, bf16[256,640]{1,0:T(8,128)(2,1)}, u32[]{:S(2)}, u32[]{:S(2)}) collective-permute-start(bf16[256,640]{1,0:T(8,128)(2,1)S(1)} %collective-permute-done.22.refs_2_), channel_id=1, source_target_pairs={{0,1},{1,0},{2,3},{3,2},{4,5},{5,4},{6,7},{7,6},{8,9},{9,8},{10,11... | collective-permute-start | bytes 983048 | tf_op jit(solution)/shard_map/ppermute | solution.py:280
  137.5 12.0 %collective-permute-start.35 = (bf16[256,640]{1,0:T(8,128)(2,1)S(1)}, bf16[256,640]{1,0:T(8,128)(2,1)}, u32[]{:S(2)}, u32[]{:S(2)}) collective-permute-start(bf16[256,640]{1,0:T(8,128)(2,1)S(1)} %fusion.30.refs_0_), channel_id=1, source_target_pairs={{0,24},{4,28},{8,16},{12,20},{16,8},{20,12},{24,0},{28,4},{1,25},{... | collective-permute-start | bytes 983048 | tf_op jit(solution)/shard_map/ppermute | solution.py:273
  140.7 11.8 %collective-permute-start.36 = (bf16[256,640]{1,0:T(8,128)(2,1)}, bf16[256,640]{1,0:T(8,128)(2,1)}, u32[]{:S(2)}, u32[]{:S(2)}) collective-permute-start(bf16[256,640]{1,0:T(8,128)(2,1)} %collective-permute-done.34.refs_0_), channel_id=1, source_target_pairs={{0,2},{1,3},{2,0},{3,1},{4,6},{5,7},{6,4},{7,5},{8,10},{9,11},{10,... | collective-permute-start | bytes 983048 | tf_op jit(solution)/shard_map/ppermute | solution.py:280
  145.4 23.1 %collective-permute-start.51 = (bf16[320,512]{1,0:T(8,128)(2,1)}, bf16[320,512]{1,0:T(8,128)(2,1)}, u32[]{:S(2)}, u32[]{:S(2)}) collective-permute-start(bf16[320,512]{1,0:T(8,128)(2,1)} %refs_4_.3), channel_id=1, source_target_pairs={{0,16},{4,20},{8,24},{12,28},{16,0},{20,4},{24,8},{28,12},{1,17},{... | collective-permute-start | bytes 983048 | tf_op jit(solution)/shard_map/ppermute | solution.py:273
  145.5 24.8 %collective-permute-start.38 = (bf16[256,640]{1,0:T(8,128)(2,1)}, bf16[256,640]{1,0:T(8,128)(2,1)}, u32[]{:S(2)}, u32[]{:S(2)}) collective-permute-start(bf16[256,640]{1,0:T(8,128)(2,1)} %collective-permute-done.34.refs_0_), channel_id=1, source_target_pairs={{0,1},{1,0},{2,3},{3,2},{4,5},{5,4},{6,7},{7,6},{8,9},{9,8},{10,11... | collective-permute-start | bytes 983048 | tf_op jit(solution)/shard_map/ppermute | solution.py:280
  149.5 22.6 %collective-permute-start.37 = (bf16[256,640]{1,0:T(8,128)(2,1)}, bf16[256,640]{1,0:T(8,128)(2,1)}, u32[]{:S(2)}, u32[]{:S(2)}) collective-permute-start(bf16[256,640]{1,0:T(8,128)(2,1)} %collective-permute-done.35.refs_1_), channel_id=1, source_target_pairs={{0,2},{1,3},{2,0},{3,1},{4,6},{5,7},{6,4},{7,5},{8,10},{9,11},{10,... | collective-permute-start | bytes 983048 | tf_op jit(solution)/shard_map/ppermute | solution.py:280
  152.5 19.6 %collective-permute-start.39 = (bf16[256,640]{1,0:T(8,128)(2,1)}, bf16[256,640]{1,0:T(8,128)(2,1)}, u32[]{:S(2)}, u32[]{:S(2)}) collective-permute-start(bf16[256,640]{1,0:T(8,128)(2,1)} %collective-permute-done.35.refs_1_), channel_id=1, source_target_pairs={{0,1},{1,0},{2,3},{3,2},{4,5},{5,4},{6,7},{7,6},{8,9},{9,8},{10,11... | collective-permute-start | bytes 983048 | tf_op jit(solution)/shard_map/ppermute | solution.py:280
  152.5 20.0 %collective-permute-start.40 = (bf16[256,640]{1,0:T(8,128)(2,1)}, bf16[256,640]{1,0:T(8,128)(2,1)}, u32[]{:S(2)}, u32[]{:S(2)}) collective-permute-start(bf16[256,640]{1,0:T(8,128)(2,1)} %collective-permute-done.36.refs_2_), channel_id=1, source_target_pairs={{0,1},{1,0},{2,3},{3,2},{4,5},{5,4},{6,7},{7,6},{8,9},{9,8},{10,11... | collective-permute-start | bytes 983048 | tf_op jit(solution)/shard_map/ppermute | solution.py:280
  168.5 12.2 %collective-permute-start.53 = (bf16[320,512]{1,0:T(8,128)(2,1)}, bf16[320,512]{1,0:T(8,128)(2,1)S(1)}, u32[]{:S(2)}, u32[]{:S(2)}) collective-permute-start(bf16[320,512]{1,0:T(8,128)(2,1)} %refs_4_.3), channel_id=1, source_target_pairs={{0,24},{4,28},{8,16},{12,20},{16,8},{20,12},{24,0},{28,4},{1,25},{... | collective-permute-start | bytes 983048 | tf_op jit(solution)/shard_map/ppermute | solution.py:273
  170.3 25.3 %collective-permute-start.43 = (bf16[512,256]{1,0:T(8,128)(2,1)}, bf16[512,256]{1,0:T(8,128)(2,1)S(1)}, u32[]{:S(2)}, u32[]{:S(2)}) collective-permute-start(bf16[512,256]{1,0:T(8,128)(2,1)} %get-tuple-element.48.refs_0_), channel_id=1, source_target_pairs={{0,4},{4,0},{8,12},{12,8},{16,20},{20,16},{24,28},{28,24},{1,5},{5... | collective-permute-start | bytes 786440 | tf_op jit(solution)/shard_map/ppermute | solution.py:284
  172.1 38.1 %collective-permute-start.48 = (bf16[320,512]{1,0:T(8,128)(2,1)}, bf16[320,512]{1,0:T(8,128)(2,1)S(1)}, u32[]{:S(2)}, u32[]{:S(2)}) collective-permute-start(bf16[320,512]{1,0:T(8,128)(2,1)} %refs_4_.3), channel_id=1, source_target_pairs={{0,4},{4,0},{8,12},{12,8},{16,20},{20,16},{24,28},{28,24},{1,5},{5... | collective-permute-start | bytes 983048 | tf_op jit(solution)/shard_map/ppermute | solution.py:284
  172.5 38.3 %collective-permute-start.50 = (bf16[320,512]{1,0:T(8,128)(2,1)}, bf16[320,512]{1,0:T(8,128)(2,1)S(1)}, u32[]{:S(2)}, u32[]{:S(2)}) collective-permute-start(bf16[320,512]{1,0:T(8,128)(2,1)} %collective-permute-done.49.refs_6_), channel_id=1, source_target_pairs={{0,4},{4,0},{8,12},{12,8},{16,20},{20,16},{24,28},{28,24},{1,5},{5... | collective-permute-start | bytes 983048 | tf_op jit(solution)/shard_map/ppermute | solution.py:284
  174.3 18.9 %collective-permute-start.42 = (s32[1,1024]{1,0:T(1,128)S(1)}, s32[1,1024]{1,0:T(1,128)S(1)}, u32[]{:S(2)}, u32[]{:S(2)}) collective-permute-start(s32[1,1024]{1,0:T(1,128)S(1)} %bitcast.153), channel_id=1, source_target_pairs={{0,4},{4,0},{8,12},{12,8},{16,20},{20,16},{24,28},{28,24},{1,5},{5... | collective-permute-start | bytes 12296 | tf_op jit(solution)/shard_map/ppermute | solution.py:284
  180.7 21.3 %collective-permute-start.44 = (bf16[512,256]{1,0:T(8,128)(2,1)}, bf16[512,256]{1,0:T(8,128)(2,1)S(1)}, u32[]{:S(2)}, u32[]{:S(2)}) collective-permute-start(bf16[512,256]{1,0:T(8,128)(2,1)} %get-tuple-element.49.refs_1_), channel_id=1, source_target_pairs={{0,4},{4,0},{8,12},{12,8},{16,20},{20,16},{24,28},{28,24},{1,5},{5... | collective-permute-start | bytes 786440 | tf_op jit(solution)/shard_map/ppermute | solution.py:284
  193.1 19.6 %collective-permute-start.52 = (bf16[320,512]{1,0:T(8,128)(2,1)}, bf16[320,512]{1,0:T(8,128)(2,1)S(1)}, u32[]{:S(2)}, u32[]{:S(2)}) collective-permute-start(bf16[320,512]{1,0:T(8,128)(2,1)} %collective-permute-done.51.refs_8_), channel_id=1, source_target_pairs={{0,4},{4,0},{8,12},{12,8},{16,20},{20,16},{24,28},{28,24},{1,5},{5... | collective-permute-start | bytes 983048 | tf_op jit(solution)/shard_map/ppermute | solution.py:284
  195.6 17.1 %collective-permute-start.54 = (bf16[320,512]{1,0:T(8,128)(2,1)S(1)}, bf16[320,512]{1,0:T(8,128)(2,1)S(1)}, u32[]{:S(2)}, u32[]{:S(2)}) collective-permute-start(bf16[320,512]{1,0:T(8,128)(2,1)S(1)} %collective-permute-done.53.refs_10_), channel_id=1, source_target_pairs={{0,4},{4,0},{8,12},{12,8},{16,20},{20,16},{24,28},{28,24},{1,5},{5... | collective-permute-start | bytes 983048 | tf_op jit(solution)/shard_map/ppermute | solution.py:284
  225.5 9.8 %collective-permute-start.56 = (bf16[256,640]{1,0:T(8,128)(2,1)S(1)}, bf16[256,640]{1,0:T(8,128)(2,1)S(1)}, u32[]{:S(2)}, u32[]{:S(2)}) collective-permute-start(bf16[256,640]{1,0:T(8,128)(2,1)S(1)} %fusion.32), channel_id=1, source_target_pairs={{0,2},{1,3},{2,0},{3,1},{4,6},{5,7},{6,4},{7,5},{8,10},{9,11},{10,... | collective-permute-start | bytes 983048 | tf_op jit(solution)/shard_map/ppermute | solution.py:280
  (53 other events, 680.0 us)

commit v3 on v2

--- a/solution.py
+++ b/solution.py
@@ -296,8 +296,10 @@
         shape = (len(pieces), across) + pieces[0][0].shape
         placed = jnp.zeros(shape, pieces[0][0].dtype)
         for every, at in zip(pieces, order, strict=True):
-            for piece, spot in zip(every, spots_x, strict=True):
-                placed = lax.dynamic_update_slice(placed, piece[None, None], (at, spot, 0, 0))
+            if across == 2:
+                first = x == 0
+                every = [jnp.where(first, *every), jnp.where(first, every[1], every[0])]
+            placed = lax.dynamic_update_slice(placed, jnp.stack(every)[None], (at, 0, 0, 0))
         return placed.reshape(shape[0], shape[1] * shape[2], shape[3])
 
     def integers(values):

time: 260 us -> 261 us (level)
  other arithmetic: 11 us -> 14.3 us
  local copies, waits for them, and re-layouts: 20.1 us -> 17.1 us
    dynamic_update_slice x8 -> x0, local copies, waits for them, and re-layouts: 3.2 us -> none  [place(): lax.dynamic_update_slice(placed, piece[None, None], (at, spot, 0, 0))]
    another operation x0 -> x4, other arithmetic: none -> 3.06 us  [place(): jnp.stack(every)[None]]
where the time goes in v3:
time: 261 us; the launch traced here: 260 us
  waiting for transfers between devices  102 us (39%)
  starting transfers between devices  63.5 us (24%)
  Pallas kernels  30.3 us (12%)
  blocking collectives  21.5 us (8%)
  local copies, waits for them, and re-layouts  17.1 us (7%)
  other arithmetic  14.3 us (5%)
  matrix products  10.1 us (4%)
    ppermute x22, waiting for transfers between devices, swap_z(): lax.ppermute(value, 'seq', [(a * across + b, (a ^ k) * across + b) for a...  71.8 us
    ppermute x22, starting transfers between devices, swap_z(): lax.ppermute(value, 'seq', [(a * across + b, (a ^ k) * across + b) for a...  35.6 us
    all_to_all x1, blocking collectives, shards(): lax.all_to_all(spread, 'seq', split_axis=0, concat_axis=0, tiled=True)  21.5 us
    ppermute x18, waiting for transfers between devices, swap_t(): lax.ppermute(value, 'tensor', [(a, a ^ k) for a in range(tensor_count)])  19.5 us
    ppermute x17, starting transfers between devices, from_x(): lax.ppermute(value, 'seq', [(a, a ^ 1) for a in range(seq_count)])  18.4 us
    pallas_call x2, Pallas kernels, project_rows(): pl.pallas_call(rows_kernel, in_specs=[pl.BlockSpec(memory_space=pltpu.SME...  11.5 us
    ppermute x17, waiting for transfers between devices, from_x(): lax.ppermute(value, 'seq', [(a, a ^ 1) for a in range(seq_count)])  11.1 us
    unnamed x99, local copies, waits for them, and re-layouts  10.4 us
  transfers between devices with their start and end apart: 57, of which 21 were waited for; matrix products, arithmetic and copies ran while one was open for 10% of the time, Pallas kernels for 9%

profile of v3, /device:TPU:0, one launch (start us, length us, event | category | flops | bytes accessed | tf_op | source)
XLA Modules:
  0.0 259.9 jit_solution(4124373505237136503)
XLA Ops:
  2.9 5.1 %collective-permute-start.2 = (bf16[80,640]{1,0:T(8,128)(2,1)S(1)}, bf16[80,640]{1,0:T(8,128)(2,1)S(1)}, u32[]{:S(2)}, u32[]{:S(2)}) collective-permute-start(bf16[80,640]{1,0:T(8,128)(2,1)S(1)} %pad_maximum_fusion.8), channel_id=1, source_target_pairs={{0,24},{4,28},{8,16},{12,20},{16,8},{20,12},{24,0},{28,4},{1,25},{... | collective-permute-start | bytes 307208 | tf_op jit(solution)/shard_map/ppermute | solution.py:273
  8.6 3.2 %collective-permute-done.2 = bf16[80,640]{1,0:T(8,128)(2,1)S(1)} collective-permute-done((bf16[80,640]{1,0:T(8,128)(2,1)S(1)}, bf16[80,640]{1,0:T(8,128)(2,1)S(1)}, u32[]{:S(2)}, u32[]{:S(2)}) %collective-permute-start.2) | collective-permute-done | bytes 102432 | tf_op jit(solution)/shard_map/ppermute | solution.py:273
  11.8 4.8 %collective-permute-done.1 = bf16[80,640]{1,0:T(8,128)(2,1)S(1)} collective-permute-done((bf16[80,640]{1,0:T(8,128)(2,1)S(1)}, bf16[80,640]{1,0:T(8,128)(2,1)S(1)}, u32[]{:S(2)}, u32[]{:S(2)}) %collective-permute-start.1) | collective-permute-done | bytes 102432 | tf_op jit(solution)/shard_map/ppermute | solution.py:273
  16.7 1.6 collective-permute-start.3
  18.3 2.0 constant_dynamic-slice_fusion
  20.3 1.6 collective-permute-start.5
  23.8 2.6 %collective-permute-start.8 = (bf16[320,384]{1,0:T(8,128)(2,1)}, bf16[320,384]{1,0:T(8,128)(2,1)}, u32[]{:S(2)}, u32[]{:S(2)}) collective-permute-start(bf16[320,384]{1,0:T(8,128)(2,1)} %bitcast.144), channel_id=1, source_target_pairs={{0,16},{4,20},{8,24},{12,28},{16,0},{20,4},{24,8},{28,12},{1,17},{... | collective-permute-start | bytes 737288 | tf_op jit(solution)/shard_map/ppermute | solution.py:273
  29.1 4.4 %collective-permute-done.6 = bf16[320,384]{1,0:T(8,128)(2,1)} collective-permute-done((bf16[320,384]{1,0:T(8,128)(2,1)}, bf16[320,384]{1,0:T(8,128)(2,1)}, u32[]{:S(2)}, u32[]{:S(2)}) %collective-permute-start.6) | collective-permute-done | bytes 245792 | tf_op jit(solution)/shard_map/ppermute | solution.py:273
  34.1 9.6 %collective-permute-done.8 = bf16[320,384]{1,0:T(8,128)(2,1)} collective-permute-done((bf16[320,384]{1,0:T(8,128)(2,1)}, bf16[320,384]{1,0:T(8,128)(2,1)}, u32[]{:S(2)}, u32[]{:S(2)}) %collective-permute-start.8) | collective-permute-done | bytes 245792 | tf_op jit(solution)/shard_map/ppermute | solution.py:273
  48.8 6.1 %convert_reduce_fusion = (f32[1024]{0:T(1024)S(1)}, bf16[1024,2560]{1,0:T(8,128)(2,1)S(1)}) fusion(bf16[256,2560]{1,0:T(8,128)(2,1)S(1)} %copy-done.42, bf16[640,2560]{1,0:T(8,128)(2,1)S(1)} %copy-done.41, bf16[1024,256]{1,0:T(8,128)(2,1)S(1)} %fusion.26, bf16[768,640]{1,0:T(8,128)(2,1)S(1)} %bitcast.155, bf16[256,640]{1,0:T(8,128)(2,1)S(1)} %gather_fusion), kind=kOutput, calls=%fused_computation.3 | convolution fusion | flops 4720163840 | bytes 11669504 | tf_op jit(solution)/shard_map/dot_general | solution.py:351
  55.0 3.4 %collective-permute-start.16 = (bf16[320,512]{1,0:T(8,128)(2,1)}, bf16[320,512]{1,0:T(8,128)(2,1)S(1)}, u32[]{:S(2)}, u32[]{:S(2)}) collective-permute-start(bf16[320,512]{1,0:T(8,128)(2,1)} %refs_4_.2), channel_id=1, source_target_pairs={{0,8},{4,12},{8,0},{12,4},{16,24},{20,28},{24,16},{28,20},{1,9},{5... | collective-permute-start | bytes 983048 | tf_op jit(solution)/shard_map/ppermute | solution.py:273
  63.8 3.0 %fusion.19 = bf16[1024,384]{1,0:T(8,128)(2,1)S(1)} fusion(bf16[2560,384]{1,0:T(8,128)(2,1)S(1)} %bitcast.152, bf16[1024,2560]{1,0:T(8,128)(2,1)S(1)} %get-tuple-element.102, f32[2560]{0:T(1024)S(1)} %copy-done.43, f32[1024]{0:T(1024)S(1)} %add_rsqrt_fusion, f32[1024]{0:T(1024)S(1)} %broadcast_multiply_fusion), kind=kOutput, calls=%fused_computation.22 | convolution fusion | flops 2026766336 | bytes 8013824 | tf_op jit(solution)/shard_map/dot_general | solution.py:360
  71.6 1.8 collective-permute-start.14
  74.6 1.5 collective-permute-done.12.refs_1_
  76.2 4.3 %collective-permute-done.13.refs_2_ = bf16[2,256,128]{2,1,0:T(8,128)(2,1)S(1)} collective-permute-done((bf16[2,256,128]{2,1,0:T(8,128)(2,1)S(1)}, bf16[2,256,128]{2,1,0:T(8,128)(2,1)S(1)}, u32[]{:S(2)}, u32[]{:S(2)}) %collective-permute-start.13) | collective-permute-done | bytes 131104 | tf_op jit(solution)/shard_map/ppermute | solution.py:273
  81.4 3.8 %project_back.2 = (f32[2,256,640]{2,1,0:T(8,128)}, bf16[2,256,640]{2,1,0:T(8,128)(2,1)}) custom-call(s32[7]{0:T(128)} %stack.161.bits_ref, s32[4]{0:T(128)} %pad_add_fusion.spots_ref, bf16[2,256,128]{2,1,0:T(8,128)(2,1)} %get-tuple-element.90.refs_0_, bf16[2,256,128]{2,1,0:T(8,128)(2,1)} %copy-done.32, bf16[2,256,128]{2,1,0:T(8,128)(2,1)} %copy-done.33, ...), custom_call_target="tpu_custom_call" | custom-call | tf_op jit(solution)/shard_map/project_back/pallas_call | solution.py:219
  85.3 2.3 collective-permute-done.18
  87.6 1.8 fusion.35
  90.7 2.5 collective-permute-start.28
  94.7 2.4 collective-permute-start.30
  97.1 8.1 %collective-permute-done.28.refs_10_ = bf16[320,384]{1,0:T(8,128)(2,1)S(1)} collective-permute-done((bf16[320,384]{1,0:T(8,128)(2,1)S(1)}, bf16[320,384]{1,0:T(8,128)(2,1)S(1)}, u32[]{:S(2)}, u32[]{:S(2)}) %collective-permute-start.28) | collective-permute-done | bytes 245792 | tf_op jit(solution)/shard_map/ppermute | solution.py:273
  105.3 1.9 collective-permute-start.32
  111.6 2.5 collective-permute-start.34
  115.6 4.0 %collective-permute-done.32.refs_14_ = bf16[320,384]{1,0:T(8,128)(2,1)S(1)} collective-permute-done((bf16[320,384]{1,0:T(8,128)(2,1)}, bf16[320,384]{1,0:T(8,128)(2,1)S(1)}, u32[]{:S(2)}, u32[]{:S(2)}) %collective-permute-start.32) | collective-permute-done | bytes 245792 | tf_op jit(solution)/shard_map/ppermute | solution.py:273
  121.6 13.6 %collective-permute-done.20.refs_1_ = bf16[256,640]{1,0:T(8,128)(2,1)S(1)} collective-permute-done((bf16[256,640]{1,0:T(8,128)(2,1)S(1)}, bf16[256,640]{1,0:T(8,128)(2,1)S(1)}, u32[]{:S(2)}, u32[]{:S(2)}) %collective-permute-start.20) | collective-permute-done | bytes 327712 | tf_op jit(solution)/shard_map/ppermute | solution.py:273
  135.2 1.6 collective-permute-start.21
  138.0 1.9 collective-permute-start.35
  141.6 4.2 %collective-permute-done.21.refs_3_ = bf16[256,640]{1,0:T(8,128)(2,1)S(1)} collective-permute-done((bf16[256,640]{1,0:T(8,128)(2,1)S(1)}, bf16[256,640]{1,0:T(8,128)(2,1)S(1)}, u32[]{:S(2)}, u32[]{:S(2)}) %collective-permute-start.21) | collective-permute-done | bytes 327712 | tf_op jit(solution)/shard_map/ppermute | solution.py:280
  146.6 3.4 %collective-permute-done.35.refs_1_ = bf16[256,640]{1,0:T(8,128)(2,1)} collective-permute-done((bf16[256,640]{1,0:T(8,128)(2,1)S(1)}, bf16[256,640]{1,0:T(8,128)(2,1)}, u32[]{:S(2)}, u32[]{:S(2)}) %collective-permute-start.35) | collective-permute-done | bytes 327712 | tf_op jit(solution)/shard_map/ppermute | solution.py:273
  150.4 2.6 collective-permute-done.36.refs_2_
  153.6 5.9 %project_rows.2 = (bf16[512,128]{1,0:T(8,128)(2,1)}, bf16[512,256]{1,0:T(8,128)(2,1)}) custom-call(s32[7]{0:T(128)} %stack.161.bits_ref, s32[6]{0:T(128)} %stack.183.spots_ref, f32[4,1,640]{2,1,0:T(1,128)} %reshape.197.gains_ref, bf16[256,640]{1,0:T(8,128)(2,1)} %copy-done.3, bf16[256,640]{1,0:T(8,128)(2,1)} %copy-done.6, bf16[256,640]{1,0:T(8,128)(2,1)} %copy-done.8, ...), custom_call_target="tpu_custom_call" | custom-call | tf_op jit(solution)/shard_map/project_rows/pallas_call | solution.py:181
  159.5 9.5 %collective-permute-done.51.refs_8_ = bf16[320,512]{1,0:T(8,128)(2,1)} collective-permute-done((bf16[320,512]{1,0:T(8,128)(2,1)}, bf16[320,512]{1,0:T(8,128)(2,1)}, u32[]{:S(2)}, u32[]{:S(2)}) %collective-permute-start.51) | collective-permute-done | bytes 327712 | tf_op jit(solution)/shard_map/ppermute | solution.py:273
  169.0 1.9 collective-permute-start.53
  170.8 1.7 collective-permute-start.43
  172.9 1.7 collective-permute-start.50
  175.5 5.7 %project_rows.3 = (bf16[512,128]{1,0:T(8,128)(2,1)}, bf16[512,256]{1,0:T(8,128)(2,1)}) custom-call(s32[7]{0:T(128)} %stack.161.bits_ref, s32[6]{0:T(128)} %stack.183.spots_ref, f32[4,1,640]{2,1,0:T(1,128)} %reshape.197.gains_ref, bf16[256,640]{1,0:T(8,128)(2,1)} %collective-permute-done.34.refs_0_, bf16[256,640]{1,0:T(8,128)(2,1)} %collective-permute-done.35.refs_1_, ...), custom_call_target="tpu_custom_call" | custom-call | tf_op jit(solution)/shard_map/project_rows/pallas_call | solution.py:181
  182.6 11.0 %collective-permute-done.42.codes_ref = s32[1,1024]{1,0:T(1,128)S(1)} collective-permute-done((s32[1,1024]{1,0:T(1,128)S(1)}, s32[1,1024]{1,0:T(1,128)S(1)}, u32[]{:S(2)}, u32[]{:S(2)}) %collective-permute-start.42) | collective-permute-done | bytes 4128 | tf_op jit(solution)/shard_map/ppermute | solution.py:284
  193.6 2.5 collective-permute-start.52
  197.2 5.3 %own_attend.1 = (f32[1024,1]{1,0:T(8,128)}, f32[1024,1]{1,0:T(8,128)}, f32[1024,128]{1,0:T(8,128)}) custom-call(s32[1]{0:T(128)} %constant.123.clone.1.own_ref, bf16[512,128]{1,0:T(8,128)(2,1)} %get-tuple-element.45.query_a, bf16[512,128]{1,0:T(8,128)(2,1)} %get-tuple-element.47.query_b, s32[1024,1]{1,0:T(8,128)} %bitcast.149, s32[1,1024]{1,0:T(1,128)} %bitcast.170, ...), custom_call_target="tpu_custom_call" | custom-call | tf_op jit(solution)/shard_map/own_attend/pallas_call | solution.py:117
  203.2 5.5 %rest_attend.1 = (bf16[1,256,128]{2,1,0:T(8,128)(2,1)}, bf16[1,256,128]{2,1,0:T(8,128)(2,1)}, bf16[1,256,128]{2,1,0:T(8,128)(2,1)}, bf16[1,256,128]{2,1,0:T(8,128)(2,1)}) custom-call(bf16[512,128]{1,0:T(8,128)(2,1)} %get-tuple-element.45.query_a, bf16[512,128]{1,0:T(8,128)(2,1)} %get-tuple-element.47.query_b, s32[1024,1]{1,0:T(8,128)} %bitcast.150, ...), custom_call_target="tpu_custom_call" | custom-call | tf_op jit(solution)/shard_map/rest_attend/pallas_call | solution.py:125
  208.7 2.0 collective-permute-start.45
  211.3 1.9 collective-permute-start.47
  214.1 2.4 collective-permute-done.46.refs_2_
  218.3 4.2 %project_back.3 = (f32[2,256,640]{2,1,0:T(8,128)}, bf16[2,256,640]{2,1,0:T(8,128)(2,1)}) custom-call(s32[7]{0:T(128)} %stack.161.bits_ref, s32[6]{0:T(128)} %stack.183.spots_ref, bf16[1,256,128]{2,1,0:T(8,128)(2,1)} %get-tuple-element.53.refs_0_, bf16[1,256,128]{2,1,0:T(8,128)(2,1)} %copy-done.35, bf16[1,256,128]{2,1,0:T(8,128)(2,1)} %copy-done.36, ...), custom_call_target="tpu_custom_call" | custom-call | tf_op jit(solution)/shard_map/project_back/pallas_call | solution.py:219
  222.5 2.3 collective-permute-done.55
  226.0 1.8 collective-permute-start.56
  227.7 8.0 %collective-permute-done.56 = bf16[256,640]{1,0:T(8,128)(2,1)S(1)} collective-permute-done((bf16[256,640]{1,0:T(8,128)(2,1)S(1)}, bf16[256,640]{1,0:T(8,128)(2,1)S(1)}, u32[]{:S(2)}, u32[]{:S(2)}) %collective-permute-start.56) | collective-permute-done | bytes 327712 | tf_op jit(solution)/shard_map/ppermute | solution.py:280
  237.6 21.5 %all_to_all.5 = bf16[8,2,32,640]{3,2,1,0:T(8,128)(2,1)S(1)} all-to-all(bf16[8,2,32,640]{3,2,1,0:T(8,128)(2,1)S(1)} %copy.36), channel_id=1, replica_groups=mesh['seq'=8,'tensor'=4] {'seq'}, dimensions={0} | all-to-all | bytes 1310720 | tf_op jit(solution)/shard_map/all_to_all | solution.py:439
  (237 shorter events, 52.9 us)
Async XLA Ops:
  2.9 9.0 %collective-permute-start.2 = (bf16[80,640]{1,0:T(8,128)(2,1)S(1)}, bf16[80,640]{1,0:T(8,128)(2,1)S(1)}, u32[]{:S(2)}, u32[]{:S(2)}) collective-permute-start(bf16[80,640]{1,0:T(8,128)(2,1)S(1)} %pad_maximum_fusion.8), channel_id=1, source_target_pairs={{0,24},{4,28},{8,16},{12,20},{16,8},{20,12},{24,0},{28,4},{1,25},{... | collective-permute-start | bytes 307208 | tf_op jit(solution)/shard_map/ppermute | solution.py:273
  8.0 8.6 %collective-permute-start.1 = (bf16[80,640]{1,0:T(8,128)(2,1)S(1)}, bf16[80,640]{1,0:T(8,128)(2,1)S(1)}, u32[]{:S(2)}, u32[]{:S(2)}) collective-permute-start(bf16[80,640]{1,0:T(8,128)(2,1)S(1)} %pad_maximum_fusion.8), channel_id=1, source_target_pairs={{0,16},{4,20},{8,24},{12,28},{16,0},{20,4},{24,8},{28,12},{1,17},{... | collective-permute-start | bytes 307208 | tf_op jit(solution)/shard_map/ppermute | solution.py:273
  8.0 8.6 %collective-permute-start = (bf16[80,640]{1,0:T(8,128)(2,1)S(1)}, bf16[80,640]{1,0:T(8,128)(2,1)S(1)}, u32[]{:S(2)}, u32[]{:S(2)}) collective-permute-start(bf16[80,640]{1,0:T(8,128)(2,1)S(1)} %pad_maximum_fusion.8), channel_id=1, source_target_pairs={{0,8},{4,12},{8,0},{12,4},{16,24},{20,28},{24,16},{28,20},{1,9},{5... | collective-permute-start | bytes 307208 | tf_op jit(solution)/shard_map/ppermute | solution.py:273
  16.7 11.8 %collective-permute-start.3 = (bf16[3,80,640]{2,1,0:T(8,128)(2,1)S(1)}, bf16[3,80,640]{2,1,0:T(8,128)(2,1)S(1)}, u32[]{:S(2)}, u32[]{:S(2)}) collective-permute-start(bf16[3,80,640]{2,1,0:T(8,128)(2,1)S(1)} %get-tuple-element.32), channel_id=1, source_target_pairs={{0,2},{1,3},{2,0},{3,1},{4,6},{5,7},{6,4},{7,5},{8,10},{9,11},{10,... | collective-permute-start | bytes 921608 | tf_op jit(solution)/shard_map/ppermute | solution.py:280
  20.3 34.6 %collective-permute-start.5 = (bf16[320,384]{1,0:T(8,128)(2,1)S(1)}, bf16[320,384]{1,0:T(8,128)(2,1)S(1)}, u32[]{:S(2)}, u32[]{:S(2)}) collective-permute-start(bf16[320,384]{1,0:T(8,128)(2,1)S(1)} %bitcast.156), channel_id=1, source_target_pairs={{0,4},{4,0},{8,12},{12,8},{16,20},{20,16},{24,28},{28,24},{1,5},{5... | collective-permute-start | bytes 737288 | tf_op jit(solution)/shard_map/ppermute | solution.py:284
  22.6 10.9 %collective-permute-start.6 = (bf16[320,384]{1,0:T(8,128)(2,1)}, bf16[320,384]{1,0:T(8,128)(2,1)}, u32[]{:S(2)}, u32[]{:S(2)}) collective-permute-start(bf16[320,384]{1,0:T(8,128)(2,1)} %bitcast.145), channel_id=1, source_target_pairs={{0,8},{4,12},{8,0},{12,4},{16,24},{20,28},{24,16},{28,20},{1,9},{5... | collective-permute-start | bytes 737288 | tf_op jit(solution)/shard_map/ppermute | solution.py:273
  23.8 19.8 %collective-permute-start.8 = (bf16[320,384]{1,0:T(8,128)(2,1)}, bf16[320,384]{1,0:T(8,128)(2,1)}, u32[]{:S(2)}, u32[]{:S(2)}) collective-permute-start(bf16[320,384]{1,0:T(8,128)(2,1)} %bitcast.144), channel_id=1, source_target_pairs={{0,16},{4,20},{8,24},{12,28},{16,0},{20,4},{24,8},{28,12},{1,17},{... | collective-permute-start | bytes 737288 | tf_op jit(solution)/shard_map/ppermute | solution.py:273
  27.1 17.0 %collective-permute-start.10 = (bf16[320,384]{1,0:T(8,128)(2,1)}, bf16[320,384]{1,0:T(8,128)(2,1)}, u32[]{:S(2)}, u32[]{:S(2)}) collective-permute-start(bf16[320,384]{1,0:T(8,128)(2,1)} %bitcast.143), channel_id=1, source_target_pairs={{0,24},{4,28},{8,16},{12,20},{16,8},{20,12},{24,0},{28,4},{1,25},{... | collective-permute-start | bytes 737288 | tf_op jit(solution)/shard_map/ppermute | solution.py:273
  28.6 17.0 %collective-permute-start.4 = (bf16[2,3,80,640]{3,2,1,0:T(8,128)(2,1)S(1)}, bf16[2,3,80,640]{3,2,1,0:T(8,128)(2,1)S(1)}, u32[]{:S(2)}, u32[]{:S(2)}) collective-permute-start(bf16[2,3,80,640]{3,2,1,0:T(8,128)(2,1)S(1)} %pad_maximum_fusion.2), channel_id=1, source_target_pairs={{0,1},{1,0},{2,3},{3,2},{4,5},{5,4},{6,7},{7,6},{8,9},{9,8},{10,11... | collective-permute-start | bytes 1843208 | tf_op jit(solution)/shard_map/ppermute | solution.py:280
  33.5 41.1 %collective-permute-start.15 = (bf16[320,512]{1,0:T(8,128)(2,1)}, bf16[320,512]{1,0:T(8,128)(2,1)}, u32[]{:S(2)}, u32[]{:S(2)}) collective-permute-start(bf16[320,512]{1,0:T(8,128)(2,1)} %refs_4_.2), channel_id=1, source_target_pairs={{0,4},{4,0},{8,12},{12,8},{16,20},{20,16},{24,28},{28,24},{1,5},{5... | collective-permute-start | bytes 983048 | tf_op jit(solution)/shard_map/ppermute | solution.py:284
  43.6 14.7 %collective-permute-start.7 = (bf16[320,384]{1,0:T(8,128)(2,1)}, bf16[320,384]{1,0:T(8,128)(2,1)S(1)}, u32[]{:S(2)}, u32[]{:S(2)}) collective-permute-start(bf16[320,384]{1,0:T(8,128)(2,1)} %collective-permute-done.6), channel_id=1, source_target_pairs={{0,4},{4,0},{8,12},{12,8},{16,20},{20,16},{24,28},{28,24},{1,5},{5... | collective-permute-start | bytes 737288 | tf_op jit(solution)/shard_map/ppermute | solution.py:284
  44.2 14.2 %collective-permute-start.9 = (bf16[320,384]{1,0:T(8,128)(2,1)}, bf16[320,384]{1,0:T(8,128)(2,1)S(1)}, u32[]{:S(2)}, u32[]{:S(2)}) collective-permute-start(bf16[320,384]{1,0:T(8,128)(2,1)} %collective-permute-done.8), channel_id=1, source_target_pairs={{0,4},{4,0},{8,12},{12,8},{16,20},{20,16},{24,28},{28,24},{1,5},{5... | collective-permute-start | bytes 737288 | tf_op jit(solution)/shard_map/ppermute | solution.py:284
  45.7 12.7 %collective-permute-start.11 = (bf16[320,384]{1,0:T(8,128)(2,1)}, bf16[320,384]{1,0:T(8,128)(2,1)S(1)}, u32[]{:S(2)}, u32[]{:S(2)}) collective-permute-start(bf16[320,384]{1,0:T(8,128)(2,1)} %collective-permute-done.10), channel_id=1, source_target_pairs={{0,4},{4,0},{8,12},{12,8},{16,20},{20,16},{24,28},{28,24},{1,5},{5... | collective-permute-start | bytes 737288 | tf_op jit(solution)/shard_map/ppermute | solution.py:284
  55.0 12.7 %collective-permute-start.16 = (bf16[320,512]{1,0:T(8,128)(2,1)}, bf16[320,512]{1,0:T(8,128)(2,1)S(1)}, u32[]{:S(2)}, u32[]{:S(2)}) collective-permute-start(bf16[320,512]{1,0:T(8,128)(2,1)} %refs_4_.2), channel_id=1, source_target_pairs={{0,8},{4,12},{8,0},{12,4},{16,24},{20,28},{24,16},{28,20},{1,9},{5... | collective-permute-start | bytes 983048 | tf_op jit(solution)/shard_map/ppermute | solution.py:273
  67.7 12.9 %collective-permute-start.17 = (bf16[320,512]{1,0:T(8,128)(2,1)S(1)}, bf16[320,512]{1,0:T(8,128)(2,1)S(1)}, u32[]{:S(2)}, u32[]{:S(2)}) collective-permute-start(bf16[320,512]{1,0:T(8,128)(2,1)S(1)} %collective-permute-done.16.refs_6_), channel_id=1, source_target_pairs={{0,4},{4,0},{8,12},{12,8},{16,20},{20,16},{24,28},{28,24},{1,5},{5... | collective-permute-start | bytes 983048 | tf_op jit(solution)/shard_map/ppermute | solution.py:284
  70.4 10.1 %collective-permute-start.13 = (bf16[2,256,128]{2,1,0:T(8,128)(2,1)S(1)}, bf16[2,256,128]{2,1,0:T(8,128)(2,1)S(1)}, u32[]{:S(2)}, u32[]{:S(2)}) collective-permute-start(bf16[2,256,128]{2,1,0:T(8,128)(2,1)S(1)} %get-tuple-element.89), channel_id=1, source_target_pairs={{0,16},{4,20},{8,24},{12,28},{16,0},{20,4},{24,8},{28,12},{1,17},{... | collective-permute-start | bytes 393224 | tf_op jit(solution)/shard_map/ppermute | solution.py:273
  71.6 9.0 %collective-permute-start.14 = (bf16[2,256,128]{2,1,0:T(8,128)(2,1)S(1)}, bf16[2,256,128]{2,1,0:T(8,128)(2,1)S(1)}, u32[]{:S(2)}, u32[]{:S(2)}) collective-permute-start(bf16[2,256,128]{2,1,0:T(8,128)(2,1)S(1)} %get-tuple-element.87), channel_id=1, source_target_pairs={{0,24},{4,28},{8,16},{12,20},{16,8},{20,12},{24,0},{28,4},{1,25},{... | collective-permute-start | bytes 393224 | tf_op jit(solution)/shard_map/ppermute | solution.py:273
  89.3 17.8 %collective-permute-start.19 = (bf16[256,640]{1,0:T(8,128)(2,1)}, bf16[256,640]{1,0:T(8,128)(2,1)S(1)}, u32[]{:S(2)}, u32[]{:S(2)}) collective-permute-start(bf16[256,640]{1,0:T(8,128)(2,1)} %fusion.35), channel_id=1, source_target_pairs={{0,2},{1,3},{2,0},{3,1},{4,6},{5,7},{6,4},{7,5},{8,10},{9,11},{10,... | collective-permute-start | bytes 983048 | tf_op jit(solution)/shard_map/ppermute | solution.py:280
  90.7 14.5 %collective-permute-start.28 = (bf16[320,384]{1,0:T(8,128)(2,1)S(1)}, bf16[320,384]{1,0:T(8,128)(2,1)S(1)}, u32[]{:S(2)}, u32[]{:S(2)}) collective-permute-start(bf16[320,384]{1,0:T(8,128)(2,1)S(1)} %get-tuple-element.65), channel_id=1, source_target_pairs={{0,8},{4,12},{8,0},{12,4},{16,24},{20,28},{24,16},{28,20},{1,9},{5... | collective-permute-start | bytes 737288 | tf_op jit(solution)/shard_map/ppermute | solution.py:273
  93.2 18.4 %collective-permute-start.49 = (bf16[320,512]{1,0:T(8,128)(2,1)}, bf16[320,512]{1,0:T(8,128)(2,1)}, u32[]{:S(2)}, u32[]{:S(2)}) collective-permute-start(bf16[320,512]{1,0:T(8,128)(2,1)} %refs_4_.3), channel_id=1, source_target_pairs={{0,8},{4,12},{8,0},{12,4},{16,24},{20,28},{24,16},{28,20},{1,9},{5... | collective-permute-start | bytes 983048 | tf_op jit(solution)/shard_map/ppermute | solution.py:273
  93.2 18.3 %collective-permute-start.27 = (bf16[320,384]{1,0:T(8,128)(2,1)S(1)}, bf16[320,384]{1,0:T(8,128)(2,1)S(1)}, u32[]{:S(2)}, u32[]{:S(2)}) collective-permute-start(bf16[320,384]{1,0:T(8,128)(2,1)S(1)} %get-tuple-element.66.refs_8_), channel_id=1, source_target_pairs={{0,4},{4,0},{8,12},{12,8},{16,20},{20,16},{24,28},{28,24},{1,5},{5... | collective-permute-start | bytes 737288 | tf_op jit(solution)/shard_map/ppermute | solution.py:284
  94.7 19.3 %collective-permute-start.30 = (bf16[320,384]{1,0:T(8,128)(2,1)}, bf16[320,384]{1,0:T(8,128)(2,1)S(1)}, u32[]{:S(2)}, u32[]{:S(2)}) collective-permute-start(bf16[320,384]{1,0:T(8,128)(2,1)} %get-tuple-element.64), channel_id=1, source_target_pairs={{0,16},{4,20},{8,24},{12,28},{16,0},{20,4},{24,8},{28,12},{1,17},{... | collective-permute-start | bytes 737288 | tf_op jit(solution)/shard_map/ppermute | solution.py:273
  105.3 14.3 %collective-permute-start.32 = (bf16[320,384]{1,0:T(8,128)(2,1)}, bf16[320,384]{1,0:T(8,128)(2,1)S(1)}, u32[]{:S(2)}, u32[]{:S(2)}) collective-permute-start(bf16[320,384]{1,0:T(8,128)(2,1)} %get-tuple-element.63), channel_id=1, source_target_pairs={{0,24},{4,28},{8,16},{12,20},{16,8},{20,12},{24,0},{28,4},{1,25},{... | collective-permute-start | bytes 737288 | tf_op jit(solution)/shard_map/ppermute | solution.py:273
  107.9 13.2 %collective-permute-start.29 = (bf16[320,384]{1,0:T(8,128)(2,1)S(1)}, bf16[320,384]{1,0:T(8,128)(2,1)S(1)}, u32[]{:S(2)}, u32[]{:S(2)}) collective-permute-start(bf16[320,384]{1,0:T(8,128)(2,1)S(1)} %collective-permute-done.28.refs_10_), channel_id=1, source_target_pairs={{0,4},{4,0},{8,12},{12,8},{16,20},{20,16},{24,28},{28,24},{1,5},{5... | collective-permute-start | bytes 737288 | tf_op jit(solution)/shard_map/ppermute | solution.py:284
  111.6 23.6 %collective-permute-start.20 = (bf16[256,640]{1,0:T(8,128)(2,1)S(1)}, bf16[256,640]{1,0:T(8,128)(2,1)S(1)}, u32[]{:S(2)}, u32[]{:S(2)}) collective-permute-start(bf16[256,640]{1,0:T(8,128)(2,1)S(1)} %fusion.30.refs_0_), channel_id=1, source_target_pairs={{0,16},{4,20},{8,24},{12,28},{16,0},{20,4},{24,8},{28,12},{1,17},{... | collective-permute-start | bytes 983048 | tf_op jit(solution)/shard_map/ppermute | solution.py:273
  111.6 23.6 %collective-permute-start.34 = (bf16[256,640]{1,0:T(8,128)(2,1)S(1)}, bf16[256,640]{1,0:T(8,128)(2,1)}, u32[]{:S(2)}, u32[]{:S(2)}) collective-permute-start(bf16[256,640]{1,0:T(8,128)(2,1)S(1)} %fusion.30.refs_0_), channel_id=1, source_target_pairs={{0,8},{4,12},{8,0},{12,4},{16,24},{20,28},{24,16},{28,20},{1,9},{5... | collective-permute-start | bytes 983048 | tf_op jit(solution)/shard_map/ppermute | solution.py:273
  114.0 22.9 %collective-permute-start.22 = (bf16[256,640]{1,0:T(8,128)(2,1)S(1)}, bf16[256,640]{1,0:T(8,128)(2,1)S(1)}, u32[]{:S(2)}, u32[]{:S(2)}) collective-permute-start(bf16[256,640]{1,0:T(8,128)(2,1)S(1)} %fusion.30.refs_0_), channel_id=1, source_target_pairs={{0,2},{1,3},{2,0},{3,1},{4,6},{5,7},{6,4},{7,5},{8,10},{9,11},{10,... | collective-permute-start | bytes 983048 | tf_op jit(solution)/shard_map/ppermute | solution.py:280
  119.6 17.2 %collective-permute-start.31 = (bf16[320,384]{1,0:T(8,128)(2,1)S(1)}, bf16[320,384]{1,0:T(8,128)(2,1)S(1)}, u32[]{:S(2)}, u32[]{:S(2)}) collective-permute-start(bf16[320,384]{1,0:T(8,128)(2,1)S(1)} %collective-permute-done.30.refs_12_), channel_id=1, source_target_pairs={{0,4},{4,0},{8,12},{12,8},{16,20},{20,16},{24,28},{28,24},{1,5},{5... | collective-permute-start | bytes 737288 | tf_op jit(solution)/shard_map/ppermute | solution.py:284
  121.1 16.2 %collective-permute-start.33 = (bf16[320,384]{1,0:T(8,128)(2,1)S(1)}, bf16[320,384]{1,0:T(8,128)(2,1)S(1)}, u32[]{:S(2)}, u32[]{:S(2)}) collective-permute-start(bf16[320,384]{1,0:T(8,128)(2,1)S(1)} %collective-permute-done.32.refs_14_), channel_id=1, source_target_pairs={{0,4},{4,0},{8,12},{12,8},{16,20},{20,16},{24,28},{28,24},{1,5},{5... | collective-permute-start | bytes 737288 | tf_op jit(solution)/shard_map/ppermute | solution.py:284
  135.2 10.6 %collective-permute-start.21 = (bf16[256,640]{1,0:T(8,128)(2,1)S(1)}, bf16[256,640]{1,0:T(8,128)(2,1)S(1)}, u32[]{:S(2)}, u32[]{:S(2)}) collective-permute-start(bf16[256,640]{1,0:T(8,128)(2,1)S(1)} %collective-permute-done.20.refs_1_), channel_id=1, source_target_pairs={{0,2},{1,3},{2,0},{3,1},{4,6},{5,7},{6,4},{7,5},{8,10},{9,11},{10,... | collective-permute-start | bytes 983048 | tf_op jit(solution)/shard_map/ppermute | solution.py:280
  136.8 9.1 %collective-permute-start.24 = (bf16[256,640]{1,0:T(8,128)(2,1)S(1)}, bf16[256,640]{1,0:T(8,128)(2,1)}, u32[]{:S(2)}, u32[]{:S(2)}) collective-permute-start(bf16[256,640]{1,0:T(8,128)(2,1)S(1)} %collective-permute-done.20.refs_1_), channel_id=1, source_target_pairs={{0,1},{1,0},{2,3},{3,2},{4,5},{5,4},{6,7},{7,6},{8,9},{9,8},{10,11... | collective-permute-start | bytes 983048 | tf_op jit(solution)/shard_map/ppermute | solution.py:280
  137.0 9.0 %collective-permute-start.25 = (bf16[256,640]{1,0:T(8,128)(2,1)S(1)}, bf16[256,640]{1,0:T(8,128)(2,1)}, u32[]{:S(2)}, u32[]{:S(2)}) collective-permute-start(bf16[256,640]{1,0:T(8,128)(2,1)S(1)} %collective-permute-done.22.refs_2_), channel_id=1, source_target_pairs={{0,1},{1,0},{2,3},{3,2},{4,5},{5,4},{6,7},{7,6},{8,9},{9,8},{10,11... | collective-permute-start | bytes 983048 | tf_op jit(solution)/shard_map/ppermute | solution.py:280
  138.0 12.0 %collective-permute-start.35 = (bf16[256,640]{1,0:T(8,128)(2,1)S(1)}, bf16[256,640]{1,0:T(8,128)(2,1)}, u32[]{:S(2)}, u32[]{:S(2)}) collective-permute-start(bf16[256,640]{1,0:T(8,128)(2,1)S(1)} %fusion.30.refs_0_), channel_id=1, source_target_pairs={{0,24},{4,28},{8,16},{12,20},{16,8},{20,12},{24,0},{28,4},{1,25},{... | collective-permute-start | bytes 983048 | tf_op jit(solution)/shard_map/ppermute | solution.py:273
  141.1 11.8 %collective-permute-start.36 = (bf16[256,640]{1,0:T(8,128)(2,1)}, bf16[256,640]{1,0:T(8,128)(2,1)}, u32[]{:S(2)}, u32[]{:S(2)}) collective-permute-start(bf16[256,640]{1,0:T(8,128)(2,1)} %collective-permute-done.34.refs_0_), channel_id=1, source_target_pairs={{0,2},{1,3},{2,0},{3,1},{4,6},{5,7},{6,4},{7,5},{8,10},{9,11},{10,... | collective-permute-start | bytes 983048 | tf_op jit(solution)/shard_map/ppermute | solution.py:280
  145.9 23.1 %collective-permute-start.51 = (bf16[320,512]{1,0:T(8,128)(2,1)}, bf16[320,512]{1,0:T(8,128)(2,1)}, u32[]{:S(2)}, u32[]{:S(2)}) collective-permute-start(bf16[320,512]{1,0:T(8,128)(2,1)} %refs_4_.3), channel_id=1, source_target_pairs={{0,16},{4,20},{8,24},{12,28},{16,0},{20,4},{24,8},{28,12},{1,17},{... | collective-permute-start | bytes 983048 | tf_op jit(solution)/shard_map/ppermute | solution.py:273
  146.0 24.8 %collective-permute-start.38 = (bf16[256,640]{1,0:T(8,128)(2,1)}, bf16[256,640]{1,0:T(8,128)(2,1)}, u32[]{:S(2)}, u32[]{:S(2)}) collective-permute-start(bf16[256,640]{1,0:T(8,128)(2,1)} %collective-permute-done.34.refs_0_), channel_id=1, source_target_pairs={{0,1},{1,0},{2,3},{3,2},{4,5},{5,4},{6,7},{7,6},{8,9},{9,8},{10,11... | collective-permute-start | bytes 983048 | tf_op jit(solution)/shard_map/ppermute | solution.py:280
  150.0 22.6 %collective-permute-start.37 = (bf16[256,640]{1,0:T(8,128)(2,1)}, bf16[256,640]{1,0:T(8,128)(2,1)}, u32[]{:S(2)}, u32[]{:S(2)}) collective-permute-start(bf16[256,640]{1,0:T(8,128)(2,1)} %collective-permute-done.35.refs_1_), channel_id=1, source_target_pairs={{0,2},{1,3},{2,0},{3,1},{4,6},{5,7},{6,4},{7,5},{8,10},{9,11},{10,... | collective-permute-start | bytes 983048 | tf_op jit(solution)/shard_map/ppermute | solution.py:280
  153.0 19.6 %collective-permute-start.39 = (bf16[256,640]{1,0:T(8,128)(2,1)}, bf16[256,640]{1,0:T(8,128)(2,1)}, u32[]{:S(2)}, u32[]{:S(2)}) collective-permute-start(bf16[256,640]{1,0:T(8,128)(2,1)} %collective-permute-done.35.refs_1_), channel_id=1, source_target_pairs={{0,1},{1,0},{2,3},{3,2},{4,5},{5,4},{6,7},{7,6},{8,9},{9,8},{10,11... | collective-permute-start | bytes 983048 | tf_op jit(solution)/shard_map/ppermute | solution.py:280
  153.0 20.0 %collective-permute-start.40 = (bf16[256,640]{1,0:T(8,128)(2,1)}, bf16[256,640]{1,0:T(8,128)(2,1)}, u32[]{:S(2)}, u32[]{:S(2)}) collective-permute-start(bf16[256,640]{1,0:T(8,128)(2,1)} %collective-permute-done.36.refs_2_), channel_id=1, source_target_pairs={{0,1},{1,0},{2,3},{3,2},{4,5},{5,4},{6,7},{7,6},{8,9},{9,8},{10,11... | collective-permute-start | bytes 983048 | tf_op jit(solution)/shard_map/ppermute | solution.py:280
  169.0 12.2 %collective-permute-start.53 = (bf16[320,512]{1,0:T(8,128)(2,1)}, bf16[320,512]{1,0:T(8,128)(2,1)S(1)}, u32[]{:S(2)}, u32[]{:S(2)}) collective-permute-start(bf16[320,512]{1,0:T(8,128)(2,1)} %refs_4_.3), channel_id=1, source_target_pairs={{0,24},{4,28},{8,16},{12,20},{16,8},{20,12},{24,0},{28,4},{1,25},{... | collective-permute-start | bytes 983048 | tf_op jit(solution)/shard_map/ppermute | solution.py:273
  170.8 25.3 %collective-permute-start.43 = (bf16[512,256]{1,0:T(8,128)(2,1)}, bf16[512,256]{1,0:T(8,128)(2,1)S(1)}, u32[]{:S(2)}, u32[]{:S(2)}) collective-permute-start(bf16[512,256]{1,0:T(8,128)(2,1)} %get-tuple-element.48.refs_0_), channel_id=1, source_target_pairs={{0,4},{4,0},{8,12},{12,8},{16,20},{20,16},{24,28},{28,24},{1,5},{5... | collective-permute-start | bytes 786440 | tf_op jit(solution)/shard_map/ppermute | solution.py:284
  172.6 38.1 %collective-permute-start.48 = (bf16[320,512]{1,0:T(8,128)(2,1)}, bf16[320,512]{1,0:T(8,128)(2,1)S(1)}, u32[]{:S(2)}, u32[]{:S(2)}) collective-permute-start(bf16[320,512]{1,0:T(8,128)(2,1)} %refs_4_.3), channel_id=1, source_target_pairs={{0,4},{4,0},{8,12},{12,8},{16,20},{20,16},{24,28},{28,24},{1,5},{5... | collective-permute-start | bytes 983048 | tf_op jit(solution)/shard_map/ppermute | solution.py:284
  172.9 38.3 %collective-permute-start.50 = (bf16[320,512]{1,0:T(8,128)(2,1)}, bf16[320,512]{1,0:T(8,128)(2,1)S(1)}, u32[]{:S(2)}, u32[]{:S(2)}) collective-permute-start(bf16[320,512]{1,0:T(8,128)(2,1)} %collective-permute-done.49.refs_6_), channel_id=1, source_target_pairs={{0,4},{4,0},{8,12},{12,8},{16,20},{20,16},{24,28},{28,24},{1,5},{5... | collective-permute-start | bytes 983048 | tf_op jit(solution)/shard_map/ppermute | solution.py:284
  174.7 18.9 %collective-permute-start.42 = (s32[1,1024]{1,0:T(1,128)S(1)}, s32[1,1024]{1,0:T(1,128)S(1)}, u32[]{:S(2)}, u32[]{:S(2)}) collective-permute-start(s32[1,1024]{1,0:T(1,128)S(1)} %bitcast.169), channel_id=1, source_target_pairs={{0,4},{4,0},{8,12},{12,8},{16,20},{20,16},{24,28},{28,24},{1,5},{5... | collective-permute-start | bytes 12296 | tf_op jit(solution)/shard_map/ppermute | solution.py:284
  181.1 21.3 %collective-permute-start.44 = (bf16[512,256]{1,0:T(8,128)(2,1)}, bf16[512,256]{1,0:T(8,128)(2,1)S(1)}, u32[]{:S(2)}, u32[]{:S(2)}) collective-permute-start(bf16[512,256]{1,0:T(8,128)(2,1)} %get-tuple-element.49.refs_1_), channel_id=1, source_target_pairs={{0,4},{4,0},{8,12},{12,8},{16,20},{20,16},{24,28},{28,24},{1,5},{5... | collective-permute-start | bytes 786440 | tf_op jit(solution)/shard_map/ppermute | solution.py:284
  193.6 19.5 %collective-permute-start.52 = (bf16[320,512]{1,0:T(8,128)(2,1)}, bf16[320,512]{1,0:T(8,128)(2,1)S(1)}, u32[]{:S(2)}, u32[]{:S(2)}) collective-permute-start(bf16[320,512]{1,0:T(8,128)(2,1)} %collective-permute-done.51.refs_8_), channel_id=1, source_target_pairs={{0,4},{4,0},{8,12},{12,8},{16,20},{20,16},{24,28},{28,24},{1,5},{5... | collective-permute-start | bytes 983048 | tf_op jit(solution)/shard_map/ppermute | solution.py:284
  196.1 17.1 %collective-permute-start.54 = (bf16[320,512]{1,0:T(8,128)(2,1)S(1)}, bf16[320,512]{1,0:T(8,128)(2,1)S(1)}, u32[]{:S(2)}, u32[]{:S(2)}) collective-permute-start(bf16[320,512]{1,0:T(8,128)(2,1)S(1)} %collective-permute-done.53.refs_10_), channel_id=1, source_target_pairs={{0,4},{4,0},{8,12},{12,8},{16,20},{20,16},{24,28},{28,24},{1,5},{5... | collective-permute-start | bytes 983048 | tf_op jit(solution)/shard_map/ppermute | solution.py:284
  226.0 9.8 %collective-permute-start.56 = (bf16[256,640]{1,0:T(8,128)(2,1)S(1)}, bf16[256,640]{1,0:T(8,128)(2,1)S(1)}, u32[]{:S(2)}, u32[]{:S(2)}) collective-permute-start(bf16[256,640]{1,0:T(8,128)(2,1)S(1)} %fusion.36), channel_id=1, source_target_pairs={{0,2},{1,3},{2,0},{3,1},{4,6},{5,7},{6,4},{7,5},{8,10},{9,11},{10,... | collective-permute-start | bytes 983048 | tf_op jit(solution)/shard_map/ppermute | solution.py:280
  (53 other events, 677.6 us)
